TPU v7x, 128 devices: a whole 4x4x4 slice. The times are simulated.
128 devices in a mesh: slab: 32 (over x, z, core), leaf: 4 (over y).
Axes of the slice: x: 4, y: 4, z: 4, core: 2. Of those that a mesh axis runs over, the one named last changes fastest.
Arguments:
- particles: float32 [3, 128, 16, 256], P(None, 'slab', 'leaf'), may hold values from -1.05 to 1.05, as said below
- near_mask: int32 [16, 128, 16], P(None, 'slab', 'leaf'), may hold values from 0 to 1, as said below
Outputs:
- velocity: float32 [2, 128, 16, 256], P(None, 'slab', 'leaf')
Inputs may be any that keep to these rules, and one draw needn't show every extreme that they name: `particles`: entries 0 and 1 of the first dimension are offsets; entry 2 is the circulation. near_mask[o, i, j] = near_mask[15 - o, i + dx, j + dy], where (dx, dy) is step o of the 16 steps with max(|dx|, |dy|) = 2 in row-major order over dx, then dy; it is 0 where leaf (i + dx, j + dy) lies outside the grid.
All inputs are finite; a program needn't handle non-finite values.
Results may differ from a plain program's by a relative error of at most 0.0003.
Values sent between devices are 32-bit elements; how exact they have to be, the bound alone decides.
No kernel may reach another device: no remote copies, remote signals or barrier semaphores. Data moves between devices by JAX's collectives and lax.ppermute only.
A program may use at most 64 MiB of HBM per device.

v0:
```python
import math

import jax
import jax.numpy as jnp
import numpy as np
from jax import lax
from jax.sharding import Mesh
from jax.sharding import PartitionSpec as P

ORDER = 10
SLAB = ("slab_0", "slab_1", "slab_2")
SLAB_LEAF = ("slab_0", "slab_1", "slab_2", "leaf")


DELTA_SQUARED = 0.0025
TWO_PI = 2.0 * math.pi
inner_steps = [(a, b) for a in range(-1, 2) for b in range(-1, 2)]
cycle_steps = [(a, b) for a in range(-2, 3) for b in range(-2, 3) if max(abs(a), abs(b)) == 2]


def with_halo(shard, sides, width):
    for axis, dim in sides:
        size, length = (lax.axis_size(axis), shard.shape[dim])
        up = [(i, (i + 1) % size) for i in range(size - 1)]
        down = [(j, i) for i, j in up]
        last = lax.slice_in_dim(shard, length - width, length, axis=dim)
        first = lax.slice_in_dim(shard, 0, width, axis=dim)
        before = lax.ppermute(last, axis, up)
        after = lax.ppermute(first, axis, down)
        shard = jnp.concatenate([before, shard, after], axis=dim)
    return shard


def joined_along(blocks, dim):
    lengths = list(blocks.shape[1:])
    lengths[dim] *= blocks.shape[0]
    return jnp.moveaxis(blocks, 0, dim).reshape(lengths)


def stacked_from(shard, axes, order):
    blocks = shard[None]
    for k in order:
        blocks = lax.all_gather(blocks, axes[k], axis=0, tiled=True)
    current = [lax.axis_size(axes[k]) for k in reversed(order)]
    blocks = blocks.reshape(*current, *shard.shape)
    turned = sorted(range(len(order)), key=lambda place: order[len(order) - 1 - place])
    return blocks.transpose(*turned, *range(len(order), blocks.ndim)).reshape(-1, *shard.shape)


def whole_of(shard, axes, order, dim):
    return joined_along(stacked_from(shard, axes, order), dim)


def complex_powers(base_real, base_imaginary, count):
    power_real = [jnp.ones_like(base_real)]
    power_imaginary = [jnp.zeros_like(base_imaginary)]
    for repeat in range(1, count):
        last_real = power_real[-1]
        last_imaginary = power_imaginary[-1]
        power_real.append(last_real * base_real - last_imaginary * base_imaginary)
        power_imaginary.append(last_real * base_imaginary + last_imaginary * base_real)
    return (jnp.stack(power_real, -1), jnp.stack(power_imaginary, -1))


def translation(shift_real, shift_imaginary):
    hankel = np.arange(ORDER)[:, None] + np.arange(ORDER)[None, :] + 1
    weights = np.array(
        [[math.comb(i + k, k) * (-1.0) ** (k + 1) for k in range(ORDER)] for i in range(ORDER)],
        dtype=np.float32,
    )
    denominator = shift_real * shift_real + shift_imaginary * shift_imaginary
    inverse_real = shift_real / denominator
    inverse_imaginary = -shift_imaginary / denominator
    power_real, power_imaginary = complex_powers(inverse_real, inverse_imaginary, 2 * ORDER)
    return (power_real[..., hankel] * weights, power_imaginary[..., hankel] * weights)


def body(particles, near_mask):
    block_side = particles.shape[1]
    highest = lax.Precision.HIGHEST
    slab_index = lax.axis_index(SLAB)
    leaf_index = lax.axis_index("leaf")
    slab_count = lax.axis_size(SLAB)
    leaf_count = lax.axis_size("leaf")
    device_count = slab_count * leaf_count
    offset_x, offset_y, strength = (particles[0], particles[1], particles[2])
    power_real, power_imaginary = complex_powers(offset_x, offset_y, ORDER)
    leaf_multipole = jnp.stack(
        [
            jnp.sum(strength[..., None] * power_real, axis=2),
            jnp.sum(strength[..., None] * power_imaginary, axis=2),
        ]
    )
    centred = jnp.arange(block_side, dtype=jnp.float32) - (block_side - 1) / 2.0
    window = with_halo(leaf_multipole, ((SLAB, 1), ("leaf", 2)), block_side)
    block_power_real, block_power_imaginary = complex_powers(
        centred[:, None, None] + offset_x, centred[None, :, None] + offset_y, ORDER
    )
    own_block = jnp.stack(
        [
            jnp.sum(strength[..., None] * block_power_real, axis=(0, 1, 2)),
            jnp.sum(strength[..., None] * block_power_imaginary, axis=(0, 1, 2)),
        ]
    )
    blocks = whole_of(own_block[None], SLAB_LEAF, (0, 1, 3, 2), 0)
    near = with_halo(particles, ((SLAB, 1), ("leaf", 2)), 2)
    mask_float = near_mask.astype(jnp.float32)

    def direct_row(row):
        target_x = offset_x[row]
        target_y = offset_y[row]
        row_real = jnp.zeros(target_x.shape, jnp.float32)
        row_imaginary = jnp.zeros(target_x.shape, jnp.float32)
        for number, (step_x, step_y) in enumerate(inner_steps + cycle_steps):
            source_row = lax.dynamic_index_in_dim(near, 2 + step_x + row, 1, keepdims=False)
            source = source_row[:, 2 + step_y : 2 + step_y + block_side, :]
            if number < 9:
                circulation = source[2]
            else:
                mask_row = lax.dynamic_index_in_dim(mask_float[number - 9], row, 0, keepdims=False)
                circulation = source[2] * mask_row[:, None]
            delta_x = target_x[:, :, None] - (step_x + source[0][:, None, :])
            delta_y = target_y[:, :, None] - (step_y + source[1][:, None, :])
            factor = circulation[:, None, :] / (
                delta_x * delta_x + delta_y * delta_y + DELTA_SQUARED
            )
            row_real = row_real + jnp.sum(factor * delta_x, -1)
            row_imaginary = row_imaginary - jnp.sum(factor * delta_y, -1)
        return (row_real, row_imaginary)

    sum_real, sum_imaginary = lax.map(direct_row, jnp.arange(block_side, dtype=jnp.int32))
    margin = block_side - 1
    outer = 2 * block_side - 1
    padded_window = jnp.pad(window, ((0, 0), (margin, margin), (margin, margin), (0, 0)))
    far_list = [
        (a, b)
        for a in range(-outer, outer + 1)
        for b in range(-outer, outer + 1)
        if max(abs(a), abs(b)) >= 3
    ]
    step_table = np.array(cycle_steps + far_list, dtype=np.int32)
    group_count = 2 * (block_side - 1)
    group_size = step_table.shape[0] // group_count
    weights = jnp.concatenate(
        [1.0 - mask_float, jnp.ones((len(far_list), block_side, block_side), jnp.float32)]
    )
    weights = weights.reshape(group_count, group_size, block_side, block_side)
    grouped_table = jnp.asarray(step_table.reshape(group_count, group_size, 2))
    place = jnp.arange(block_side, dtype=jnp.int32)

    def leaf_group(totals, pieces):
        table, weight = pieces
        rows = outer + table[:, 0][:, None] + place[None, :]
        columns = outer + table[:, 1][:, None] + place[None, :]
        sources = (
            padded_window[:, rows[:, :, None], columns[:, None, :], :] * weight[None, :, :, :, None]
        )
        matrix_real, matrix_imaginary = translation(
            table[:, 0].astype(jnp.float32), table[:, 1].astype(jnp.float32)
        )
        part_real = jnp.einsum(
            "sijk,slk->ijl", sources[0], matrix_real, precision=highest
        ) - jnp.einsum("sijk,slk->ijl", sources[1], matrix_imaginary, precision=highest)
        part_imaginary = jnp.einsum(
            "sijk,slk->ijl", sources[0], matrix_imaginary, precision=highest
        ) + jnp.einsum("sijk,slk->ijl", sources[1], matrix_real, precision=highest)
        return ((totals[0] + part_real, totals[1] + part_imaginary), None)

    zero_local = jnp.zeros((block_side, block_side, ORDER), jnp.float32)
    (local_real, local_imaginary), unused = lax.scan(
        leaf_group, (zero_local, zero_local), (grouped_table, weights)
    )
    device_number = np.arange(device_count)
    block_x = jnp.asarray(device_number // leaf_count, jnp.int32)
    block_y = jnp.asarray(device_number % leaf_count, jnp.int32)
    global_x = (slab_index * block_side + jnp.arange(block_side, dtype=jnp.int32)).astype(
        jnp.float32
    )
    global_y = (leaf_index * block_side + jnp.arange(block_side, dtype=jnp.int32)).astype(
        jnp.float32
    )
    remote = jnp.maximum(jnp.abs(block_x - slab_index), jnp.abs(block_y - leaf_index)) >= 2
    centre_x = (block_x * block_side).astype(jnp.float32) + (block_side - 1) / 2.0
    centre_y = (block_y * block_side).astype(jnp.float32) + (block_side - 1) / 2.0
    far_blocks = blocks * remote.astype(jnp.float32)[:, None, None]
    block_groups = device_count // 8

    def block_group(totals, pieces):
        group_x, group_y, group_remote, group_blocks = pieces
        grid_shape = (8, block_side, block_side)
        shift_real = jnp.broadcast_to(group_x[:, None, None] - global_x[None, :, None], grid_shape)
        shift_imaginary = jnp.broadcast_to(
            group_y[:, None, None] - global_y[None, None, :], grid_shape
        )
        shift_real = jnp.where(group_remote[:, None, None], shift_real, 1.0)
        shift_imaginary = jnp.where(group_remote[:, None, None], shift_imaginary, 1.0)
        matrix_real, matrix_imaginary = translation(shift_real, shift_imaginary)
        part_real = jnp.einsum(
            "nijlk,nk->ijl", matrix_real, group_blocks[:, 0], precision=highest
        ) - jnp.einsum("nijlk,nk->ijl", matrix_imaginary, group_blocks[:, 1], precision=highest)
        part_imaginary = jnp.einsum(
            "nijlk,nk->ijl", matrix_imaginary, group_blocks[:, 0], precision=highest
        ) + jnp.einsum("nijlk,nk->ijl", matrix_real, group_blocks[:, 1], precision=highest)
        return ((totals[0] + part_real, totals[1] + part_imaginary), None)

    block_pieces = (
        centre_x.reshape(block_groups, 8),
        centre_y.reshape(block_groups, 8),
        remote.reshape(block_groups, 8),
        far_blocks.reshape(block_groups, 8, 2, ORDER),
    )
    (local_real, local_imaginary), unused = lax.scan(
        block_group, (local_real, local_imaginary), block_pieces
    )
    sum_real = sum_real + jnp.sum(
        local_real[:, :, None, :] * power_real - local_imaginary[:, :, None, :] * power_imaginary,
        -1,
    )
    sum_imaginary = sum_imaginary + jnp.sum(
        local_real[:, :, None, :] * power_imaginary + local_imaginary[:, :, None, :] * power_real,
        -1,
    )
    return jnp.stack([sum_imaginary, sum_real]) / TWO_PI


def solution(mesh):
    finer = Mesh(
        mesh.devices.reshape(4, 4, 2, mesh.shape["leaf"]), ("slab_0", "slab_1", "slab_2", "leaf")
    )
    in_specs = (P(None, SLAB, "leaf", None), P(None, SLAB, "leaf"))
    out_specs = P(None, SLAB, "leaf", None)
    return jax.shard_map(body, mesh=finer, in_specs=in_specs, out_specs=out_specs, check_vma=False)
```

profile of v0, /device:TPU:0, one launch (start us, length us, event | category | flops | bytes accessed | tf_op | source)
XLA Modules:
  0.0 608.0 jit_solution(8807773859138143936)
XLA Ops:
  19.6 15.9 %all-gather.1 = f32[4,2,10]{2,1,0:T(2,128)S(1)} all-gather(f32[1,2,10]{2,1,0:T(2,128)S(1)} %maximum_bitcast_fusion), channel_id=2, replica_groups=mesh['slab_0'=4,'slab_1'=4,'slab_2'=2,'leaf'=4] {'slab_0'}, dimensions={0}, use_global_device_ids=true | all-gather | bytes 400 | tf_op jit(solution)/shard_map/all_gather | solution.py:43
  35.5 12.0 %all_gather.13 = f32[16,1,2,10]{3,2,1,0:T(2,128)S(1)} all-gather(f32[4,1,2,10]{3,2,1,0:T(2,128)S(1)} %bitcast.1178), channel_id=1, replica_groups=mesh['slab_0'=4,'slab_1'=4,'slab_2'=2,'leaf'=4] {'slab_1'}, dimensions={0}, use_global_device_ids=true | all-gather | bytes 1600 | tf_op jit(solution)/shard_map/all_gather | solution.py:43
  47.5 12.4 %all_gather.14 = f32[64,1,2,10]{3,2,1,0:T(2,128)S(1)} all-gather(f32[16,1,2,10]{3,2,1,0:T(2,128)S(1)} %all_gather.13), channel_id=1, replica_groups=mesh['slab_0'=4,'slab_1'=4,'slab_2'=2,'leaf'=4] {'leaf'}, dimensions={0}, use_global_device_ids=true | all-gather | bytes 6400 | tf_op jit(solution)/shard_map/all_gather | solution.py:43
  63.4 4.5 collective-permute-start.6
  70.0 57.2 %while.46 = (s32[]{:T(128)}, f32[4,4,10]{2,1,0:T(4,128)S(1)}, f32[4,4,10]{2,1,0:T(4,128)S(1)}, f32[2,18,18,10]{3,0,2,1:T(2,128)S(1)}, f32[6,36,4,4]{1,3,2,0:T(4,...) while((s32[]{:T(128)}, f32[4,4,10]{2,1,0:T(4,128)S(1)}, ...), condition=%wide.region_55.56_spmd.clone.clone.clone, body=%wide.region_54.55_spmd.sunk.clone.clone.clone.sunk | while | flops 2792347 | bytes 1186424 | solution.py:170
  72.7 4.9 gather_fusion.4
  82.2 4.9 gather_fusion.4
  91.7 4.9 gather_fusion.4
  101.3 4.9 gather_fusion.4
  110.8 4.9 gather_fusion.4
  120.4 4.9 gather_fusion.4
  127.2 374.6 %while.45 = (s32[]{:T(128)}, f32[4,4,10]{2,1,0:T(4,128)S(1)}, f32[4,4,10]{2,1,0:T(4,128)S(1)}, pred[16,8]{1,0:T(8,128)(4,1)S(1)}, f32[16,8]{1,0:T(8,128)}, /*ind...) while((s32[]{:T(128)}, f32[4,4,10]{2,1,0:T(4,128)S(1)}, ...), condition=%wide.region_59.60_spmd.clone.clone.clone, body=%wide.region_58.59_spmd.sunk.clone.clone.clone.sunk | while | flops 970834 | bytes 1127061 | solution.py:212
  137.2 3.8 fusion.358
  170.4 3.8 fusion.357
  184.0 3.8 fusion.358
  193.8 3.8 fusion.357
  207.4 3.8 fusion.358
  217.2 3.8 fusion.357
  254.2 3.8 fusion.358
  264.0 3.8 fusion.357
  277.6 3.8 fusion.358
  502.2 4.2 collective-permute-start.2
  508.1 4.3 collective-permute-done.3
  512.5 94.9 %while.44 = (s32[]{:T(128)}, f32[4,4,256]{2,1,0:T(4,128)S(1)}, f32[4,4,256]{2,1,0:T(4,128)S(1)}, s32[4]{0:T(128)S(1)}, f32[3,8,8,256]{3,2,0,1:T(8,128)S(1)}, /*i...) while((s32[]{:T(128)}, f32[4,4,256]{2,1,0:T(4,128)S(1)}, ...), condition=%wide.region_51.52_spmd, body=%wide.region_0.51_spmd.sunk | while | flops 72145936 | bytes 1645816 | solution.py:131
  (1269 shorter events, 454.7 us)
Async XLA Ops:
  0.0 9.2 %copy-start = (f32[3,4,4,256]{3,2,1,0:T(4,128)S(1)}, f32[3,4,4,256]{3,2,1,0:T(4,128)}, u32[]{:S(2)}) copy-start(f32[3,4,4,256]{3,2,1,0:T(4,128)} %param.19) | copy-start | bytes 147460
  8.3 11.1 %copy-start.4 = (s32[128]{0:T(128)S(1)}, s32[128]{0:T(128)}, u32[]{:S(2)}) copy-start(s32[128]{0:T(128)} %constant.303.clone) | copy-start | bytes 1540
  8.4 11.1 %copy-start.5 = (s32[128]{0:T(128)S(1)}, s32[128]{0:T(128)}, u32[]{:S(2)}) copy-start(s32[128]{0:T(128)} %constant.302.clone) | copy-start | bytes 1540
  9.5 52.4 %copy-start.3 = (s32[16,4,4]{0,2,1:T(4,128)S(1)}, s32[16,4,4]{0,2,1:T(4,128)}, u32[]{:S(2)}) copy-start(s32[16,4,4]{0,2,1:T(4,128)} %param.20) | copy-start | bytes 3076
  10.2 51.9 %collective-permute-start.5 = (f32[2,4,4,10]{3,2,1,0:T(4,128)S(1)}, f32[2,4,4,10]{3,2,1,0:T(4,128)S(1)}, u32[]{:S(2)}, u32[]{:S(2)}) collective-permute-start(f32[2,4,4,10]{3,2,1,0:T(4,128)S(1)} %pad_maximum_fusion.3), channel_id=1, source_target_pairs={{4,0},{8,4},{12,8},{16,12},{20,16},{24,20},{28,24},{32,28},{36,32}... | collective-permute-start | bytes 3848 | tf_op jit(solution)/shard_map/ppermute | solution.py:29
  11.5 50.6 %collective-permute-start.4 = (f32[2,4,4,10]{3,2,1,0:T(4,128)S(1)}, f32[2,4,4,10]{3,2,1,0:T(4,128)S(1)}, u32[]{:S(2)}, u32[]{:S(2)}) collective-permute-start(f32[2,4,4,10]{3,2,1,0:T(4,128)S(1)} %pad_maximum_fusion.3), channel_id=1, source_target_pairs={{0,4},{4,8},{8,12},{12,16},{16,20},{20,24},{24,28},{28,32},{32,36}... | collective-permute-start | bytes 3848 | tf_op jit(solution)/shard_map/ppermute | solution.py:28
  14.5 487.5 %collective-permute-start = (f32[3,2,4,256]{3,2,0,1:T(4,128)S(1)}, f32[3,2,4,256]{3,2,0,1:T(4,128)S(1)}, u32[]{:S(2)}, u32[]{:S(2)}) collective-permute-start(f32[3,2,4,256]{3,2,0,1:T(4,128)S(1)} %copy.196), channel_id=1, source_target_pairs={{0,4},{4,8},{8,12},{12,16},{16,20},{20,24},{24,28},{28,32},{32,36}... | collective-permute-start | bytes 73736 | tf_op jit(solution)/shard_map/ppermute | solution.py:28
  18.1 484.0 %collective-permute-start.1 = (f32[3,2,4,256]{3,2,0,1:T(4,128)S(1)}, f32[3,2,4,256]{3,2,0,1:T(4,128)S(1)}, u32[]{:S(2)}, u32[]{:S(2)}) collective-permute-start(f32[3,2,4,256]{3,2,0,1:T(4,128)S(1)} %copy.197), channel_id=1, source_target_pairs={{4,0},{8,4},{12,8},{16,12},{20,16},{24,20},{28,24},{32,28},{36,32}... | collective-permute-start | bytes 73736 | tf_op jit(solution)/shard_map/ppermute | solution.py:29
  62.1 6.3 %collective-permute-start.7 = (f32[2,12,4,10]{3,2,1,0:T(4,128)S(1)}, f32[2,12,4,10]{3,2,1,0:T(4,128)S(1)}, u32[]{:S(2)}, u32[]{:S(2)}) collective-permute-start(f32[2,12,4,10]{3,2,1,0:T(4,128)S(1)} %pad_maximum_fusion.2), channel_id=1, source_target_pairs={{1,0},{2,1},{3,2},{5,4},{6,5},{7,6},{9,8},{10,9},{11,10},{13,12},{... | collective-permute-start | bytes 11528 | tf_op jit(solution)/shard_map/ppermute | solution.py:29
  63.4 6.3 %collective-permute-start.6 = (f32[2,12,4,10]{3,2,1,0:T(4,128)S(1)}, f32[2,12,4,10]{3,2,1,0:T(4,128)S(1)}, u32[]{:S(2)}, u32[]{:S(2)}) collective-permute-start(f32[2,12,4,10]{3,2,1,0:T(4,128)S(1)} %pad_maximum_fusion.2), channel_id=1, source_target_pairs={{0,1},{1,2},{2,3},{4,5},{5,6},{6,7},{8,9},{9,10},{10,11},{12,13},{... | collective-permute-start | bytes 11528 | tf_op jit(solution)/shard_map/ppermute | solution.py:28
  68.0 1.9 copy-start.1
  68.0 1.9 copy-start.2
  502.2 6.0 collective-permute-start.2
  506.4 6.0 collective-permute-start.3
where the time goes:
time: 611 us; the launch traced here: 608 us
  matrix products  249 us (41%)
  local copies, waits for them, and re-layouts  146 us (24%)
  other arithmetic  108 us (18%)
  blocking collectives  42.2 us (7%)
  loops' own time  36.4 us (6%)
  starting transfers between devices  20.6 us (3%)
    dot_general x16, matrix products, block_group(): jnp.einsum('nijlk,nk->ijl', matrix_real, group_blocks[:, 1], precision=hi...  60.3 us
    dot_general x16, matrix products, block_group(): jnp.einsum('nijlk,nk->ijl', matrix_imaginary, group_blocks[:, 0], precisi...  60.3 us
    dot_general x16, matrix products, block_group(): jnp.einsum('nijlk,nk->ijl', matrix_real, group_blocks[:, 0], precision=hi...  60.1 us
    dot_general x16, matrix products, block_group(): jnp.einsum('nijlk,nk->ijl', matrix_imaginary, group_blocks[:, 1], precisi...  60.1 us
    reduce_sum x20, other arithmetic, direct_row(): row_imaginary = row_imaginary - jnp.sum(factor * delta_y, -1)  55.9 us
    all_gather x4, blocking collectives, stacked_from(): blocks = lax.all_gather(blocks, axes[k], axis=0, tiled=True)  42.2 us
    gather x44, local copies, waits for them, and re-layouts, translation(): power_imaginary[..., hankel] * weights  39.8 us
    gather x44, local copies, waits for them, and re-layouts, translation(): power_real[..., hankel] * weights  39.6 us
  transfers between devices with their start and end apart: 8, of which 3 were waited for; matrix products, arithmetic and copies ran while one was open for 71% of the time, Pallas kernels for 0%

commit v1 on v0

v1 whole, which is shorter than its diff:
```python
import functools
import math

import jax
import jax.numpy as jnp
import numpy as np
from jax import lax
from jax.experimental import pallas as pl
from jax.experimental.pallas import tpu as pltpu
from jax.sharding import Mesh
from jax.sharding import PartitionSpec as P

ORDER = 10
SIDE = 4
LEAVES = 16
SIZE = 256
FEATURES = 32
DELTA_SQUARED = 0.0025
TWO_PI = 2.0 * math.pi
SLAB = ("slab_0", "slab_1", "slab_2")
ALL = ("slab_0", "slab_1", "slab_2", "leaf")
F32 = jnp.float32
BF16 = jnp.bfloat16
VMEM_LIMIT = 56 << 20
cycle_steps = [(a, b) for a in range(-2, 3) for b in range(-2, 3) if max(abs(a), abs(b)) == 2]
near_steps = [(a, b) for a in range(-2, 3) for b in range(-2, 3)]


def exchange_pairs(partner):
    pairs = []
    for x in range(4):
        for z in range(4):
            for c in range(2):
                for y in range(4):
                    other = partner(x, z, c, y)
                    if other is not None:
                        a, b, d, e = other
                        pairs.append((((x * 4 + z) * 2 + c) * 4 + y, ((a * 4 + b) * 2 + d) * 4 + e))
    return pairs


def slab_between_chips(x, z, c, y):
    slab = (x * 4 + z) * 2 + c
    other = slab + 1 if c == 1 else slab - 1
    if not 0 <= other < 32:
        return None
    return (other // 8, (other // 2) % 4, other % 2, y)


def near_side(k):
    return k ^ 1


def far_side(k):
    return 3 - k


SWAPS = {
    "core": exchange_pairs(lambda x, z, c, y: (x, z, 1 - c, y)),
    "slab": exchange_pairs(slab_between_chips),
    "leaf_near": exchange_pairs(lambda x, z, c, y: (x, z, c, near_side(y))),
    "leaf_far": exchange_pairs(lambda x, z, c, y: (x, z, c, far_side(y))),
    "z_near": exchange_pairs(lambda x, z, c, y: (x, near_side(z), c, y)),
    "z_far": exchange_pairs(lambda x, z, c, y: (x, far_side(z), c, y)),
    "x_near": exchange_pairs(lambda x, z, c, y: (near_side(x), z, c, y)),
    "x_far": exchange_pairs(lambda x, z, c, y: (far_side(x), z, c, y)),
}


def swap(value, name):
    return lax.ppermute(value, ALL, SWAPS[name])


def pieces(value, count):
    parts = []
    for unused in range(count):
        part = value.astype(BF16).astype(F32)
        parts.append(part)
        value = value - part
    return parts


def build_features(wx, wy, g, ox, oy, stage_t, stage_s, stage_w, t_ref, s_ref, w_ref, first, with_target):
    count = wx.shape[0]
    one = jnp.ones_like(wx)
    zero = jnp.zeros_like(wx)
    coarse_x = jnp.round(wx * 32.0) * (1.0 / 32.0)
    coarse_y = jnp.round(wy * 32.0) * (1.0 / 32.0)
    fine_x = wx - coarse_x
    fine_y = wy - coarse_y
    big_x = coarse_x + ox
    big_y = coarse_y + oy
    big = pieces(big_x * big_x + big_y * big_y, 2)
    rest = 2.0 * (big_x * fine_x + big_y * fine_y) + fine_x * fine_x + fine_y * fine_y
    px = pieces(fine_x, 2)
    py = pieces(fine_y, 2)
    if with_target:
        rows = [big_x, big_y, big[0], big[1], one, one, zero, zero]
        rows += [big_x, big_x, big_y, big_y, px[0], px[1], py[0], py[1]]
        rows += [px[0], px[0], px[1], py[0], py[0], py[1]]
        rows += pieces(rest + DELTA_SQUARED, 3) + [one, one, one]
        rows += [zero] * (FEATURES - len(rows))
        for f, row in enumerate(rows):
            stage_t[:count, f, :] = row
    twice = lambda v: -2.0 * v
    rows = [twice(big_x), twice(big_y), one, one, big[0], big[1], zero, zero]
    rows += [twice(px[0]), twice(px[1]), twice(py[0]), twice(py[1])]
    rows += [twice(big_x), twice(big_x), twice(big_y), twice(big_y)]
    rows += [twice(px[0]), twice(px[1]), twice(px[0]), twice(py[0]), twice(py[1]), twice(py[0])]
    rows += [one, one, one] + pieces(rest, 3)
    rows += [zero] * (FEATURES - len(rows))
    for f, row in enumerate(rows):
        stage_s[:count, f, :] = row
    rows = pieces(g, 3) + pieces(g * (wx + ox), 3) + pieces(g * (wy + oy), 3)
    rows += [zero] * (16 - len(rows))
    for f, row in enumerate(rows):
        stage_w[:count, f, :] = row
    for n in range(count):
        if with_target:
            t_ref[first + n] = stage_t[n].astype(BF16)
        s_ref[first + n] = jnp.transpose(stage_s[n]).astype(BF16)
        w_ref[first + n] = stage_w[n].astype(BF16)


def power_list(base_re, base_im, count):
    re = [jnp.ones_like(base_re)]
    im = [jnp.zeros_like(base_im)]
    for unused in range(1, count):
        a, b = re[-1], im[-1]
        re.append(a * base_re - b * base_im)
        im.append(a * base_im + b * base_re)
    return re, im


def row_of(n):
    return lax.broadcasted_iota(jnp.int32, (n, 1), 0)


def leaf_offsets():
    n = row_of(LEAVES)
    ox = (n >> 2).astype(F32) - 1.5
    oy = (n & 3).astype(F32) - 1.5
    return ox, oy


def own_rows(ref, part):
    return jnp.concatenate([ref[part, i] for i in range(SIDE)], axis=0)


SLAB_ROWS = 72
LEAF_ROWS = 96


def prepare_own(info, part_ref, t_ref, s_ref, w_ref, m_ref, f_ref, a_ref, b_ref, stage_t, stage_s, stage_w):
    wx = own_rows(part_ref, 0)
    wy = own_rows(part_ref, 1)
    g = own_rows(part_ref, 2)
    ox, oy = leaf_offsets()
    lane = lax.broadcasted_iota(jnp.int32, (LEAVES, 128), 1)
    table = jnp.zeros((LEAVES, 128), F32)
    for start, base_re, base_im in ((0, wx, wy), (32, wx + ox, wy + oy)):
        re, im = power_list(base_re, base_im, ORDER)
        for k in range(ORDER):
            table = jnp.where(lane == start + k, jnp.sum(g * re[k], 1, keepdims=True), table)
            if k:
                table = jnp.where(lane == start + ORDER + k, jnp.sum(g * im[k], 1, keepdims=True), table)
    turned = jnp.transpose(table)
    leaf_part = jnp.concatenate([turned[0:24], jnp.zeros((24, 112), F32)], axis=1)
    block_part = jnp.sum(turned[32:56], axis=1, keepdims=True)
    me = info[0] * 4 + info[1]
    wide = lax.broadcasted_iota(jnp.int32, (24, 128), 1)
    block_row = jnp.where(wide == me, block_part, 0.0)
    m_ref[...] = leaf_part
    f_ref[...] = block_row
    even = info[2] == 0
    for c in range(3):
        first = jnp.concatenate([part_ref[c, 0], part_ref[c, 1]], axis=0)
        last = jnp.concatenate([part_ref[c, 2], part_ref[c, 3]], axis=0)
        a_ref[8 * c : 8 * c + 8] = jnp.where(even, last, first)
        b_ref[8 * c : 8 * c + 8] = jnp.where(even, first, last)
    none = jnp.zeros((24, 128), F32)
    for ref in (a_ref, b_ref):
        ref[24:48, 0:128] = leaf_part
        ref[24:48, 128:256] = none
        ref[48:72, 0:128] = block_row
        ref[48:72, 128:256] = none
    build_features(wx, wy, g, ox, oy, stage_t, stage_s, stage_w, t_ref, s_ref, w_ref, 0, True)


def prepare_slab(
    info, part_ref, ra_ref, rb_ref, m_ref, f_ref, after_ref, s_ref, w_ref, m_out, f_out, near_ref, far_ref, stage_s, stage_w
):
    even = info[2] == 0
    leaf_even = info[3] == 0
    halo = []
    for c in range(3):
        ra = ra_ref[8 * c : 8 * c + 8]
        rb = rb_ref[8 * c : 8 * c + 8]
        before = jnp.where(even, rb, ra)
        after = jnp.where(even, ra, rb)
        halo.append(jnp.concatenate([before, after], axis=0))
        rows = [before[0:4], before[4:8]] + [part_ref[c, i] for i in range(SIDE)] + [after[0:4], after[4:8]]
        left = jnp.concatenate([r[0:2] for r in rows], axis=0)
        right = jnp.concatenate([r[2:4] for r in rows], axis=0)
        near_ref[16 * c : 16 * c + 16] = jnp.where(leaf_even, right, left)
        far_ref[16 * c : 16 * c + 16] = jnp.where(leaf_even, left, right)
    ma = ra_ref[24:48, 0:16]
    mb = rb_ref[24:48, 0:16]
    window = jnp.concatenate(
        [m_ref[:, 0:16], jnp.where(even, mb, ma), jnp.where(even, ma, mb), jnp.zeros((24, 80), F32)], axis=1
    )
    blocks = f_ref[...] + ra_ref[48:72, 0:128]
    m_out[...] = window
    f_out[...] = blocks
    none = jnp.zeros((24, 128), F32)
    for ref in (near_ref, far_ref):
        ref[48:72, 0:128] = window
        ref[48:72, 128:256] = none
    near_ref[72:96, 0:128] = blocks
    near_ref[72:96, 128:256] = none
    n = row_of(LEAVES)
    i = (n >> 2) - 2
    ox = jnp.where(i >= 0, i + 4, i).astype(F32) - 1.5
    oy = (n & 3).astype(F32) - 1.5
    build_features(halo[0], halo[1], halo[2], ox, oy, None, stage_s, stage_w, None, s_ref, w_ref, 0, False)


def leaf_halo(which, info, r_ref, s_ref, w_ref, stage_s, stage_w):
    leaf_even = info[3] == 0
    to_right = leaf_even if which == 0 else jnp.logical_not(leaf_even)
    valid = jnp.float32(1.0) if which == 0 else info[4].astype(F32)
    n = row_of(LEAVES)
    ox = (n >> 1).astype(F32) - 3.5
    side = (n & 1).astype(F32)
    oy = jnp.where(to_right, side + 4.0, side - 2.0) - 1.5
    build_features(
        r_ref[0:16], r_ref[16:32], r_ref[32:48] * valid, ox, oy, None, stage_s, stage_w, None, s_ref, w_ref, 0, False
    )


def prepare_leaf_near(info, r_ref, f_ref, send_ref, after_ref, s_ref, w_ref, f_out, send_out, stage_s, stage_w):
    blocks = f_ref[...] + r_ref[72:96, 0:128]
    f_out[...] = blocks
    send_out[0:72] = send_ref[...]
    send_out[72:96, 0:128] = blocks
    send_out[72:96, 128:256] = jnp.zeros((24, 128), F32)
    leaf_halo(0, info, r_ref, s_ref, w_ref, stage_s, stage_w)


def prepare_leaf_far(info, r_ref, f_ref, after_ref, s_ref, w_ref, f_out, stage_s, stage_w):
    f_out[...] = f_ref[...] + r_ref[72:96, 0:128]
    leaf_halo(1, info, r_ref, s_ref, w_ref, stage_s, stage_w)


def direct(bodies, unroll, zero, info, table, mask, t_ref, s_ref, w_ref, *refs):
    acc_ref = refs[-1]
    if zero:
        acc_ref[...] = jnp.zeros_like(acc_ref)
    else:
        acc_ref[...] = refs[0][...]
    shift = info[5]

    def step(b, unused):
        for n in range(unroll):
            at = (b * unroll + n) * 3 + shift
            t = table[at]
            s = table[at + 1]
            weight = mask[table[at + 2] * LEAVES + t]
            distance = jnp.dot(s_ref[s], t_ref[t], preferred_element_type=F32)
            kernel = 1.0 / distance
            high = kernel.astype(BF16)
            low = (kernel - high.astype(F32)).astype(BF16)
            w = w_ref[s]
            total = jnp.dot(w, high, preferred_element_type=F32) + jnp.dot(w, low, preferred_element_type=F32)
            acc_ref[t] = acc_ref[t] + weight * total
        return 0

    lax.fori_loop(0, bodies, step, 0)


def pair_table(kind, to_right=False):
    out = []
    for t in range(LEAVES):
        i, j = divmod(t, SIDE)
        for a, b in near_steps:
            o = cycle_steps.index((a, b)) if max(abs(a), abs(b)) == 2 else 16
            si, sj = i + a, j + b
            in_row, in_column = 0 <= si < SIDE, 0 <= sj < SIDE
            if kind == "own" and in_row and in_column:
                out.append((t, si * SIDE + sj, o))
            if kind == "slab" and not in_row and in_column:
                out.append((t, ((si + 2) if si < 0 else (si - 2)) * SIDE + sj, o))
            if kind == "leaf" and not in_column and (sj >= SIDE) == to_right:
                out.append((t, (si + 2) * 2 + (sj - SIDE if to_right else sj + 2), o))
    return np.array(out, np.int32)


def finish(info, part_ref, nm_ref, acc_ref, m_ref, r1_ref, r2_ref, f_ref, out_ref):
    leaf_even = info[3] == 0
    valid = info[4].astype(F32)
    wx = own_rows(part_ref, 0)
    wy = own_rows(part_ref, 1)
    ox, oy = leaf_offsets()
    n = row_of(LEAVES)
    ti = n >> 2
    tj = n & 3
    lane = lax.broadcasted_iota(jnp.int32, (LEAVES, 128), 1)
    k = lane >> 4
    r = lane & 15
    si = jnp.where(k == 0, r >> 2, jnp.where(k == 1, (r >> 2) - 4, (r >> 2) + 4))
    near_shift = jnp.where(leaf_even, 4, -4)
    xs = []
    ys = []
    weights = []
    for column in (0, near_shift, -near_shift):
        sj = (r & 3) + column
        dx = si - ti
        dy = sj - tj
        reach = jnp.maximum(jnp.abs(dx), jnp.abs(dy))
        weight = jnp.where(reach >= 3, 1.0, 0.0).astype(F32)
        for o, (a, b) in enumerate(cycle_steps):
            hit = jnp.logical_and(dx == a, dy == b)
            weight = jnp.where(hit, 1.0 - nm_ref[:, o : o + 1], weight)
        weight = jnp.where(k < 3, weight, 0.0)
        used = jnp.logical_and(reach >= 2, k < 3)
        xs.append(jnp.where(used, dx.astype(F32), 1.0))
        ys.append(jnp.where(used, dy.astype(F32), 1.0))
        weights.append(weight)
    bx = (lane >> 2) - info[0]
    by = (lane & 3) - info[1]
    remote = jnp.maximum(jnp.abs(bx), jnp.abs(by)) >= 2
    xs.append(jnp.where(remote, (bx * SIDE - ti).astype(F32) + 1.5, 1.0))
    ys.append(jnp.where(remote, (by * SIDE - tj).astype(F32) + 1.5, 1.0))
    weights.append(jnp.where(remote, 1.0, 0.0).astype(F32))
    tx = jnp.concatenate(xs, axis=1)
    ty = jnp.concatenate(ys, axis=1)
    weight = jnp.concatenate(weights, axis=1)
    square = tx * tx + ty * ty
    inv_x = tx / square
    inv_y = -ty / square
    h_re = [weight * inv_x]
    h_im = [weight * inv_y]
    for order in range(1, 2 * ORDER - 1):
        a, b = h_re[-1], h_im[-1]
        h_re.append((a * inv_x - b * inv_y) * float(order))
        h_im.append((a * inv_y + b * inv_x) * float(order))

    def source(row):
        return jnp.concatenate(
            [
                m_ref[row : row + 1, :],
                r1_ref[48 + row : 49 + row, 0:128],
                r2_ref[48 + row : 49 + row, 0:128] * valid,
                f_ref[row : row + 1, :],
            ],
            axis=1,
        )

    a_re = []
    a_im = []
    for k_ in range(ORDER):
        scale = (-1.0) ** (k_ + 1) / math.factorial(k_)
        a_re.append(jnp.broadcast_to(source(k_) * scale, (LEAVES, 512)))
        a_im.append(jnp.broadcast_to(source(ORDER + k_) * scale, (LEAVES, 512)))
    p_re, p_im = power_list(wx, wy, ORDER)
    x = wx + ox
    y = wy + oy
    rows = lambda at: acc_ref[:, at, :] + acc_ref[:, at + 1, :] + acc_ref[:, at + 2, :]
    total = rows(0)
    sum_re = x * total - rows(3)
    sum_im = rows(6) - y * total
    for m in range(ORDER):
        part_re = jnp.zeros((LEAVES, 512), F32)
        part_im = jnp.zeros((LEAVES, 512), F32)
        for k_ in range(ORDER):
            part_re = part_re + (h_re[m + k_] * a_re[k_] - h_im[m + k_] * a_im[k_])
            part_im = part_im + (h_re[m + k_] * a_im[k_] + h_im[m + k_] * a_re[k_])
        scale = 1.0 / math.factorial(m)
        l_re = jnp.sum(part_re, 1, keepdims=True) * scale
        l_im = jnp.sum(part_im, 1, keepdims=True) * scale
        sum_re = sum_re + (l_re * p_re[m] - l_im * p_im[m])
        sum_im = sum_im + (l_re * p_im[m] + l_im * p_re[m])
    sum_re = sum_re * (1.0 / TWO_PI)
    sum_im = sum_im * (1.0 / TWO_PI)
    for i in range(SIDE):
        out_ref[0, i] = sum_im[4 * i : 4 * i + 4]
        out_ref[1, i] = sum_re[4 * i : 4 * i + 4]


V = pl.BlockSpec(memory_space=pltpu.VMEM)
S = pl.BlockSpec(memory_space=pltpu.SMEM)
A = pl.BlockSpec(memory_space=pl.ANY)


def shaped(*shape, dtype=F32):
    return jax.ShapeDtypeStruct(shape, dtype)


def call(kernel, name, in_specs, outs, scratch, cost, aliases=None):
    return pl.pallas_call(
        kernel,
        out_shape=outs,
        in_specs=in_specs,
        out_specs=jax.tree.map(lambda unused: V, outs),
        scratch_shapes=scratch,
        name=name,
        input_output_aliases=aliases or {},
        cost_estimate=pl.CostEstimate(flops=cost, bytes_accessed=1 << 20, transcendentals=0),
        compiler_params=pltpu.CompilerParams(vmem_limit_bytes=VMEM_LIMIT),
    )


def features_out(count):
    return [shaped(count, SIZE, FEATURES, dtype=BF16), shaped(count, 16, SIZE, dtype=BF16)]


def stages(with_target):
    out = [pltpu.VMEM((LEAVES, FEATURES, SIZE), F32), pltpu.VMEM((LEAVES, 16, SIZE), F32)]
    return ([pltpu.VMEM((LEAVES, FEATURES, SIZE), F32)] if with_target else []) + out


SMALL = 4_000_000
PAIR = 400_000_000


def run_direct(name, info, table, mask, feats, acc, bodies, unroll, shift):
    zero = acc is None
    ins = [info.at[5].set(shift) if shift is not None else info, table, mask, *feats]
    if not zero:
        ins.append(acc)
    return call(
        functools.partial(direct, bodies, unroll, zero),
        name,
        [S, S, S, V, V, V] + ([] if zero else [V]),
        shaped(LEAVES, 16, SIZE),
        [],
        PAIR * bodies * unroll,
        {} if zero else {6: 0},
    )(*ins)


def body(particles, near_mask):
    slab = lax.axis_index(SLAB)
    leaf = lax.axis_index("leaf")
    has_far = jnp.logical_and(leaf > 0, leaf < 3).astype(jnp.int32)
    zero = jnp.zeros_like(slab)
    info = jnp.stack([slab, leaf, slab % 2, leaf % 2, has_far, zero, zero, zero]).astype(jnp.int32)
    mask_rows = near_mask.reshape(16, LEAVES).astype(F32)
    mask = jnp.concatenate([mask_rows.reshape(-1), jnp.ones((LEAVES,), F32)])
    mask_turned = mask_rows.T

    t0, s0, w0, m0, f0, send_a, send_b = call(
        prepare_own,
        "prepare_own",
        [S, V],
        [shaped(LEAVES, FEATURES, SIZE, dtype=BF16), *features_out(LEAVES), shaped(24, 128), shaped(24, 128)]
        + [shaped(SLAB_ROWS, SIZE)] * 2,
        stages(True),
        SMALL,
    )(info, particles)
    recv_a = swap(send_a, "core")
    recv_b = swap(send_b, "slab")
    own = jnp.asarray(pair_table("own").reshape(-1))
    feats = (t0, s0, w0)
    acc = run_direct("direct_own_0", info, own, mask, feats, None, 3, 28, None)
    s1, w1, m1, f1, send_near, send_far = call(
        prepare_slab,
        "prepare_slab",
        [S, V, V, V, V, V, A],
        [*features_out(LEAVES), shaped(24, 128), shaped(24, 128), shaped(LEAF_ROWS, SIZE), shaped(72, SIZE)],
        stages(False),
        SMALL,
    )(info, particles, recv_a, recv_b, m0, f0, acc)
    send_near, acc = lax.optimization_barrier((send_near, acc))
    recv_near = swap(send_near, "leaf_near")
    own_1 = jnp.asarray(pair_table("own")[84:140].reshape(-1))
    own_2 = jnp.asarray(pair_table("own")[140:].reshape(-1))
    acc = run_direct("direct_own_1", info, own_1, mask, feats, acc, 2, 28, None)
    s2, w2, f2, send_far = call(
        prepare_leaf_near,
        "prepare_leaf_near",
        [S, V, V, V, A],
        [*features_out(LEAVES), shaped(24, 128), shaped(LEAF_ROWS, SIZE)],
        stages(False),
        SMALL,
    )(info, recv_near, f1, send_far, acc)
    send_far, acc = lax.optimization_barrier((send_far, acc))
    recv_far = swap(send_far, "leaf_far")
    acc = run_direct("direct_own_2", info, own_2, mask, feats, acc, 2, 28, None)
    s3, w3, f3 = call(
        prepare_leaf_far,
        "prepare_leaf_far",
        [S, V, V, A],
        [*features_out(LEAVES), shaped(24, 128)],
        stages(False),
        SMALL,
    )(info, recv_far, f2, acc)
    f3, acc = lax.optimization_barrier((f3, acc))
    got = swap(f3, "z_near")
    slab_pairs = jnp.asarray(pair_table("slab").reshape(-1))
    acc = run_direct("direct_slab", info, slab_pairs, mask, (t0, s1, w1), acc, 3, 28, None)
    got, acc = lax.optimization_barrier((got, acc))
    f4 = f3 + got
    f4, acc = lax.optimization_barrier((f4, acc))
    got = swap(f4, "z_far")
    right = pair_table("leaf", True).reshape(-1)
    left = pair_table("leaf", False).reshape(-1)
    parity = leaf % 2
    near_pairs = jnp.asarray(np.concatenate([right, left]))
    far_pairs = jnp.asarray(np.concatenate([left, right]))
    acc = run_direct("direct_leaf_near", info, near_pairs, mask, (t0, s2, w2), acc, 2, 30, parity * 180)
    got, acc = lax.optimization_barrier((got, acc))
    f5 = f4 + got
    f5, acc = lax.optimization_barrier((f5, acc))
    got = swap(f5, "x_near")
    acc = run_direct("direct_leaf_far_0", info, far_pairs, mask, (t0, s3, w3), acc, 1, 30, parity * 180)
    got, acc = lax.optimization_barrier((got, acc))
    f6 = f5 + got
    f6, acc = lax.optimization_barrier((f6, acc))
    got = swap(f6, "x_far")
    acc = run_direct("direct_leaf_far_1", info, far_pairs, mask, (t0, s3, w3), acc, 1, 30, parity * 180 + 90)
    got, acc = lax.optimization_barrier((got, acc))
    f7 = f6 + got
    return call(
        finish, "finish", [S] + [V] * 7, shaped(2, SIDE, SIDE, SIZE), [], SMALL
    )(info, particles, mask_turned, acc, m1, recv_near, recv_far, f7)


def solution(mesh):
    finer = Mesh(mesh.devices.reshape(4, 4, 2, mesh.shape["leaf"]), ALL)
    in_specs = (P(None, SLAB, "leaf", None), P(None, SLAB, "leaf"))
    out_specs = P(None, SLAB, "leaf", None)
    run = jax.shard_map(body, mesh=finer, in_specs=in_specs, out_specs=out_specs, check_vma=False)

    def whole(particles, near_mask):
        with jax.sharding.use_abstract_mesh(mesh.abstract_mesh):
            return run(particles, near_mask)

    return run
```

time: 611 us -> 79.9 us (0.13)
  matrix products: 249 us -> 0 us
  local copies, waits for them, and re-layouts: 146 us -> 4.34 us
  other arithmetic: 108 us -> 0.62 us
  Pallas kernels: 0 us -> 59.3 us
  blocking collectives: 42.2 us -> 0 us
  loops' own time: 36.4 us -> 0 us
  starting transfers between devices: 20.6 us -> 14.3 us
    dot_general x88 -> x0, matrix products: 249 us -> none  [the longest x16 60.3 us: block_group(): jnp.einsum('nijlk,nk->ijl', matrix_real, group_blocks[:, 1], precision=hi...]
    gather x100 -> x0, local copies, waits for them, and re-layouts: 112 us -> none  [the longest x44 39.8 us: translation(): power_imaginary[..., hankel] * weights]
    pallas_call x0 -> x12, Pallas kernels: none -> 59.3 us  [the longest x7 45.9 us: run_direct(): call(functools.partial(direct, bodies, unroll, zero), name, [S, S, S, V,...]
    reduce_sum x22 -> x0, other arithmetic: 56.4 us -> none  [the longest x20 55.9 us: direct_row(): row_imaginary = row_imaginary - jnp.sum(factor * delta_y, -1)]
    all_gather x4 -> x0, blocking collectives: 42.2 us -> none  [stacked_from(): blocks = lax.all_gather(blocks, axes[k], axis=0, tiled=True)]
    another operation x3 -> x0, loops' own time: 36.4 us -> none  [the longest x1 34 us: body(): lax.map(direct_row, jnp.arange(block_side, dtype=jnp.int32))]
    while x544 -> x0, other arithmetic: 31.8 us -> none
    sub x36 -> x0, local copies, waits for them, and re-layouts: 22.3 us -> none  [the longest x16 11.2 us: block_group(): group_y[:, None, None] - global_y[None, None, :]]
  transfers between devices with their start and end apart: 8 -> 8, of which waited for: 3 -> 0; matrix products, arithmetic and copies ran while one was open for 71% -> 1% of each run, Pallas kernels for 0% -> 58%
where the time goes in v1:
time: 79.9 us; the launch traced here: 78.7 us
  Pallas kernels  59.3 us (74%)
  starting transfers between devices  14.3 us (18%)
  local copies, waits for them, and re-layouts  4.34 us (5%)
    pallas_call x7, Pallas kernels, run_direct(): call(functools.partial(direct, bodies, unroll, zero), name, [S, S, S, V,...  45.9 us
    ppermute x8, starting transfers between devices, swap(): return lax.ppermute(value, ALL, SWAPS[name])  14.3 us
    pallas_call x1, Pallas kernels, body(): call(finish, 'finish', [S] + [V] * 7, shaped(2, SIDE, SIDE, SIZE), [], SM...  3.2 us
    unnamed x22, local copies, waits for them, and re-layouts  2.9 us
    pallas_call x1, Pallas kernels, body(): call(prepare_own, 'prepare_own', [S, V], [shaped(LEAVES, FEATURES, SIZE,...  2.66 us
    pallas_call x1, Pallas kernels, body(): call(prepare_slab, 'prepare_slab', [S, V, V, V, V, V, A], [*features_out(...  2.57 us
    pallas_call x1, Pallas kernels, body(): call(prepare_leaf_near, 'prepare_leaf_near', [S, V, V, V, A], [*features_...  2.53 us
    pallas_call x1, Pallas kernels, body(): call(prepare_leaf_far, 'prepare_leaf_far', [S, V, V, A], [*features_out(L...  2.48 us
  transfers between devices with their start and end apart: 8, of which 0 were waited for; matrix products, arithmetic and copies ran while one was open for 1% of the time, Pallas kernels for 58%

profile of v1, /device:TPU:0, one launch (start us, length us, event | category | flops | bytes accessed | tf_op | source)
XLA Modules:
  0.0 78.7 jit_solution(9914922062176420480)
XLA Ops:
  0.0 0.6 stack.27.info
  0.6 2.7 %prepare_own.1 = (bf16[16,32,256]{2,1,0:T(8,128)(2,1)}, bf16[16,256,32]{2,1,0:T(8,128)(2,1)}, bf16[16,16,256]{2,1,0:T(8,128)(2,1)}, f32[24,128]{1,0:T(8,128)}, f...) custom-call(s32[8]{0:T(128)} %stack.27.info, f32[3,4,4,256]{3,2,1,0:T(4,128)} %part_ref.5), custom_call_target="tpu_custom_call" | custom-call | flops 4000000 | bytes 1048576 | tf_op jit(solution)/shard_map/prepare_own/pallas_call | solution.py:452
  3.3 0.7 collective-permute-start.1
  4.7 0.6 concatenate.8.mask
  5.3 8.6 %direct_own_0.1.after_ref.refs_0_ = f32[16,16,256]{2,1,0:T(8,128)} custom-call(s32[8]{0:T(128)} %stack.27.info, s32[588]{0:T(1024)} %constant.115.clone.table, f32[272]{0:T(512)} %concatenate.8.mask, bf16[16,32,256]{2,1,0:T(8,128)(2,1)} %get-tuple-element.81.t_ref, bf16[16,256,32]{2,1,0:T(8,128)(2,1)} %get-tuple-element.82.s_ref, ...), custom_call_target="tpu_custom_call" | custom-call | flops 33600000000 | bytes 1048576 | tf_op jit(solution)/shard_map/direct_own_0/pallas_call | solution.py:431
  15.1 2.6 %prepare_slab.1 = (bf16[16,256,32]{2,1,0:T(8,128)(2,1)}, bf16[16,16,256]{2,1,0:T(8,128)(2,1)}, f32[24,128]{1,0:T(8,128)}, f32[24,128]{1,0:T(8,128)}, f32[96,256]{1,0:T(8,128)}, /*index=5*/f32[72,256]{1,0:T(8,128)}) custom-call(s32[8]{0:T(128)} %stack.27.info, f32[3,4,4,256]{3,2,1,0:T(4,128)} %part_ref.5, f32[72,256]{1,0:T(8,128)} %copy-done.2, ...), custom_call_target="tpu_custom_call" | custom-call | flops 4000000 | bytes 1048576 | tf_op jit(solution)/shard_map/prepare_slab/pallas_call | solution.py:466
  17.7 1.7 %collective-permute-start.2 = (f32[96,256]{1,0:T(8,128)}, f32[96,256]{1,0:T(8,128)S(1)}, u32[]{:S(2)}, u32[]{:S(2)}) collective-permute-start(f32[96,256]{1,0:T(8,128)} %get-tuple-element.85), channel_id=1, source_target_pairs={{0,1},{1,0},{2,3},{3,2},{4,5},{5,4},{6,7},{7,6},{8,9},{9,8},{10,11... | collective-permute-start | bytes 294920 | tf_op jit(solution)/shard_map/ppermute | solution.py:71
  19.3 6.5 %direct_own_1.1.after_ref.refs_0_ = f32[16,16,256]{2,1,0:T(8,128)} custom-call(s32[8]{0:T(128)} %stack.27.info, s32[168]{0:T(256)} %constant.116.clone.table, f32[272]{0:T(512)} %concatenate.8.mask, bf16[16,32,256]{2,1,0:T(8,128)(2,1)} %get-tuple-element.81.t_ref, bf16[16,256,32]{2,1,0:T(8,128)(2,1)} %get-tuple-element.82.s_ref, ...), custom_call_target="tpu_custom_call", output_to_operand_aliasing={{}: (6, {})} | custom-call | flops 22400000000 | bytes 1048576 | tf_op jit(solution)/shard_map/direct_own_1/pallas_call | solution.py:431
  25.8 0.6 copy-done
  26.5 2.5 %prepare_leaf_near.1 = (bf16[16,256,32]{2,1,0:T(8,128)(2,1)}, bf16[16,16,256]{2,1,0:T(8,128)(2,1)}, f32[24,128]{1,0:T(8,128)}, f32[96,256]{1,0:T(8,128)}) custom-call(s32[8]{0:T(128)} %stack.27.info, f32[96,256]{1,0:T(8,128)} %copy-done, f32[24,128]{1,0:T(8,128)} %get-tuple-element.86.f_ref, f32[72,256]{1,0:T(8,128)} %get-tuple-element.87.send_ref, ...), custom_call_target="tpu_custom_call" | custom-call | flops 4000000 | bytes 1048576 | tf_op jit(solution)/shard_map/prepare_leaf_near/pallas_call | solution.py:479
  29.0 2.2 %collective-permute-start.3 = (f32[96,256]{1,0:T(8,128)}, f32[96,256]{1,0:T(8,128)S(1)}, u32[]{:S(2)}, u32[]{:S(2)}) collective-permute-start(f32[96,256]{1,0:T(8,128)} %get-tuple-element.90), channel_id=1, source_target_pairs={{0,3},{1,2},{2,1},{3,0},{4,7},{5,6},{6,5},{7,4},{8,11},{9,10},{10,... | collective-permute-start | bytes 294920 | tf_op jit(solution)/shard_map/ppermute | solution.py:71
  31.2 6.5 %direct_own_2.1.after_ref.refs_0_ = f32[16,16,256]{2,1,0:T(8,128)} custom-call(s32[8]{0:T(128)} %stack.27.info, s32[168]{0:T(256)} %constant.117.clone.table, f32[272]{0:T(512)} %concatenate.8.mask, bf16[16,32,256]{2,1,0:T(8,128)(2,1)} %get-tuple-element.81.t_ref, bf16[16,256,32]{2,1,0:T(8,128)(2,1)} %get-tuple-element.82.s_ref, ...), custom_call_target="tpu_custom_call", output_to_operand_aliasing={{}: (6, {})} | custom-call | flops 22400000000 | bytes 1048576 | tf_op jit(solution)/shard_map/direct_own_2/pallas_call | solution.py:431
  37.7 0.6 copy-done.1
  38.3 2.5 %prepare_leaf_far.1 = (bf16[16,256,32]{2,1,0:T(8,128)(2,1)}, bf16[16,16,256]{2,1,0:T(8,128)(2,1)}, f32[24,128]{1,0:T(8,128)}) custom-call(s32[8]{0:T(128)} %stack.27.info, f32[96,256]{1,0:T(8,128)} %copy-done.1, f32[24,128]{1,0:T(8,128)} %get-tuple-element.91.f_ref, f32[16,16,256]{2,1,0:T(8,128)} %direct_own_2.1.after_ref.refs_0_), custom_call_target="tpu_custom_call" | custom-call | flops 4000000 | bytes 1048576 | tf_op jit(solution)/shard_map/prepare_leaf_far/pallas_call | solution.py:490
  40.8 3.4 %collective-permute-start.4 = (f32[24,128]{1,0:T(8,128)}, f32[24,128]{1,0:T(8,128)S(1)}, u32[]{:S(2)}, u32[]{:S(2)}) collective-permute-start(f32[24,128]{1,0:T(8,128)} %get-tuple-element.94), channel_id=1, source_target_pairs={{0,8},{1,9},{2,10},{3,11},{4,12},{5,13},{6,14},{7,15},{8,0},{9,1},... | collective-permute-start | bytes 36872 | tf_op jit(solution)/shard_map/ppermute | solution.py:71
  44.2 8.7 %direct_slab.1.refs_0_ = f32[16,16,256]{2,1,0:T(8,128)} custom-call(s32[8]{0:T(128)} %stack.27.info, s32[252]{0:T(256)} %constant.118.clone.table, f32[272]{0:T(512)} %concatenate.8.mask, bf16[16,32,256]{2,1,0:T(8,128)(2,1)} %get-tuple-element.81.t_ref, bf16[16,256,32]{2,1,0:T(8,128)(2,1)} %get-tuple-element.95.s_ref, ...), custom_call_target="tpu_custom_call", output_to_operand_aliasing={{}: (6, {})} | custom-call | flops 33600000000 | bytes 1048576 | tf_op jit(solution)/shard_map/direct_slab/pallas_call | solution.py:431
  52.9 2.6 %collective-permute-start.5 = (f32[24,128]{1,0:T(8,128)S(1)}, f32[24,128]{1,0:T(8,128)S(1)}, u32[]{:S(2)}, u32[]{:S(2)}) collective-permute-start(f32[24,128]{1,0:T(8,128)S(1)} %add.40), channel_id=1, source_target_pairs={{0,24},{1,25},{2,26},{3,27},{4,28},{5,29},{6,30},{7,31},{8,16},{9,... | collective-permute-start | bytes 36872 | tf_op jit(solution)/shard_map/ppermute | solution.py:71
  55.5 6.8 %direct_leaf_near.1.refs_0_ = f32[16,16,256]{2,1,0:T(8,128)} custom-call(s32[8]{0:T(128)} %copy-done.9, s32[360]{0:T(512)} %constant.119.clone.table, f32[272]{0:T(512)} %concatenate.8.mask, bf16[16,32,256]{2,1,0:T(8,128)(2,1)} %get-tuple-element.81.t_ref, bf16[16,256,32]{2,1,0:T(8,128)(2,1)} %get-tuple-element.101.s_ref, ...), custom_call_target="tpu_custom_call", output_to_operand_aliasing={{}: (6, {})} | custom-call | flops 24000000000 | bytes 1048576 | tf_op jit(solution)/shard_map/direct_leaf_near/pallas_call | solution.py:431
  62.3 1.6 %collective-permute-start.6 = (f32[24,128]{1,0:T(8,128)S(1)}, f32[24,128]{1,0:T(8,128)S(1)}, u32[]{:S(2)}, u32[]{:S(2)}) collective-permute-start(f32[24,128]{1,0:T(8,128)S(1)} %add.41), channel_id=1, source_target_pairs={{0,32},{1,33},{2,34},{3,35},{4,36},{5,37},{6,38},{7,39},{8,40},{9,... | collective-permute-start | bytes 36872 | tf_op jit(solution)/shard_map/ppermute | solution.py:71
  63.8 4.4 %direct_leaf_far_0.1.refs_0_ = f32[16,16,256]{2,1,0:T(8,128)} custom-call(s32[8]{0:T(128)} %copy-done.9, s32[360]{0:T(512)} %constant.120.clone.table, f32[272]{0:T(512)} %concatenate.8.mask, bf16[16,32,256]{2,1,0:T(8,128)(2,1)} %get-tuple-element.81.t_ref, bf16[16,256,32]{2,1,0:T(8,128)(2,1)} %get-tuple-element.107.s_ref, ...), custom_call_target="tpu_custom_call", output_to_operand_aliasing={{}: (6, {})} | custom-call | flops 12000000000 | bytes 1048576 | tf_op jit(solution)/shard_map/direct_leaf_far_0/pallas_call | solution.py:431
  68.3 2.2 %collective-permute-start.7 = (f32[24,128]{1,0:T(8,128)S(1)}, f32[24,128]{1,0:T(8,128)S(1)}, u32[]{:S(2)}, u32[]{:S(2)}) collective-permute-start(f32[24,128]{1,0:T(8,128)S(1)} %add.42), channel_id=1, source_target_pairs={{0,96},{1,97},{2,98},{3,99},{4,100},{5,101},{6,102},{7,103},{8,104... | collective-permute-start | bytes 36872 | tf_op jit(solution)/shard_map/ppermute | solution.py:71
  70.4 4.4 %direct_leaf_far_1.1.acc_ref = f32[16,16,256]{2,1,0:T(8,128)} custom-call(s32[8]{0:T(128)} %copy-done.8, s32[360]{0:T(512)} %constant.120.clone.table, f32[272]{0:T(512)} %concatenate.8.mask, bf16[16,32,256]{2,1,0:T(8,128)(2,1)} %get-tuple-element.81.t_ref, bf16[16,256,32]{2,1,0:T(8,128)(2,1)} %get-tuple-element.107.s_ref, ...), custom_call_target="tpu_custom_call", output_to_operand_aliasing={{}: (6, {})} | custom-call | flops 12000000000 | bytes 1048576 | tf_op jit(solution)/shard_map/direct_leaf_far_1/pallas_call | solution.py:431
  74.9 0.6 add.44.f_ref
  75.5 3.2 %finish.1 = f32[2,4,4,256]{3,2,1,0:T(4,128)} custom-call(s32[8]{0:T(128)} %stack.27.info, f32[3,4,4,256]{3,2,1,0:T(4,128)} %part_ref.5, f32[16,16]{1,0:T(8,128)} %bitcast.10, f32[16,16,256]{2,1,0:T(8,128)} %direct_leaf_far_1.1.acc_ref, f32[24,128]{1,0:T(8,128)} %get-tuple-element.115.m_ref, f32[96,256]{1,0:T(8,128)} %copy-done, f32[96,256]{1,0:T(8,128)} %copy-done.1, ...), custom_call_target="tpu_custom_call" | custom-call | flops 4000000 | bytes 1048576 | tf_op jit(solution)/shard_map/finish/pallas_call | solution.py:524
  (38 shorter events, 1.9 us)
Async XLA Ops:
  0.6 3.3 %copy-start.7 = (s32[16,4,4]{0,2,1:T(4,128)S(1)}, s32[16,4,4]{0,2,1:T(4,128)}, u32[]{:S(2)}) copy-start(s32[16,4,4]{0,2,1:T(4,128)} %param.15) | copy-start | bytes 3076
  3.3 11.2 %collective-permute-start = (f32[72,256]{1,0:T(8,128)}, f32[72,256]{1,0:T(8,128)S(1)}, u32[]{:S(2)}, u32[]{:S(2)}) collective-permute-start(f32[72,256]{1,0:T(8,128)} %get-tuple-element.77), channel_id=1, source_target_pairs={{0,4},{1,5},{2,6},{3,7},{4,0},{5,1},{6,2},{7,3},{8,12},{9,13},{10,... | collective-permute-start | bytes 221192 | tf_op jit(solution)/shard_map/ppermute | solution.py:71
  3.3 11.2 %collective-permute-start.1 = (f32[72,256]{1,0:T(8,128)}, f32[72,256]{1,0:T(8,128)S(1)}, u32[]{:S(2)}, u32[]{:S(2)}) collective-permute-start(f32[72,256]{1,0:T(8,128)} %get-tuple-element.78), channel_id=1, source_target_pairs={{4,8},{5,9},{6,10},{7,11},{8,4},{9,5},{10,6},{11,7},{12,16},{13,17... | collective-permute-start | bytes 221192 | tf_op jit(solution)/shard_map/ppermute | solution.py:71
  4.0 0.6 copy-start.4
  5.3 8.6 %copy-start.5 = (s32[8]{0:T(128)S(1)}, s32[8]{0:T(128)}, u32[]{:S(2)}) copy-start(s32[8]{0:T(128)} %stack.27.info) | copy-start | bytes 100
  13.9 0.5 copy-start.9
  14.4 0.6 copy-start.8
  14.4 0.6 copy-start.2
  14.5 0.6 copy-start.3
  17.7 8.2 %collective-permute-start.2 = (f32[96,256]{1,0:T(8,128)}, f32[96,256]{1,0:T(8,128)S(1)}, u32[]{:S(2)}, u32[]{:S(2)}) collective-permute-start(f32[96,256]{1,0:T(8,128)} %get-tuple-element.85), channel_id=1, source_target_pairs={{0,1},{1,0},{2,3},{3,2},{4,5},{5,4},{6,7},{7,6},{8,9},{9,8},{10,11... | collective-permute-start | bytes 294920 | tf_op jit(solution)/shard_map/ppermute | solution.py:71
  25.8 0.6 copy-start
  29.0 8.7 %collective-permute-start.3 = (f32[96,256]{1,0:T(8,128)}, f32[96,256]{1,0:T(8,128)S(1)}, u32[]{:S(2)}, u32[]{:S(2)}) collective-permute-start(f32[96,256]{1,0:T(8,128)} %get-tuple-element.90), channel_id=1, source_target_pairs={{0,3},{1,2},{2,1},{3,0},{4,7},{5,6},{6,5},{7,4},{8,11},{9,10},{10,... | collective-permute-start | bytes 294920 | tf_op jit(solution)/shard_map/ppermute | solution.py:71
  37.7 0.6 copy-start.1
  40.8 12.1 %collective-permute-start.4 = (f32[24,128]{1,0:T(8,128)}, f32[24,128]{1,0:T(8,128)S(1)}, u32[]{:S(2)}, u32[]{:S(2)}) collective-permute-start(f32[24,128]{1,0:T(8,128)} %get-tuple-element.94), channel_id=1, source_target_pairs={{0,8},{1,9},{2,10},{3,11},{4,12},{5,13},{6,14},{7,15},{8,0},{9,1},... | collective-permute-start | bytes 36872 | tf_op jit(solution)/shard_map/ppermute | solution.py:71
  44.2 8.7 %copy-start.6 = (f32[24,128]{1,0:T(8,128)S(1)}, f32[24,128]{1,0:T(8,128)}, u32[]{:S(2)}) copy-start(f32[24,128]{1,0:T(8,128)} %get-tuple-element.94) | copy-start | bytes 36868
  52.9 9.4 %collective-permute-start.5 = (f32[24,128]{1,0:T(8,128)S(1)}, f32[24,128]{1,0:T(8,128)S(1)}, u32[]{:S(2)}, u32[]{:S(2)}) collective-permute-start(f32[24,128]{1,0:T(8,128)S(1)} %add.40), channel_id=1, source_target_pairs={{0,24},{1,25},{2,26},{3,27},{4,28},{5,29},{6,30},{7,31},{8,16},{9,... | collective-permute-start | bytes 36872 | tf_op jit(solution)/shard_map/ppermute | solution.py:71
  62.3 6.0 %collective-permute-start.6 = (f32[24,128]{1,0:T(8,128)S(1)}, f32[24,128]{1,0:T(8,128)S(1)}, u32[]{:S(2)}, u32[]{:S(2)}) collective-permute-start(f32[24,128]{1,0:T(8,128)S(1)} %add.41), channel_id=1, source_target_pairs={{0,32},{1,33},{2,34},{3,35},{4,36},{5,37},{6,38},{7,39},{8,40},{9,... | collective-permute-start | bytes 36872 | tf_op jit(solution)/shard_map/ppermute | solution.py:71
  68.3 6.6 %collective-permute-start.7 = (f32[24,128]{1,0:T(8,128)S(1)}, f32[24,128]{1,0:T(8,128)S(1)}, u32[]{:S(2)}, u32[]{:S(2)}) collective-permute-start(f32[24,128]{1,0:T(8,128)S(1)} %add.42), channel_id=1, source_target_pairs={{0,96},{1,97},{2,98},{3,99},{4,100},{5,101},{6,102},{7,103},{8,104... | collective-permute-start | bytes 36872 | tf_op jit(solution)/shard_map/ppermute | solution.py:71

commit v2 on v1

--- a/solution.py
+++ b/solution.py
@@ -21,7 +21,7 @@
 ALL = ("slab_0", "slab_1", "slab_2", "leaf")
 F32 = jnp.float32
 BF16 = jnp.bfloat16
-VMEM_LIMIT = 56 << 20
+VMEM_LIMIT = 6 << 20
 cycle_steps = [(a, b) for a in range(-2, 3) for b in range(-2, 3) if max(abs(a), abs(b)) == 2]
 near_steps = [(a, b) for a in range(-2, 3) for b in range(-2, 3)]
 
@@ -147,11 +147,19 @@
     return jnp.concatenate([ref[part, i] for i in range(SIDE)], axis=0)
 
 
+def position():
+    slab = lax.axis_index(SLAB)
+    leaf = lax.axis_index("leaf")
+    between = jnp.logical_and(leaf > 0, leaf < 3).astype(jnp.int32)
+    return slab, leaf, slab & 1, leaf & 1, between
+
+
 SLAB_ROWS = 72
 LEAF_ROWS = 96
 
 
-def prepare_own(info, part_ref, t_ref, s_ref, w_ref, m_ref, f_ref, a_ref, b_ref, stage_t, stage_s, stage_w):
+def prepare_own(part_ref, t_ref, s_ref, w_ref, m_ref, f_ref, a_ref, b_ref, stage_t, stage_s, stage_w):
+    info = position()
     wx = own_rows(part_ref, 0)
     wy = own_rows(part_ref, 1)
     g = own_rows(part_ref, 2)
@@ -188,8 +196,9 @@
 
 
 def prepare_slab(
-    info, part_ref, ra_ref, rb_ref, m_ref, f_ref, after_ref, s_ref, w_ref, m_out, f_out, near_ref, far_ref, stage_s, stage_w
+    part_ref, ra_ref, rb_ref, m_ref, f_ref, after_ref, s_ref, w_ref, m_out, f_out, near_ref, far_ref, stage_s, stage_w
 ):
+    info = position()
     even = info[2] == 0
     leaf_even = info[3] == 0
     halo = []
@@ -213,9 +222,10 @@
     m_out[...] = window
     f_out[...] = blocks
     none = jnp.zeros((24, 128), F32)
-    for ref in (near_ref, far_ref):
-        ref[48:72, 0:128] = window
-        ref[48:72, 128:256] = none
+    near_ref[48:72, 0:128] = jnp.concatenate([none[:, 0:48], window[:, 0:48], none[:, 0:32]], axis=1)
+    near_ref[48:72, 128:256] = none
+    far_ref[48:72, 0:128] = window
+    far_ref[48:72, 128:256] = none
     near_ref[72:96, 0:128] = blocks
     near_ref[72:96, 128:256] = none
     n = row_of(LEAVES)
@@ -225,7 +235,8 @@
     build_features(halo[0], halo[1], halo[2], ox, oy, None, stage_s, stage_w, None, s_ref, w_ref, 0, False)
 
 
-def leaf_halo(which, info, r_ref, s_ref, w_ref, stage_s, stage_w):
+def leaf_halo(which, r_ref, s_ref, w_ref, stage_s, stage_w):
+    info = position()
     leaf_even = info[3] == 0
     to_right = leaf_even if which == 0 else jnp.logical_not(leaf_even)
     valid = jnp.float32(1.0) if which == 0 else info[4].astype(F32)
@@ -238,34 +249,35 @@
     )
 
 
-def prepare_leaf_near(info, r_ref, f_ref, send_ref, after_ref, s_ref, w_ref, f_out, send_out, stage_s, stage_w):
+def prepare_leaf_near(r_ref, f_ref, send_ref, after_ref, s_ref, w_ref, f_out, send_out, stage_s, stage_w):
     blocks = f_ref[...] + r_ref[72:96, 0:128]
     f_out[...] = blocks
     send_out[0:72] = send_ref[...]
     send_out[72:96, 0:128] = blocks
     send_out[72:96, 128:256] = jnp.zeros((24, 128), F32)
-    leaf_halo(0, info, r_ref, s_ref, w_ref, stage_s, stage_w)
-
-
-def prepare_leaf_far(info, r_ref, f_ref, after_ref, s_ref, w_ref, f_out, stage_s, stage_w):
+    leaf_halo(0, r_ref, s_ref, w_ref, stage_s, stage_w)
+
+
+def prepare_leaf_far(r_ref, f_ref, after_ref, s_ref, w_ref, f_out, stage_s, stage_w):
     f_out[...] = f_ref[...] + r_ref[72:96, 0:128]
-    leaf_halo(1, info, r_ref, s_ref, w_ref, stage_s, stage_w)
-
-
-def direct(bodies, unroll, zero, info, table, mask, t_ref, s_ref, w_ref, *refs):
+    leaf_halo(1, r_ref, s_ref, w_ref, stage_s, stage_w)
+
+
+def direct(bodies, unroll, zero, by_side, table, mask, t_ref, s_ref, w_ref, *refs):
     acc_ref = refs[-1]
     if zero:
         acc_ref[...] = jnp.zeros_like(acc_ref)
     else:
         acc_ref[...] = refs[0][...]
-    shift = info[5]
+    shift = position()[3] * by_side if by_side else 0
 
     def step(b, unused):
         for n in range(unroll):
             at = (b * unroll + n) * 3 + shift
             t = table[at]
             s = table[at + 1]
-            weight = mask[table[at + 2] * LEAVES + t]
+            o = table[at + 2]
+            weight = jnp.where(o == 16, 1, mask[t >> 2, t & 3, o & 15]).astype(F32)
             distance = jnp.dot(s_ref[s], t_ref[t], preferred_element_type=F32)
             kernel = 1.0 / distance
             high = kernel.astype(BF16)
@@ -295,91 +307,111 @@
     return np.array(out, np.int32)
 
 
-def finish(info, part_ref, nm_ref, acc_ref, m_ref, r1_ref, r2_ref, f_ref, out_ref):
+WIDE = 3 * 128
+
+
+def finish(part_ref, nm_ref, acc_ref, m_ref, r1_ref, r2_ref, f_ref, got_ref, out_ref, h_ref, a_ref):
+    info = position()
     leaf_even = info[3] == 0
     valid = info[4].astype(F32)
-    wx = own_rows(part_ref, 0)
-    wy = own_rows(part_ref, 1)
-    ox, oy = leaf_offsets()
     n = row_of(LEAVES)
     ti = n >> 2
     tj = n & 3
     lane = lax.broadcasted_iota(jnp.int32, (LEAVES, 128), 1)
-    k = lane >> 4
-    r = lane & 15
+    near_mask = jnp.concatenate([nm_ref[i] for i in range(SIDE)], axis=0).astype(F32)
+    near_shift = jnp.where(leaf_even, 4, -4)
+    second = lane >= 48
+    place = jnp.where(second, lane - 48, lane)
+    k = place >> 4
+    r = place & 15
     si = jnp.where(k == 0, r >> 2, jnp.where(k == 1, (r >> 2) - 4, (r >> 2) + 4))
-    near_shift = jnp.where(leaf_even, 4, -4)
     xs = []
     ys = []
     weights = []
-    for column in (0, near_shift, -near_shift):
-        sj = (r & 3) + column
+    for column, lanes in ((jnp.where(second, near_shift, 0), 96), (-near_shift, 48)):
         dx = si - ti
-        dy = sj - tj
+        dy = (r & 3) + column - tj
         reach = jnp.maximum(jnp.abs(dx), jnp.abs(dy))
         weight = jnp.where(reach >= 3, 1.0, 0.0).astype(F32)
         for o, (a, b) in enumerate(cycle_steps):
             hit = jnp.logical_and(dx == a, dy == b)
-            weight = jnp.where(hit, 1.0 - nm_ref[:, o : o + 1], weight)
-        weight = jnp.where(k < 3, weight, 0.0)
-        used = jnp.logical_and(reach >= 2, k < 3)
+            weight = jnp.where(hit, 1.0 - near_mask[:, o : o + 1], weight)
+        inside = lane < lanes
+        used = jnp.logical_and(reach >= 2, inside)
         xs.append(jnp.where(used, dx.astype(F32), 1.0))
         ys.append(jnp.where(used, dy.astype(F32), 1.0))
-        weights.append(weight)
+        weights.append(jnp.where(inside, weight, 0.0))
     bx = (lane >> 2) - info[0]
     by = (lane & 3) - info[1]
     remote = jnp.maximum(jnp.abs(bx), jnp.abs(by)) >= 2
     xs.append(jnp.where(remote, (bx * SIDE - ti).astype(F32) + 1.5, 1.0))
     ys.append(jnp.where(remote, (by * SIDE - tj).astype(F32) + 1.5, 1.0))
     weights.append(jnp.where(remote, 1.0, 0.0).astype(F32))
-    tx = jnp.concatenate(xs, axis=1)
-    ty = jnp.concatenate(ys, axis=1)
-    weight = jnp.concatenate(weights, axis=1)
-    square = tx * tx + ty * ty
-    inv_x = tx / square
-    inv_y = -ty / square
-    h_re = [weight * inv_x]
-    h_im = [weight * inv_y]
-    for order in range(1, 2 * ORDER - 1):
-        a, b = h_re[-1], h_im[-1]
-        h_re.append((a * inv_x - b * inv_y) * float(order))
-        h_im.append((a * inv_y + b * inv_x) * float(order))
-
-    def source(row):
-        return jnp.concatenate(
-            [
-                m_ref[row : row + 1, :],
-                r1_ref[48 + row : 49 + row, 0:128],
-                r2_ref[48 + row : 49 + row, 0:128] * valid,
-                f_ref[row : row + 1, :],
-            ],
-            axis=1,
-        )
-
-    a_re = []
-    a_im = []
+    for group in range(3):
+        span = slice(128 * group, 128 * group + 128)
+        tx, ty, weight = xs[group], ys[group], weights[group]
+        square = tx * tx + ty * ty
+        inv_x = tx / square
+        inv_y = -ty / square
+        re = weight * inv_x
+        im = weight * inv_y
+        h_ref[0, :, span] = re
+        h_ref[1, :, span] = im
+        for order in range(1, 2 * ORDER - 1):
+            re, im = (re * inv_x - im * inv_y) * float(order), (re * inv_y + im * inv_x) * float(order)
+            h_ref[2 * order, :, span] = re
+            h_ref[2 * order + 1, :, span] = im
+    row = row_of(24)
+    which = jnp.where(row >= ORDER, row - ORDER, row)
+    scale = jnp.zeros((24, 1), F32)
     for k_ in range(ORDER):
-        scale = (-1.0) ** (k_ + 1) / math.factorial(k_)
-        a_re.append(jnp.broadcast_to(source(k_) * scale, (LEAVES, 512)))
-        a_im.append(jnp.broadcast_to(source(ORDER + k_) * scale, (LEAVES, 512)))
-    p_re, p_im = power_list(wx, wy, ORDER)
+        scale = jnp.where(which == k_, (-1.0) ** (k_ + 1) / math.factorial(k_), scale)
+    a_ref[:, 0:128] = (m_ref[...] + r1_ref[48:72, 0:128]) * scale
+    a_ref[:, 128:256] = r2_ref[48:72, 0:128] * (valid * scale)
+    a_ref[:, 256:384] = (f_ref[...] + got_ref[...]) * scale
+    wx = own_rows(part_ref, 0)
+    wy = own_rows(part_ref, 1)
+    ox, oy = leaf_offsets()
     x = wx + ox
     y = wy + oy
     rows = lambda at: acc_ref[:, at, :] + acc_ref[:, at + 1, :] + acc_ref[:, at + 2, :]
     total = rows(0)
     sum_re = x * total - rows(3)
     sum_im = rows(6) - y * total
+    locals_ = [[None] * ORDER, [None] * ORDER]
+    half = ORDER // 2
+    for first in (0, half):
+        sums_re = [0.0] * half
+        sums_im = [0.0] * half
+        for group in range(3):
+            span = slice(128 * group, 128 * group + 128)
+            part_re = [None] * half
+            part_im = [None] * half
+            for k_ in range(ORDER):
+                a_re = a_ref[k_ : k_ + 1, span]
+                a_im = a_ref[ORDER + k_ : ORDER + k_ + 1, span]
+                for m in range(half):
+                    at = first + m + k_
+                    h_re = h_ref[2 * at, :, span]
+                    h_im = h_ref[2 * at + 1, :, span]
+                    term_re = h_re * a_re - h_im * a_im
+                    term_im = h_re * a_im + h_im * a_re
+                    part_re[m] = term_re if k_ == 0 else part_re[m] + term_re
+                    part_im[m] = term_im if k_ == 0 else part_im[m] + term_im
+            for m in range(half):
+                sums_re[m] = sums_re[m] + part_re[m]
+                sums_im[m] = sums_im[m] + part_im[m]
+        for m in range(half):
+            factor = 1.0 / math.factorial(first + m)
+            locals_[0][first + m] = jnp.sum(sums_re[m], 1, keepdims=True) * factor
+            locals_[1][first + m] = jnp.sum(sums_im[m], 1, keepdims=True) * factor
+    p_re = jnp.ones_like(wx)
+    p_im = jnp.zeros_like(wx)
     for m in range(ORDER):
-        part_re = jnp.zeros((LEAVES, 512), F32)
-        part_im = jnp.zeros((LEAVES, 512), F32)
-        for k_ in range(ORDER):
-            part_re = part_re + (h_re[m + k_] * a_re[k_] - h_im[m + k_] * a_im[k_])
-            part_im = part_im + (h_re[m + k_] * a_im[k_] + h_im[m + k_] * a_re[k_])
-        scale = 1.0 / math.factorial(m)
-        l_re = jnp.sum(part_re, 1, keepdims=True) * scale
-        l_im = jnp.sum(part_im, 1, keepdims=True) * scale
-        sum_re = sum_re + (l_re * p_re[m] - l_im * p_im[m])
-        sum_im = sum_im + (l_re * p_im[m] + l_im * p_re[m])
+        if m:
+            p_re, p_im = p_re * wx - p_im * wy, p_re * wy + p_im * wx
+        sum_re = sum_re + (locals_[0][m] * p_re - locals_[1][m] * p_im)
+        sum_im = sum_im + (locals_[0][m] * p_im + locals_[1][m] * p_re)
     sum_re = sum_re * (1.0 / TWO_PI)
     sum_im = sum_im * (1.0 / TWO_PI)
     for i in range(SIDE):
@@ -423,107 +455,100 @@
 PAIR = 400_000_000
 
 
-def run_direct(name, info, table, mask, feats, acc, bodies, unroll, shift):
+def run_direct(name, table, mask, feats, acc, bodies, unroll, by_side=0):
     zero = acc is None
-    ins = [info.at[5].set(shift) if shift is not None else info, table, mask, *feats]
+    ins = [jnp.asarray(table.reshape(-1)), mask, *feats]
     if not zero:
         ins.append(acc)
     return call(
-        functools.partial(direct, bodies, unroll, zero),
+        functools.partial(direct, bodies, unroll, zero, by_side),
         name,
-        [S, S, S, V, V, V] + ([] if zero else [V]),
+        [S, S, V, V, V] + ([] if zero else [V]),
         shaped(LEAVES, 16, SIZE),
         [],
         PAIR * bodies * unroll,
-        {} if zero else {6: 0},
+        {} if zero else {5: 0},
     )(*ins)
 
 
 def body(particles, near_mask):
-    slab = lax.axis_index(SLAB)
-    leaf = lax.axis_index("leaf")
-    has_far = jnp.logical_and(leaf > 0, leaf < 3).astype(jnp.int32)
-    zero = jnp.zeros_like(slab)
-    info = jnp.stack([slab, leaf, slab % 2, leaf % 2, has_far, zero, zero, zero]).astype(jnp.int32)
-    mask_rows = near_mask.reshape(16, LEAVES).astype(F32)
-    mask = jnp.concatenate([mask_rows.reshape(-1), jnp.ones((LEAVES,), F32)])
-    mask_turned = mask_rows.T
-
+    mask = near_mask.transpose(1, 2, 0)
     t0, s0, w0, m0, f0, send_a, send_b = call(
         prepare_own,
         "prepare_own",
-        [S, V],
+        [V],
         [shaped(LEAVES, FEATURES, SIZE, dtype=BF16), *features_out(LEAVES), shaped(24, 128), shaped(24, 128)]
         + [shaped(SLAB_ROWS, SIZE)] * 2,
         stages(True),
         SMALL,
-    )(info, particles)
+    )(particles)
     recv_a = swap(send_a, "core")
     recv_b = swap(send_b, "slab")
-    own = jnp.asarray(pair_table("own").reshape(-1))
+    own = pair_table("own")
     feats = (t0, s0, w0)
-    acc = run_direct("direct_own_0", info, own, mask, feats, None, 3, 28, None)
+    acc = run_direct("direct_own_0", own, mask, feats, None, 2, 49)
     s1, w1, m1, f1, send_near, send_far = call(
         prepare_slab,
         "prepare_slab",
-        [S, V, V, V, V, V, A],
+        [V, V, V, V, V, A],
         [*features_out(LEAVES), shaped(24, 128), shaped(24, 128), shaped(LEAF_ROWS, SIZE), shaped(72, SIZE)],
         stages(False),
         SMALL,
-    )(info, particles, recv_a, recv_b, m0, f0, acc)
+    )(particles, recv_a, recv_b, m0, f0, acc)
     send_near, acc = lax.optimization_barrier((send_near, acc))
     recv_near = swap(send_near, "leaf_near")
-    own_1 = jnp.asarray(pair_table("own")[84:140].reshape(-1))
-    own_2 = jnp.asarray(pair_table("own")[140:].reshape(-1))
-    acc = run_direct("direct_own_1", info, own_1, mask, feats, acc, 2, 28, None)
+    acc = run_direct("direct_own_1", own[98:147], mask, feats, acc, 1, 49)
     s2, w2, f2, send_far = call(
         prepare_leaf_near,
         "prepare_leaf_near",
-        [S, V, V, V, A],
+        [V, V, V, A],
         [*features_out(LEAVES), shaped(24, 128), shaped(LEAF_ROWS, SIZE)],
         stages(False),
         SMALL,
-    )(info, recv_near, f1, send_far, acc)
+    )(recv_near, f1, send_far, acc)
     send_far, acc = lax.optimization_barrier((send_far, acc))
     recv_far = swap(send_far, "leaf_far")
-    acc = run_direct("direct_own_2", info, own_2, mask, feats, acc, 2, 28, None)
+    acc = run_direct("direct_own_2", own[147:], mask, feats, acc, 1, 49)
     s3, w3, f3 = call(
         prepare_leaf_far,
         "prepare_leaf_far",
-        [S, V, V, A],
+        [V, V, A],
         [*features_out(LEAVES), shaped(24, 128)],
         stages(False),
         SMALL,
-    )(info, recv_far, f2, acc)
+    )(recv_far, f2, acc)
     f3, acc = lax.optimization_barrier((f3, acc))
     got = swap(f3, "z_near")
-    slab_pairs = jnp.asarray(pair_table("slab").reshape(-1))
-    acc = run_direct("direct_slab", info, slab_pairs, mask, (t0, s1, w1), acc, 3, 28, None)
+    acc = run_direct("direct_slab", pair_table("slab"), mask, (t0, s1, w1), acc, 2, 42)
     got, acc = lax.optimization_barrier((got, acc))
     f4 = f3 + got
     f4, acc = lax.optimization_barrier((f4, acc))
     got = swap(f4, "z_far")
-    right = pair_table("leaf", True).reshape(-1)
-    left = pair_table("leaf", False).reshape(-1)
-    parity = leaf % 2
-    near_pairs = jnp.asarray(np.concatenate([right, left]))
-    far_pairs = jnp.asarray(np.concatenate([left, right]))
-    acc = run_direct("direct_leaf_near", info, near_pairs, mask, (t0, s2, w2), acc, 2, 30, parity * 180)
+    right = pair_table("leaf", True)
+    left = pair_table("leaf", False)
+    near_pairs = np.concatenate([right, left])
+    far_pairs = np.concatenate([left, right])
+    acc = run_direct("direct_leaf_near", near_pairs, mask, (t0, s2, w2), acc, 1, 60, 180)
     got, acc = lax.optimization_barrier((got, acc))
     f5 = f4 + got
     f5, acc = lax.optimization_barrier((f5, acc))
     got = swap(f5, "x_near")
-    acc = run_direct("direct_leaf_far_0", info, far_pairs, mask, (t0, s3, w3), acc, 1, 30, parity * 180)
+    acc = run_direct("direct_leaf_far_0", far_pairs, mask, (t0, s3, w3), acc, 1, 30, 180)
     got, acc = lax.optimization_barrier((got, acc))
     f6 = f5 + got
     f6, acc = lax.optimization_barrier((f6, acc))
     got = swap(f6, "x_far")
-    acc = run_direct("direct_leaf_far_1", info, far_pairs, mask, (t0, s3, w3), acc, 1, 30, parity * 180 + 90)
+    far_late = np.concatenate([far_pairs[30:], far_pairs[:30]])
+    acc = run_direct("direct_leaf_far_1", far_late, mask, (t0, s3, w3), acc, 1, 30, 180)
     got, acc = lax.optimization_barrier((got, acc))
-    f7 = f6 + got
     return call(
-        finish, "finish", [S] + [V] * 7, shaped(2, SIDE, SIDE, SIZE), [], SMALL
-    )(info, particles, mask_turned, acc, m1, recv_near, recv_far, f7)
+        finish,
+        "finish",
+        [V] * 8,
+        shaped(2, SIDE, SIDE, SIZE),
+        [pltpu.VMEM((4 * ORDER - 2, LEAVES, WIDE), F32), pltpu.VMEM((24, WIDE), F32)],
+        SMALL,
+    )(particles, mask, acc, m1, recv_near, recv_far, f6, got)
 
 
 def solution(mesh):

time: 79.9 us -> 57.4 us (0.72)
  Pallas kernels: 59.3 us -> 39.5 us
  local copies, waits for them, and re-layouts: 4.34 us -> 1.52 us
    pallas_call x12, Pallas kernels: 59.3 us -> 39.5 us  [the longest x7 34.8 us: run_direct(): call(functools.partial(direct, bodies, unroll, zero, by_side), name, [S,...]
    unnamed x22 -> x20, local copies, waits for them, and re-layouts: 2.9 us -> 1.52 us
  transfers between devices with their start and end apart: 8 -> 8, of which waited for: 0 -> 0; matrix products, arithmetic and copies ran while one was open for 1% -> 0% of each run, Pallas kernels for 58% -> 62%
where the time goes in v2:
time: 57.4 us; the launch traced here: 56.3 us
  Pallas kernels  39.5 us (69%)
  starting transfers between devices  15 us (26%)
  local copies, waits for them, and re-layouts  1.52 us (3%)
    pallas_call x7, Pallas kernels, run_direct(): call(functools.partial(direct, bodies, unroll, zero, by_side), name, [S,...  34.8 us
    ppermute x8, starting transfers between devices, swap(): return lax.ppermute(value, ALL, SWAPS[name])  15 us
    pallas_call x1, Pallas kernels, body(): call(finish, 'finish', [V] * 8, shaped(2, SIDE, SIDE, SIZE), [pltpu.VMEM(...  1.79 us
    unnamed x20, local copies, waits for them, and re-layouts  1.52 us
  transfers between devices with their start and end apart: 8, of which 0 were waited for; matrix products, arithmetic and copies ran while one was open for 0% of the time, Pallas kernels for 62%

profile of v2, /device:TPU:0, one launch (start us, length us, event | category | flops | bytes accessed | tf_op | source)
XLA Modules:
  0.0 56.3 jit_solution(1726736533327512696)
XLA Ops:
  0.0 0.8 %copy-done = f32[3,4,4,256]{3,2,1,0:T(4,128)S(1)} copy-done((f32[3,4,4,256]{3,2,1,0:T(4,128)S(1)}, f32[3,4,4,256]{3,2,1,0:T(4,128)}, u32[]{:S(2)}) %copy-start) | copy-done | bytes 49176
  0.8 0.9 %prepare_own.1 = (bf16[16,32,256]{2,1,0:T(8,128)(2,1)S(1)}, bf16[16,256,32]{2,1,0:T(8,128)(2,1)S(1)}, bf16[16,16,256]{2,1,0:T(8,128)(2,1)S(1)}, f32[24,128]{1,0:...) custom-call(f32[3,4,4,256]{3,2,1,0:T(4,128)S(1)} %copy-done), custom_call_target="tpu_custom_call" | custom-call | flops 4000000 | bytes 1048576 | tf_op jit(solution)/shard_map/prepare_own/pallas_call | solution.py:476
  1.7 0.1 collective-permute-start
  1.8 0.7 %collective-permute-start.1 = (f32[72,256]{1,0:T(8,128)S(1)}, f32[72,256]{1,0:T(8,128)S(1)}, u32[]{:S(2)}, u32[]{:S(2)}) collective-permute-start(f32[72,256]{1,0:T(8,128)S(1)} %get-tuple-element.46), channel_id=1, source_target_pairs={{4,8},{5,9},{6,10},{7,11},{8,4},{9,5},{10,6},{11,7},{12,16},{13,17... | collective-permute-start | bytes 221192 | tf_op jit(solution)/shard_map/ppermute | solution.py:71
  2.5 8.0 %direct_own_0.1.after_ref.refs_0_ = f32[16,16,256]{2,1,0:T(8,128)S(1)} custom-call(s32[588]{0:T(1024)S(1)} %copy-done.3, s32[4,4,16]{2,1,0:T(4,128)S(1)} %bitcast.1, bf16[16,32,256]{2,1,0:T(8,128)(2,1)S(1)} %get-tuple-element.49.t_ref, bf16[16,256,32]{2,1,0:T(8,128)(2,1)S(1)} %get-tuple-element.50.s_ref, bf16[16,16,256]{2,1,0:T(8,128)(2,1)S(1)} %get-tuple-element.51.w_ref), custom_call_target="tpu_custom_call" | custom-call | flops 39199997952 | bytes 1048576 | tf_op jit(solution)/shard_map/direct_own_0/pallas_call | solution.py:463
  10.5 0.0 collective-permute-done.1.rb_ref
  10.5 0.8 %prepare_slab.1 = (bf16[16,256,32]{2,1,0:T(8,128)(2,1)S(1)}, bf16[16,16,256]{2,1,0:T(8,128)(2,1)S(1)}, f32[24,128]{1,0:T(8,128)S(1)}, f32[24,128]{1,0:T(8,128)S(...) custom-call(f32[3,4,4,256]{3,2,1,0:T(4,128)S(1)} %copy-done.1, f32[72,256]{1,0:T(8,128)S(1)} %collective-permute-done.ra_ref, ...), custom_call_target="tpu_custom_call" | custom-call | flops 4000000 | bytes 1048576 | tf_op jit(solution)/shard_map/prepare_slab/pallas_call | solution.py:490
  11.3 1.8 %collective-permute-start.2 = (f32[96,256]{1,0:T(8,128)S(1)}, f32[96,256]{1,0:T(8,128)S(1)}, u32[]{:S(2)}, u32[]{:S(2)}) collective-permute-start(f32[96,256]{1,0:T(8,128)S(1)} %get-tuple-element.53), channel_id=1, source_target_pairs={{0,1},{1,0},{2,3},{3,2},{4,5},{5,4},{6,7},{7,6},{8,9},{9,8},{10,11... | collective-permute-start | bytes 294920 | tf_op jit(solution)/shard_map/ppermute | solution.py:71
  13.1 4.3 %direct_own_1.1.after_ref.refs_0_ = f32[16,16,256]{2,1,0:T(8,128)S(1)} custom-call(s32[147]{0:T(256)S(1)} %copy-done.9, s32[4,4,16]{2,1,0:T(4,128)S(1)} %bitcast.2, bf16[16,32,256]{2,1,0:T(8,128)(2,1)S(1)} %get-tuple-element.49.t_ref, bf16[16,256,32]{2,1,0:T(8,128)(2,1)S(1)} %get-tuple-element.50.s_ref, ...), custom_call_target="tpu_custom_call", output_to_operand_aliasing={{}: (5, {})} | custom-call | flops 19599998976 | bytes 1048576 | tf_op jit(solution)/shard_map/direct_own_1/pallas_call | solution.py:463
  17.4 0.6 %prepare_leaf_near.1 = (bf16[16,256,32]{2,1,0:T(8,128)(2,1)S(1)}, bf16[16,16,256]{2,1,0:T(8,128)(2,1)S(1)}, f32[24,128]{1,0:T(8,128)S(1)}, f32[96,256]{1,0:T(8,128)S(1)}) custom-call(f32[96,256]{1,0:T(8,128)S(1)} %collective-permute-done.2.r_ref.r1_ref, f32[24,128]{1,0:T(8,128)S(1)} %get-tuple-element.54.f_ref, f32[72,256]{1,0:T(8,128)S(1)} %get-tuple-element.55.send_ref, ...), custom_call_target="tpu_custom_call" | custom-call | flops 4000000 | bytes 1048576 | tf_op jit(solution)/shard_map/prepare_leaf_near/pallas_call | solution.py:501
  18.0 2.4 %collective-permute-start.3 = (f32[96,256]{1,0:T(8,128)S(1)}, f32[96,256]{1,0:T(8,128)S(1)}, u32[]{:S(2)}, u32[]{:S(2)}) collective-permute-start(f32[96,256]{1,0:T(8,128)S(1)} %get-tuple-element.58), channel_id=1, source_target_pairs={{0,3},{1,2},{2,1},{3,0},{4,7},{5,6},{6,5},{7,4},{8,11},{9,10},{10,... | collective-permute-start | bytes 294920 | tf_op jit(solution)/shard_map/ppermute | solution.py:71
  20.5 4.3 %direct_own_2.1.after_ref.refs_0_ = f32[16,16,256]{2,1,0:T(8,128)S(1)} custom-call(s32[147]{0:T(256)S(1)} %copy-done.8, s32[4,4,16]{2,1,0:T(4,128)S(1)} %bitcast.3, bf16[16,32,256]{2,1,0:T(8,128)(2,1)S(1)} %get-tuple-element.49.t_ref, bf16[16,256,32]{2,1,0:T(8,128)(2,1)S(1)} %get-tuple-element.50.s_ref, ...), custom_call_target="tpu_custom_call", output_to_operand_aliasing={{}: (5, {})} | custom-call | flops 19599998976 | bytes 1048576 | tf_op jit(solution)/shard_map/direct_own_2/pallas_call | solution.py:463
  24.8 0.6 %prepare_leaf_far.1 = (bf16[16,256,32]{2,1,0:T(8,128)(2,1)S(1)}, bf16[16,16,256]{2,1,0:T(8,128)(2,1)S(1)}, f32[24,128]{1,0:T(8,128)S(1)}) custom-call(f32[96,256]{1,0:T(8,128)S(1)} %collective-permute-done.3.r_ref.r2_ref, f32[24,128]{1,0:T(8,128)S(1)} %get-tuple-element.59.f_ref, f32[16,16,256]{2,1,0:T(8,128)S(1)} %direct_own_2.1.after_ref.refs_0_), custom_call_target="tpu_custom_call" | custom-call | flops 4000000 | bytes 1048576 | tf_op jit(solution)/shard_map/prepare_leaf_far/pallas_call | solution.py:512
  25.4 3.4 %collective-permute-start.4 = (f32[24,128]{1,0:T(8,128)S(1)}, f32[24,128]{1,0:T(8,128)S(1)}, u32[]{:S(2)}, u32[]{:S(2)}) collective-permute-start(f32[24,128]{1,0:T(8,128)S(1)} %get-tuple-element.62), channel_id=1, source_target_pairs={{0,8},{1,9},{2,10},{3,11},{4,12},{5,13},{6,14},{7,15},{8,0},{9,1},... | collective-permute-start | bytes 36872 | tf_op jit(solution)/shard_map/ppermute | solution.py:71
  28.9 0.7 %copy-done.7 = s32[252]{0:T(256)S(1)} copy-done((s32[252]{0:T(256)S(1)}, s32[252]{0:T(256)}, u32[]{:S(2)}) %copy-start.7) | copy-done | bytes 1032
  29.5 7.0 %direct_slab.1.refs_0_ = f32[16,16,256]{2,1,0:T(8,128)S(1)} custom-call(s32[252]{0:T(256)S(1)} %copy-done.7, s32[4,4,16]{2,1,0:T(4,128)S(1)} %bitcast.4, bf16[16,32,256]{2,1,0:T(8,128)(2,1)S(1)} %get-tuple-element.49.t_ref, bf16[16,256,32]{2,1,0:T(8,128)(2,1)S(1)} %get-tuple-element.63.s_ref, ...), custom_call_target="tpu_custom_call", output_to_operand_aliasing={{}: (5, {})} | custom-call | flops 33600000000 | bytes 1048576 | tf_op jit(solution)/shard_map/direct_slab/pallas_call | solution.py:463
  36.6 2.9 %collective-permute-start.5 = (f32[24,128]{1,0:T(8,128)S(1)}, f32[24,128]{1,0:T(8,128)S(1)}, u32[]{:S(2)}, u32[]{:S(2)}) collective-permute-start(f32[24,128]{1,0:T(8,128)S(1)} %add.9), channel_id=1, source_target_pairs={{0,24},{1,25},{2,26},{3,27},{4,28},{5,29},{6,30},{7,31},{8,16},{9,... | collective-permute-start | bytes 36872 | tf_op jit(solution)/shard_map/ppermute | solution.py:71
  39.5 5.1 %direct_leaf_near.1.refs_0_ = f32[16,16,256]{2,1,0:T(8,128)S(1)} custom-call(s32[360]{0:T(512)S(1)} %copy-done.6, s32[4,4,16]{2,1,0:T(4,128)S(1)} %bitcast.5, bf16[16,32,256]{2,1,0:T(8,128)(2,1)S(1)} %get-tuple-element.49.t_ref, bf16[16,256,32]{2,1,0:T(8,128)(2,1)S(1)} %get-tuple-element.69.s_ref, ...), custom_call_target="tpu_custom_call", output_to_operand_aliasing={{}: (5, {})} | custom-call | flops 24000000000 | bytes 1048576 | tf_op jit(solution)/shard_map/direct_leaf_near/pallas_call | solution.py:463
  44.6 1.6 %collective-permute-start.6 = (f32[24,128]{1,0:T(8,128)S(1)}, f32[24,128]{1,0:T(8,128)S(1)}, u32[]{:S(2)}, u32[]{:S(2)}) collective-permute-start(f32[24,128]{1,0:T(8,128)S(1)} %add.10), channel_id=1, source_target_pairs={{0,32},{1,33},{2,34},{3,35},{4,36},{5,37},{6,38},{7,39},{8,40},{9,... | collective-permute-start | bytes 36872 | tf_op jit(solution)/shard_map/ppermute | solution.py:71
  46.2 3.1 %direct_leaf_far_0.1.refs_0_ = f32[16,16,256]{2,1,0:T(8,128)S(1)} custom-call(s32[360]{0:T(512)S(1)} %copy-done.5, s32[4,4,16]{2,1,0:T(4,128)S(1)} %bitcast.6, bf16[16,32,256]{2,1,0:T(8,128)(2,1)S(1)} %get-tuple-element.49.t_ref, bf16[16,256,32]{2,1,0:T(8,128)(2,1)S(1)} %get-tuple-element.75.s_ref, ...), custom_call_target="tpu_custom_call", output_to_operand_aliasing={{}: (5, {})} | custom-call | flops 12000000000 | bytes 1048576 | tf_op jit(solution)/shard_map/direct_leaf_far_0/pallas_call | solution.py:463
  49.2 0.0 collective-permute-done.6
  49.3 2.2 %collective-permute-start.7 = (f32[24,128]{1,0:T(8,128)S(1)}, f32[24,128]{1,0:T(8,128)S(1)}, u32[]{:S(2)}, u32[]{:S(2)}) collective-permute-start(f32[24,128]{1,0:T(8,128)S(1)} %add.11.f_ref), channel_id=1, source_target_pairs={{0,96},{1,97},{2,98},{3,99},{4,100},{5,101},{6,102},{7,103},{8,104... | collective-permute-start | bytes 36872 | tf_op jit(solution)/shard_map/ppermute | solution.py:71
  51.4 3.1 %direct_leaf_far_1.1.acc_ref = f32[16,16,256]{2,1,0:T(8,128)S(1)} custom-call(s32[360]{0:T(512)S(1)} %copy-done.4, s32[4,4,16]{2,1,0:T(4,128)S(1)} %bitcast.7, bf16[16,32,256]{2,1,0:T(8,128)(2,1)S(1)} %get-tuple-element.49.t_ref, bf16[16,256,32]{2,1,0:T(8,128)(2,1)S(1)} %get-tuple-element.75.s_ref, ...), custom_call_target="tpu_custom_call", output_to_operand_aliasing={{}: (5, {})} | custom-call | flops 12000000000 | bytes 1048576 | tf_op jit(solution)/shard_map/direct_leaf_far_1/pallas_call | solution.py:463
  54.5 1.8 %finish.1 = f32[2,4,4,256]{3,2,1,0:T(4,128)} custom-call(f32[3,4,4,256]{3,2,1,0:T(4,128)S(1)} %copy-done.1, s32[4,4,16]{2,1,0:T(4,128)S(1)} %bitcast.8, f32[16,16,256]{2,1,0:T(8,128)S(1)} %direct_leaf_far_1.1.acc_ref, f32[24,128]{1,0:T(8,128)S(1)} %get-tuple-element.83.m_ref, f32[96,256]{1,0:T(8,128)S(1)} %collective-permute-done.2.r_ref.r1_ref, ...), custom_call_target="tpu_custom_call" | custom-call | flops 4000000 | bytes 1048576 | tf_op jit(solution)/shard_map/finish/pallas_call | solution.py:544
  (27 shorter events, 0.1 us)
Async XLA Ops:
  0.0 0.8 %copy-start = (f32[3,4,4,256]{3,2,1,0:T(4,128)S(1)}, f32[3,4,4,256]{3,2,1,0:T(4,128)}, u32[]{:S(2)}) copy-start(f32[3,4,4,256]{3,2,1,0:T(4,128)} %part_ref.5) | copy-start | bytes 147460
  0.8 1.7 %copy-start.3 = (s32[588]{0:T(1024)S(1)}, s32[588]{0:T(1024)}, u32[]{:S(2)}) copy-start(s32[588]{0:T(1024)} %constant.14.clone.table) | copy-start | bytes 7060
  1.7 0.8 %copy-start.2 = (s32[16,4,4]{0,2,1:T(4,128)S(1)}, s32[16,4,4]{0,2,1:T(4,128)}, u32[]{:S(2)}) copy-start(s32[16,4,4]{0,2,1:T(4,128)} %param.10) | copy-start | bytes 3076
  1.7 8.8 %collective-permute-start = (f32[72,256]{1,0:T(8,128)S(1)}, f32[72,256]{1,0:T(8,128)S(1)}, u32[]{:S(2)}, u32[]{:S(2)}) collective-permute-start(f32[72,256]{1,0:T(8,128)S(1)} %get-tuple-element.45), channel_id=1, source_target_pairs={{0,4},{1,5},{2,6},{3,7},{4,0},{5,1},{6,2},{7,3},{8,12},{9,13},{10,... | collective-permute-start | bytes 221192 | tf_op jit(solution)/shard_map/ppermute | solution.py:71
  1.8 8.7 %collective-permute-start.1 = (f32[72,256]{1,0:T(8,128)S(1)}, f32[72,256]{1,0:T(8,128)S(1)}, u32[]{:S(2)}, u32[]{:S(2)}) collective-permute-start(f32[72,256]{1,0:T(8,128)S(1)} %get-tuple-element.46), channel_id=1, source_target_pairs={{4,8},{5,9},{6,10},{7,11},{8,4},{9,5},{10,6},{11,7},{12,16},{13,17... | collective-permute-start | bytes 221192 | tf_op jit(solution)/shard_map/ppermute | solution.py:71
  2.5 8.0 %copy-start.1 = (f32[3,4,4,256]{3,2,1,0:T(4,128)S(1)}, f32[3,4,4,256]{3,2,1,0:T(4,128)}, u32[]{:S(2)}) copy-start(f32[3,4,4,256]{3,2,1,0:T(4,128)} %part_ref.5) | copy-start | bytes 147460
  11.3 1.8 %copy-start.9 = (s32[147]{0:T(256)S(1)}, s32[147]{0:T(256)}, u32[]{:S(2)}) copy-start(s32[147]{0:T(256)} %constant.15.clone.table) | copy-start | bytes 1768
  11.3 6.1 %collective-permute-start.2 = (f32[96,256]{1,0:T(8,128)S(1)}, f32[96,256]{1,0:T(8,128)S(1)}, u32[]{:S(2)}, u32[]{:S(2)}) collective-permute-start(f32[96,256]{1,0:T(8,128)S(1)} %get-tuple-element.53), channel_id=1, source_target_pairs={{0,1},{1,0},{2,3},{3,2},{4,5},{5,4},{6,7},{7,6},{8,9},{9,8},{10,11... | collective-permute-start | bytes 294920 | tf_op jit(solution)/shard_map/ppermute | solution.py:71
  18.0 2.5 %copy-start.8 = (s32[147]{0:T(256)S(1)}, s32[147]{0:T(256)}, u32[]{:S(2)}) copy-start(s32[147]{0:T(256)} %constant.16.clone.table) | copy-start | bytes 1768
  18.0 6.8 %collective-permute-start.3 = (f32[96,256]{1,0:T(8,128)S(1)}, f32[96,256]{1,0:T(8,128)S(1)}, u32[]{:S(2)}, u32[]{:S(2)}) collective-permute-start(f32[96,256]{1,0:T(8,128)S(1)} %get-tuple-element.58), channel_id=1, source_target_pairs={{0,3},{1,2},{2,1},{3,0},{4,7},{5,6},{6,5},{7,4},{8,11},{9,10},{10,... | collective-permute-start | bytes 294920 | tf_op jit(solution)/shard_map/ppermute | solution.py:71
  25.4 11.1 %collective-permute-start.4 = (f32[24,128]{1,0:T(8,128)S(1)}, f32[24,128]{1,0:T(8,128)S(1)}, u32[]{:S(2)}, u32[]{:S(2)}) collective-permute-start(f32[24,128]{1,0:T(8,128)S(1)} %get-tuple-element.62), channel_id=1, source_target_pairs={{0,8},{1,9},{2,10},{3,11},{4,12},{5,13},{6,14},{7,15},{8,0},{9,1},... | collective-permute-start | bytes 36872 | tf_op jit(solution)/shard_map/ppermute | solution.py:71
  28.9 0.7 %copy-start.7 = (s32[252]{0:T(256)S(1)}, s32[252]{0:T(256)}, u32[]{:S(2)}) copy-start(s32[252]{0:T(256)} %constant.17.clone.table) | copy-start | bytes 3028
  36.6 2.9 %copy-start.6 = (s32[360]{0:T(512)S(1)}, s32[360]{0:T(512)}, u32[]{:S(2)}) copy-start(s32[360]{0:T(512)} %constant.18.clone.table) | copy-start | bytes 4324
  36.6 8.0 %collective-permute-start.5 = (f32[24,128]{1,0:T(8,128)S(1)}, f32[24,128]{1,0:T(8,128)S(1)}, u32[]{:S(2)}, u32[]{:S(2)}) collective-permute-start(f32[24,128]{1,0:T(8,128)S(1)} %add.9), channel_id=1, source_target_pairs={{0,24},{1,25},{2,26},{3,27},{4,28},{5,29},{6,30},{7,31},{8,16},{9,... | collective-permute-start | bytes 36872 | tf_op jit(solution)/shard_map/ppermute | solution.py:71
  44.6 1.6 %copy-start.5 = (s32[360]{0:T(512)S(1)}, s32[360]{0:T(512)}, u32[]{:S(2)}) copy-start(s32[360]{0:T(512)} %constant.19.clone.table) | copy-start | bytes 4324
  44.6 4.6 %collective-permute-start.6 = (f32[24,128]{1,0:T(8,128)S(1)}, f32[24,128]{1,0:T(8,128)S(1)}, u32[]{:S(2)}, u32[]{:S(2)}) collective-permute-start(f32[24,128]{1,0:T(8,128)S(1)} %add.10), channel_id=1, source_target_pairs={{0,32},{1,33},{2,34},{3,35},{4,36},{5,37},{6,38},{7,39},{8,40},{9,... | collective-permute-start | bytes 36872 | tf_op jit(solution)/shard_map/ppermute | solution.py:71
  49.2 2.2 %copy-start.4 = (s32[360]{0:T(512)S(1)}, s32[360]{0:T(512)}, u32[]{:S(2)}) copy-start(s32[360]{0:T(512)} %constant.20.clone.table) | copy-start | bytes 4324
  49.3 5.2 %collective-permute-start.7 = (f32[24,128]{1,0:T(8,128)S(1)}, f32[24,128]{1,0:T(8,128)S(1)}, u32[]{:S(2)}, u32[]{:S(2)}) collective-permute-start(f32[24,128]{1,0:T(8,128)S(1)} %add.11.f_ref), channel_id=1, source_target_pairs={{0,96},{1,97},{2,98},{3,99},{4,100},{5,101},{6,102},{7,103},{8,104... | collective-permute-start | bytes 36872 | tf_op jit(solution)/shard_map/ppermute | solution.py:71

commit v3 on v2

--- a/solution.py
+++ b/solution.py
@@ -195,19 +195,15 @@
     build_features(wx, wy, g, ox, oy, stage_t, stage_s, stage_w, t_ref, s_ref, w_ref, 0, True)
 
 
-def prepare_slab(
-    part_ref, ra_ref, rb_ref, m_ref, f_ref, after_ref, s_ref, w_ref, m_out, f_out, near_ref, far_ref, stage_s, stage_w
-):
+def pack_slab(part_ref, ra_ref, rb_ref, m_ref, f_ref, after_ref, m_out, f_out, near_ref, far_ref):
     info = position()
     even = info[2] == 0
     leaf_even = info[3] == 0
-    halo = []
     for c in range(3):
         ra = ra_ref[8 * c : 8 * c + 8]
         rb = rb_ref[8 * c : 8 * c + 8]
         before = jnp.where(even, rb, ra)
         after = jnp.where(even, ra, rb)
-        halo.append(jnp.concatenate([before, after], axis=0))
         rows = [before[0:4], before[4:8]] + [part_ref[c, i] for i in range(SIDE)] + [after[0:4], after[4:8]]
         left = jnp.concatenate([r[0:2] for r in rows], axis=0)
         right = jnp.concatenate([r[2:4] for r in rows], axis=0)
@@ -228,6 +224,15 @@
     far_ref[48:72, 128:256] = none
     near_ref[72:96, 0:128] = blocks
     near_ref[72:96, 128:256] = none
+
+
+def slab_halo(ra_ref, rb_ref, s_ref, w_ref, stage_s, stage_w):
+    even = position()[2] == 0
+    halo = []
+    for c in range(3):
+        ra = ra_ref[8 * c : 8 * c + 8]
+        rb = rb_ref[8 * c : 8 * c + 8]
+        halo.append(jnp.concatenate([jnp.where(even, rb, ra), jnp.where(even, ra, rb)], axis=0))
     n = row_of(LEAVES)
     i = (n >> 2) - 2
     ox = jnp.where(i >= 0, i + 4, i).astype(F32) - 1.5
@@ -249,45 +254,69 @@
     )
 
 
-def prepare_leaf_near(r_ref, f_ref, send_ref, after_ref, s_ref, w_ref, f_out, send_out, stage_s, stage_w):
+def near_halo(r_ref, s_ref, w_ref, stage_s, stage_w):
+    leaf_halo(0, r_ref, s_ref, w_ref, stage_s, stage_w)
+
+
+def far_halo(r_ref, s_ref, w_ref, stage_s, stage_w):
+    leaf_halo(1, r_ref, s_ref, w_ref, stage_s, stage_w)
+
+
+def pack_near(r_ref, f_ref, send_ref, after_ref, f_out, send_out):
     blocks = f_ref[...] + r_ref[72:96, 0:128]
     f_out[...] = blocks
     send_out[0:72] = send_ref[...]
     send_out[72:96, 0:128] = blocks
     send_out[72:96, 128:256] = jnp.zeros((24, 128), F32)
-    leaf_halo(0, r_ref, s_ref, w_ref, stage_s, stage_w)
-
-
-def prepare_leaf_far(r_ref, f_ref, after_ref, s_ref, w_ref, f_out, stage_s, stage_w):
-    f_out[...] = f_ref[...] + r_ref[72:96, 0:128]
-    leaf_halo(1, r_ref, s_ref, w_ref, stage_s, stage_w)
-
-
-def direct(bodies, unroll, zero, by_side, table, mask, t_ref, s_ref, w_ref, *refs):
-    acc_ref = refs[-1]
+
+
+def chosen(index, values):
+    if all(v == values[0] for v in values):
+        return values[0]
+    out = values[-1]
+    for n in range(len(values) - 2, -1, -1):
+        out = jnp.where(index == n, values[n], out)
+    return out
+
+
+def direct(tables, by_side, zero, extra, extra_in, mask_ref, t_ref, s_ref, w_ref, *refs):
     if zero:
+        acc_ref, rows_ref = refs
         acc_ref[...] = jnp.zeros_like(acc_ref)
+        near_mask = jnp.concatenate([mask_ref[i] for i in range(SIDE)], axis=0).astype(F32)
+        for o in range(16):
+            rows_ref[o, :, 0, :] = jnp.broadcast_to(near_mask[:, o : o + 1], (LEAVES, SIZE))
+        rows_ref[16, :, 0, :] = jnp.ones((LEAVES, SIZE), F32)
+        mask_ref = rows_ref
     else:
+        acc_ref = refs[extra_in + 1]
         acc_ref[...] = refs[0][...]
-    shift = position()[3] * by_side if by_side else 0
-
-    def step(b, unused):
-        for n in range(unroll):
-            at = (b * unroll + n) * 3 + shift
-            t = table[at]
-            s = table[at + 1]
-            o = table[at + 2]
-            weight = jnp.where(o == 16, 1, mask[t >> 2, t & 3, o & 15]).astype(F32)
+        others = refs[1 : extra_in + 1] + refs[extra_in + 2 :]
+    count = tables.shape[1]
+
+    def step(index, unused):
+        for n in range(count):
+            t, s, o = (chosen(index, [int(v) for v in tables[:, n, c]]) for c in range(3))
             distance = jnp.dot(s_ref[s], t_ref[t], preferred_element_type=F32)
             kernel = 1.0 / distance
             high = kernel.astype(BF16)
             low = (kernel - high.astype(F32)).astype(BF16)
             w = w_ref[s]
             total = jnp.dot(w, high, preferred_element_type=F32) + jnp.dot(w, low, preferred_element_type=F32)
-            acc_ref[t] = acc_ref[t] + weight * total
+            if isinstance(o, int) and o == 16:
+                acc_ref[t] = acc_ref[t] + total
+            else:
+                acc_ref[t] = acc_ref[t] + mask_ref[o, t] * total
         return 0
 
-    lax.fori_loop(0, bodies, step, 0)
+    if by_side:
+        step(position()[3], 0)
+    elif tables.shape[0] == 1:
+        step(0, 0)
+    else:
+        lax.fori_loop(0, tables.shape[0], step, 0)
+    if extra is not None:
+        extra(*others)
 
 
 def pair_table(kind, to_right=False):
@@ -307,10 +336,56 @@
     return np.array(out, np.int32)
 
 
-WIDE = 3 * 128
-
-
-def finish(part_ref, nm_ref, acc_ref, m_ref, r1_ref, r2_ref, f_ref, got_ref, out_ref, h_ref, a_ref):
+def translate(groups, h_ref, a_ref, out_ref):
+    for group, (tx, ty, weight) in enumerate(groups):
+        span = slice(128 * group, 128 * group + 128)
+        square = tx * tx + ty * ty
+        inv_x = tx / square
+        inv_y = -ty / square
+        re = weight * inv_x
+        im = weight * inv_y
+        h_ref[0, :, span] = re
+        h_ref[1, :, span] = im
+        for order in range(1, 2 * ORDER - 1):
+            re, im = (re * inv_x - im * inv_y) * float(order), (re * inv_y + im * inv_x) * float(order)
+            h_ref[2 * order, :, span] = re
+            h_ref[2 * order + 1, :, span] = im
+    lane = lax.broadcasted_iota(jnp.int32, (LEAVES, 128), 1)
+    table = jnp.zeros((LEAVES, 128), F32)
+    half = ORDER // 2
+    for first in (0, half):
+        sums_re = [None] * half
+        sums_im = [None] * half
+        for group in range(len(groups)):
+            span = slice(128 * group, 128 * group + 128)
+            for k_ in range(ORDER):
+                a_re = a_ref[k_ : k_ + 1, span]
+                a_im = a_ref[ORDER + k_ : ORDER + k_ + 1, span]
+                for m in range(half):
+                    at = first + m + k_
+                    h_re = h_ref[2 * at, :, span]
+                    h_im = h_ref[2 * at + 1, :, span]
+                    term_re = h_re * a_re - h_im * a_im
+                    term_im = h_re * a_im + h_im * a_re
+                    sums_re[m] = term_re if sums_re[m] is None else sums_re[m] + term_re
+                    sums_im[m] = term_im if sums_im[m] is None else sums_im[m] + term_im
+        for m in range(half):
+            factor = 1.0 / math.factorial(first + m)
+            table = jnp.where(lane == first + m, jnp.sum(sums_re[m], 1, keepdims=True) * factor, table)
+            table = jnp.where(lane == 64 + first + m, jnp.sum(sums_im[m], 1, keepdims=True) * factor, table)
+    out_ref[...] = table
+
+
+def source_scale():
+    row = row_of(24)
+    which = jnp.where(row >= ORDER, row - ORDER, row)
+    scale = jnp.zeros((24, 1), F32)
+    for k_ in range(ORDER):
+        scale = jnp.where(which == k_, (-1.0) ** (k_ + 1) / math.factorial(k_), scale)
+    return scale
+
+
+def leaf_field(nm_ref, m_ref, r1_ref, r2_ref, out_ref, h_ref, a_ref):
     info = position()
     leaf_even = info[3] == 0
     valid = info[4].astype(F32)
@@ -325,9 +400,7 @@
     k = place >> 4
     r = place & 15
     si = jnp.where(k == 0, r >> 2, jnp.where(k == 1, (r >> 2) - 4, (r >> 2) + 4))
-    xs = []
-    ys = []
-    weights = []
+    groups = []
     for column, lanes in ((jnp.where(second, near_shift, 0), 96), (-near_shift, 48)):
         dx = si - ti
         dy = (r & 3) + column - tj
@@ -338,37 +411,34 @@
             weight = jnp.where(hit, 1.0 - near_mask[:, o : o + 1], weight)
         inside = lane < lanes
         used = jnp.logical_and(reach >= 2, inside)
-        xs.append(jnp.where(used, dx.astype(F32), 1.0))
-        ys.append(jnp.where(used, dy.astype(F32), 1.0))
-        weights.append(jnp.where(inside, weight, 0.0))
+        groups.append(
+            (
+                jnp.where(used, dx.astype(F32), 1.0),
+                jnp.where(used, dy.astype(F32), 1.0),
+                jnp.where(inside, weight, 0.0),
+            )
+        )
+    scale = source_scale()
+    a_ref[:, 0:128] = (m_ref[...] + r1_ref[48:72, 0:128]) * scale
+    a_ref[:, 128:256] = r2_ref[48:72, 0:128] * (valid * scale)
+    translate(groups, h_ref, a_ref, out_ref)
+
+
+def finish(part_ref, acc_ref, near_ref, f_ref, got_ref, out_ref, h_ref, a_ref, l_ref):
+    info = position()
+    n = row_of(LEAVES)
+    ti = n >> 2
+    tj = n & 3
+    lane = lax.broadcasted_iota(jnp.int32, (LEAVES, 128), 1)
     bx = (lane >> 2) - info[0]
     by = (lane & 3) - info[1]
     remote = jnp.maximum(jnp.abs(bx), jnp.abs(by)) >= 2
-    xs.append(jnp.where(remote, (bx * SIDE - ti).astype(F32) + 1.5, 1.0))
-    ys.append(jnp.where(remote, (by * SIDE - tj).astype(F32) + 1.5, 1.0))
-    weights.append(jnp.where(remote, 1.0, 0.0).astype(F32))
-    for group in range(3):
-        span = slice(128 * group, 128 * group + 128)
-        tx, ty, weight = xs[group], ys[group], weights[group]
-        square = tx * tx + ty * ty
-        inv_x = tx / square
-        inv_y = -ty / square
-        re = weight * inv_x
-        im = weight * inv_y
-        h_ref[0, :, span] = re
-        h_ref[1, :, span] = im
-        for order in range(1, 2 * ORDER - 1):
-            re, im = (re * inv_x - im * inv_y) * float(order), (re * inv_y + im * inv_x) * float(order)
-            h_ref[2 * order, :, span] = re
-            h_ref[2 * order + 1, :, span] = im
-    row = row_of(24)
-    which = jnp.where(row >= ORDER, row - ORDER, row)
-    scale = jnp.zeros((24, 1), F32)
-    for k_ in range(ORDER):
-        scale = jnp.where(which == k_, (-1.0) ** (k_ + 1) / math.factorial(k_), scale)
-    a_ref[:, 0:128] = (m_ref[...] + r1_ref[48:72, 0:128]) * scale
-    a_ref[:, 128:256] = r2_ref[48:72, 0:128] * (valid * scale)
-    a_ref[:, 256:384] = (f_ref[...] + got_ref[...]) * scale
+    tx = jnp.where(remote, (bx * SIDE - ti).astype(F32) + 1.5, 1.0)
+    ty = jnp.where(remote, (by * SIDE - tj).astype(F32) + 1.5, 1.0)
+    weight = jnp.where(remote, 1.0, 0.0).astype(F32)
+    a_ref[...] = (f_ref[...] + got_ref[...]) * source_scale()
+    translate([(tx, ty, weight)], h_ref, a_ref, l_ref)
+    local = l_ref[...] + near_ref[...]
     wx = own_rows(part_ref, 0)
     wy = own_rows(part_ref, 1)
     ox, oy = leaf_offsets()
@@ -378,40 +448,15 @@
     total = rows(0)
     sum_re = x * total - rows(3)
     sum_im = rows(6) - y * total
-    locals_ = [[None] * ORDER, [None] * ORDER]
-    half = ORDER // 2
-    for first in (0, half):
-        sums_re = [0.0] * half
-        sums_im = [0.0] * half
-        for group in range(3):
-            span = slice(128 * group, 128 * group + 128)
-            part_re = [None] * half
-            part_im = [None] * half
-            for k_ in range(ORDER):
-                a_re = a_ref[k_ : k_ + 1, span]
-                a_im = a_ref[ORDER + k_ : ORDER + k_ + 1, span]
-                for m in range(half):
-                    at = first + m + k_
-                    h_re = h_ref[2 * at, :, span]
-                    h_im = h_ref[2 * at + 1, :, span]
-                    term_re = h_re * a_re - h_im * a_im
-                    term_im = h_re * a_im + h_im * a_re
-                    part_re[m] = term_re if k_ == 0 else part_re[m] + term_re
-                    part_im[m] = term_im if k_ == 0 else part_im[m] + term_im
-            for m in range(half):
-                sums_re[m] = sums_re[m] + part_re[m]
-                sums_im[m] = sums_im[m] + part_im[m]
-        for m in range(half):
-            factor = 1.0 / math.factorial(first + m)
-            locals_[0][first + m] = jnp.sum(sums_re[m], 1, keepdims=True) * factor
-            locals_[1][first + m] = jnp.sum(sums_im[m], 1, keepdims=True) * factor
     p_re = jnp.ones_like(wx)
     p_im = jnp.zeros_like(wx)
     for m in range(ORDER):
         if m:
             p_re, p_im = p_re * wx - p_im * wy, p_re * wy + p_im * wx
-        sum_re = sum_re + (locals_[0][m] * p_re - locals_[1][m] * p_im)
-        sum_im = sum_im + (locals_[0][m] * p_im + locals_[1][m] * p_re)
+        l_re = local[:, m : m + 1]
+        l_im = local[:, 64 + m : 65 + m]
+        sum_re = sum_re + (l_re * p_re - l_im * p_im)
+        sum_im = sum_im + (l_re * p_im + l_im * p_re)
     sum_re = sum_re * (1.0 / TWO_PI)
     sum_im = sum_im * (1.0 / TWO_PI)
     for i in range(SIDE):
@@ -455,24 +500,27 @@
 PAIR = 400_000_000
 
 
-def run_direct(name, table, mask, feats, acc, bodies, unroll, by_side=0):
+def run_direct(name, tables, mask, feats, acc, by_side=False, extra=None, ins=(), outs=(), scratch=()):
     zero = acc is None
-    ins = [jnp.asarray(table.reshape(-1)), mask, *feats]
-    if not zero:
-        ins.append(acc)
-    return call(
-        functools.partial(direct, bodies, unroll, zero, by_side),
+    args = [mask, *feats] + ([] if zero else [acc]) + list(ins)
+    got = call(
+        functools.partial(direct, tables, by_side, zero, extra, len(ins)),
         name,
-        [S, S, V, V, V] + ([] if zero else [V]),
-        shaped(LEAVES, 16, SIZE),
-        [],
-        PAIR * bodies * unroll,
-        {} if zero else {5: 0},
-    )(*ins)
+        [V] * len(args),
+        [shaped(LEAVES, 16, SIZE), *outs],
+        list(scratch),
+        PAIR * (1 if by_side else tables.shape[0]) * tables.shape[1],
+        {} if zero else {4: 0},
+    )(*args)
+    return got if outs else got[0]
+
+
+def far_scratch(width):
+    return [pltpu.VMEM((4 * ORDER - 2, LEAVES, width), F32), pltpu.VMEM((24, width), F32)]
 
 
 def body(particles, near_mask):
-    mask = near_mask.transpose(1, 2, 0)
+    turned = near_mask.transpose(1, 2, 0)
     t0, s0, w0, m0, f0, send_a, send_b = call(
         prepare_own,
         "prepare_own",
@@ -486,69 +534,84 @@
     recv_b = swap(send_b, "slab")
     own = pair_table("own")
     feats = (t0, s0, w0)
-    acc = run_direct("direct_own_0", own, mask, feats, None, 2, 49)
-    s1, w1, m1, f1, send_near, send_far = call(
-        prepare_slab,
-        "prepare_slab",
+    acc, mask = run_direct(
+        "direct_own_0", own[:98].reshape(2, 49, 3), turned, feats, None, outs=[shaped(17, LEAVES, 1, SIZE)]
+    )
+    m1, f1, send_near, send_far = call(
+        pack_slab,
+        "pack_slab",
         [V, V, V, V, V, A],
-        [*features_out(LEAVES), shaped(24, 128), shaped(24, 128), shaped(LEAF_ROWS, SIZE), shaped(72, SIZE)],
-        stages(False),
+        [shaped(24, 128), shaped(24, 128), shaped(LEAF_ROWS, SIZE), shaped(72, SIZE)],
+        [],
         SMALL,
     )(particles, recv_a, recv_b, m0, f0, acc)
     send_near, acc = lax.optimization_barrier((send_near, acc))
     recv_near = swap(send_near, "leaf_near")
-    acc = run_direct("direct_own_1", own[98:147], mask, feats, acc, 1, 49)
-    s2, w2, f2, send_far = call(
-        prepare_leaf_near,
-        "prepare_leaf_near",
-        [V, V, V, A],
-        [*features_out(LEAVES), shaped(24, 128), shaped(LEAF_ROWS, SIZE)],
-        stages(False),
-        SMALL,
+    built = dict(outs=features_out(LEAVES), scratch=stages(False))
+    acc, s1, w1 = run_direct(
+        "direct_own_1", own[None, 98:147], mask, feats, acc, extra=slab_halo, ins=(recv_a, recv_b), **built
+    )
+    f2, send_far = call(
+        pack_near, "pack_near", [V, V, V, A], [shaped(24, 128), shaped(LEAF_ROWS, SIZE)], [], SMALL
     )(recv_near, f1, send_far, acc)
     send_far, acc = lax.optimization_barrier((send_far, acc))
     recv_far = swap(send_far, "leaf_far")
-    acc = run_direct("direct_own_2", own[147:], mask, feats, acc, 1, 49)
-    s3, w3, f3 = call(
-        prepare_leaf_far,
-        "prepare_leaf_far",
-        [V, V, A],
-        [*features_out(LEAVES), shaped(24, 128)],
-        stages(False),
-        SMALL,
-    )(recv_far, f2, acc)
+    acc, s2, w2 = run_direct(
+        "direct_own_2", own[None, 147:], mask, feats, acc, extra=near_halo, ins=(recv_near,), **built
+    )
+    recv_far, acc = lax.optimization_barrier((recv_far, acc))
+    f3 = f2 + recv_far[72:96, 0:128]
     f3, acc = lax.optimization_barrier((f3, acc))
     got = swap(f3, "z_near")
-    acc = run_direct("direct_slab", pair_table("slab"), mask, (t0, s1, w1), acc, 2, 42)
+    acc, s3, w3 = run_direct(
+        "direct_slab",
+        pair_table("slab").reshape(2, 42, 3),
+        mask,
+        (t0, s1, w1),
+        acc,
+        extra=far_halo,
+        ins=(recv_far,),
+        **built,
+    )
     got, acc = lax.optimization_barrier((got, acc))
     f4 = f3 + got
     f4, acc = lax.optimization_barrier((f4, acc))
     got = swap(f4, "z_far")
     right = pair_table("leaf", True)
     left = pair_table("leaf", False)
-    near_pairs = np.concatenate([right, left])
-    far_pairs = np.concatenate([left, right])
-    acc = run_direct("direct_leaf_near", near_pairs, mask, (t0, s2, w2), acc, 1, 60, 180)
+    near_pairs = np.stack([right, left])
+    far_pairs = np.stack([left, right])
+    acc, local = run_direct(
+        "direct_leaf_near",
+        near_pairs,
+        mask,
+        (t0, s2, w2),
+        acc,
+        True,
+        extra=leaf_field,
+        ins=(turned, m1, recv_near, recv_far),
+        outs=[shaped(LEAVES, 128)],
+        scratch=far_scratch(256),
+    )
     got, acc = lax.optimization_barrier((got, acc))
     f5 = f4 + got
     f5, acc = lax.optimization_barrier((f5, acc))
     got = swap(f5, "x_near")
-    acc = run_direct("direct_leaf_far_0", far_pairs, mask, (t0, s3, w3), acc, 1, 30, 180)
+    acc = run_direct("direct_leaf_far_0", far_pairs[:, :30], mask, (t0, s3, w3), acc, True)
     got, acc = lax.optimization_barrier((got, acc))
     f6 = f5 + got
     f6, acc = lax.optimization_barrier((f6, acc))
     got = swap(f6, "x_far")
-    far_late = np.concatenate([far_pairs[30:], far_pairs[:30]])
-    acc = run_direct("direct_leaf_far_1", far_late, mask, (t0, s3, w3), acc, 1, 30, 180)
+    acc = run_direct("direct_leaf_far_1", far_pairs[:, 30:], mask, (t0, s3, w3), acc, True)
     got, acc = lax.optimization_barrier((got, acc))
     return call(
         finish,
         "finish",
-        [V] * 8,
+        [V] * 5,
         shaped(2, SIDE, SIDE, SIZE),
-        [pltpu.VMEM((4 * ORDER - 2, LEAVES, WIDE), F32), pltpu.VMEM((24, WIDE), F32)],
+        far_scratch(128) + [pltpu.VMEM((LEAVES, 128), F32)],
         SMALL,
-    )(particles, mask, acc, m1, recv_near, recv_far, f6, got)
+    )(particles, acc, local, f6, got)
 
 
 def solution(mesh):

time: 57.4 us -> 51.2 us (0.89); the launches traced: 56.3 us -> 51 us
  Pallas kernels: 39.5 us -> 34.3 us
  local copies, waits for them, and re-layouts: 1.52 us -> 0.81 us
  starting transfers between devices: 15 us -> 15.6 us
    pallas_call x11 -> x10, Pallas kernels: 38.6 us -> 33.4 us  [the longest x7 32 us: run_direct(): call(functools.partial(direct, tables, by_side, zero, extra, len(ins)), n...]
    unnamed x20 -> x6, local copies, waits for them, and re-layouts: 1.52 us -> 0.81 us
    ppermute x8, starting transfers between devices: 15 us -> 15.6 us  [swap(): return lax.ppermute(value, ALL, SWAPS[name])]
  transfers between devices with their start and end apart: 8 -> 8, of which waited for: 0 -> 1; matrix products, arithmetic and copies ran while one was open for 0% -> 0% of each run, Pallas kernels for 62% -> 63%
where the time goes in v3:
time: 51.2 us; the launch traced here: 51 us
  Pallas kernels  34.3 us (67%)
  starting transfers between devices  15.6 us (30%)
  local copies, waits for them, and re-layouts  0.81 us (2%)
    pallas_call x7, Pallas kernels, run_direct(): call(functools.partial(direct, tables, by_side, zero, extra, len(ins)), n...  32 us
    ppermute x8, starting transfers between devices, swap(): return lax.ppermute(value, ALL, SWAPS[name])  15.6 us
    pallas_call x1, Pallas kernels, body(): call(finish, 'finish', [V] * 5, shaped(2, SIDE, SIDE, SIZE), far_scratch(...  1.18 us
  transfers between devices with their start and end apart: 8, of which 1 were waited for; matrix products, arithmetic and copies ran while one was open for 0% of the time, Pallas kernels for 63%

profile of v3, /device:TPU:0, one launch (start us, length us, event | category | flops | bytes accessed | tf_op | source)
XLA Modules:
  0.0 51.0 jit_solution(11490795422021465754)
XLA Ops:
  0.0 0.8 %copy-done = f32[3,4,4,256]{3,2,1,0:T(4,128)S(1)} copy-done((f32[3,4,4,256]{3,2,1,0:T(4,128)S(1)}, f32[3,4,4,256]{3,2,1,0:T(4,128)}, u32[]{:S(2)}) %copy-start) | copy-done | bytes 49176
  0.8 0.9 %prepare_own.1 = (bf16[16,32,256]{2,1,0:T(8,128)(2,1)S(1)}, bf16[16,256,32]{2,1,0:T(8,128)(2,1)S(1)}, bf16[16,16,256]{2,1,0:T(8,128)(2,1)S(1)}, f32[24,128]{1,0:...) custom-call(f32[3,4,4,256]{3,2,1,0:T(4,128)S(1)} %copy-done), custom_call_target="tpu_custom_call" | custom-call | flops 4000000 | bytes 1048576 | tf_op jit(solution)/shard_map/prepare_own/pallas_call | solution.py:524
  1.7 0.0 copy-start.2
  1.7 0.1 collective-permute-start
  1.8 0.7 %collective-permute-start.1 = (f32[72,256]{1,0:T(8,128)S(1)}, f32[72,256]{1,0:T(8,128)S(1)}, u32[]{:S(2)}, u32[]{:S(2)}) collective-permute-start(f32[72,256]{1,0:T(8,128)S(1)} %get-tuple-element.54), channel_id=1, source_target_pairs={{4,8},{5,9},{6,10},{7,11},{8,4},{9,5},{10,6},{11,7},{12,16},{13,17... | collective-permute-start | bytes 221192 | tf_op jit(solution)/shard_map/ppermute | solution.py:71
  2.5 0.0 copy-start.1
  2.5 7.4 %direct_own_0.1 = (f32[16,16,256]{2,1,0:T(8,128)S(1)}, f32[17,16,1,256]{3,2,1,0:T(1,128)S(1)}) custom-call(s32[4,4,16]{2,1,0:T(4,128)S(1)} %bitcast.1, bf16[16,32,256]{2,1,0:T(8,128)(2,1)S(1)} %get-tuple-element.57.t_ref, bf16[16,256,32]{2,1,0:T(8,128)(2,1)S(1)} %get-tuple-element.58.s_ref, bf16[16,16,256]{2,1,0:T(8,128)(2,1)S(1)} %get-tuple-element.59.w_ref), custom_call_target="tpu_custom_call" | custom-call | flops 39199997952 | bytes 1048576 | tf_op jit(solution)/shard_map/direct_own_0/pallas_call | solution.py:506
  9.9 0.0 collective-permute-done.ra_ref.refs_1_
  9.9 0.0 collective-permute-done.1.rb_ref.refs_2_
  9.9 0.2 pack_slab.1
  10.1 1.7 %collective-permute-start.2 = (f32[96,256]{1,0:T(8,128)S(1)}, f32[96,256]{1,0:T(8,128)S(1)}, u32[]{:S(2)}, u32[]{:S(2)}) collective-permute-start(f32[96,256]{1,0:T(8,128)S(1)} %get-tuple-element.62), channel_id=1, source_target_pairs={{0,1},{1,0},{2,3},{3,2},{4,5},{5,4},{6,7},{7,6},{8,9},{9,8},{10,11... | collective-permute-start | bytes 294920 | tf_op jit(solution)/shard_map/ppermute | solution.py:71
  11.8 4.0 %direct_own_1.1 = (f32[16,16,256]{2,1,0:T(8,128)S(1)}, bf16[16,256,32]{2,1,0:T(8,128)(2,1)S(1)}, bf16[16,16,256]{2,1,0:T(8,128)(2,1)S(1)}) custom-call(f32[17,16,1,256]{3,2,1,0:T(1,128)S(1)} %get-tuple-element.65.mask_ref, bf16[16,32,256]{2,1,0:T(8,128)(2,1)S(1)} %get-tuple-element.57.t_ref, ...), custom_call_target="tpu_custom_call", output_to_operand_aliasing={{0}: (4, {})} | custom-call | flops 19599998976 | bytes 1048576 | tf_op jit(solution)/shard_map/direct_own_1/pallas_call | solution.py:506
  15.9 2.4 %collective-permute-start.3 = (f32[96,256]{1,0:T(8,128)S(1)}, f32[96,256]{1,0:T(8,128)S(1)}, u32[]{:S(2)}, u32[]{:S(2)}) collective-permute-start(f32[96,256]{1,0:T(8,128)S(1)} %get-tuple-element.70), channel_id=1, source_target_pairs={{0,3},{1,2},{2,1},{3,0},{4,7},{5,6},{6,5},{7,4},{8,11},{9,10},{10,... | collective-permute-start | bytes 294920 | tf_op jit(solution)/shard_map/ppermute | solution.py:71
  18.3 4.0 %direct_own_2.1 = (f32[16,16,256]{2,1,0:T(8,128)S(1)}, bf16[16,256,32]{2,1,0:T(8,128)(2,1)S(1)}, bf16[16,16,256]{2,1,0:T(8,128)(2,1)S(1)}) custom-call(f32[17,16,1,256]{3,2,1,0:T(1,128)S(1)} %get-tuple-element.65.mask_ref, bf16[16,32,256]{2,1,0:T(8,128)(2,1)S(1)} %get-tuple-element.57.t_ref, ...), custom_call_target="tpu_custom_call", output_to_operand_aliasing={{0}: (4, {})} | custom-call | flops 19599998976 | bytes 1048576 | tf_op jit(solution)/shard_map/direct_own_2/pallas_call | solution.py:506
  22.3 3.5 %collective-permute-start.4 = (f32[24,128]{1,0:T(8,128)S(1)}, f32[24,128]{1,0:T(8,128)S(1)}, u32[]{:S(2)}, u32[]{:S(2)}) collective-permute-start(f32[24,128]{1,0:T(8,128)S(1)} %slice_add_fusion), channel_id=1, source_target_pairs={{0,8},{1,9},{2,10},{3,11},{4,12},{5,13},{6,14},{7,15},{8,0},{9,1},... | collective-permute-start | bytes 36872 | tf_op jit(solution)/shard_map/ppermute | solution.py:71
  25.8 6.9 %direct_slab.1 = (f32[16,16,256]{2,1,0:T(8,128)S(1)}, bf16[16,256,32]{2,1,0:T(8,128)(2,1)S(1)}, bf16[16,16,256]{2,1,0:T(8,128)(2,1)S(1)}) custom-call(f32[17,16,1,256]{3,2,1,0:T(1,128)S(1)} %get-tuple-element.65.mask_ref, bf16[16,32,256]{2,1,0:T(8,128)(2,1)S(1)} %get-tuple-element.57.t_ref, ...), custom_call_target="tpu_custom_call", output_to_operand_aliasing={{0}: (4, {})} | custom-call | flops 33600000000 | bytes 1048576 | tf_op jit(solution)/shard_map/direct_slab/pallas_call | solution.py:506
  32.7 3.1 %collective-permute-start.5 = (f32[24,128]{1,0:T(8,128)S(1)}, f32[24,128]{1,0:T(8,128)S(1)}, u32[]{:S(2)}, u32[]{:S(2)}) collective-permute-start(f32[24,128]{1,0:T(8,128)S(1)} %add.13), channel_id=1, source_target_pairs={{0,24},{1,25},{2,26},{3,27},{4,28},{5,29},{6,30},{7,31},{8,16},{9,... | collective-permute-start | bytes 36872 | tf_op jit(solution)/shard_map/ppermute | solution.py:71
  35.8 5.0 %direct_leaf_near.1 = (f32[16,16,256]{2,1,0:T(8,128)S(1)}, f32[16,128]{1,0:T(8,128)S(1)}) custom-call(f32[17,16,1,256]{3,2,1,0:T(1,128)S(1)} %get-tuple-element.65.mask_ref, bf16[16,32,256]{2,1,0:T(8,128)(2,1)S(1)} %get-tuple-element.57.t_ref, bf16[16,256,32]{2,1,0:T(8,128)(2,1)S(1)} %get-tuple-element.83.s_ref, ...), custom_call_target="tpu_custom_call", output_to_operand_aliasing={{0}: (4, {})} | custom-call | flops 24000000000 | bytes 1048576 | tf_op jit(solution)/shard_map/direct_leaf_near/pallas_call | solution.py:506
  40.8 1.6 %collective-permute-start.6 = (f32[24,128]{1,0:T(8,128)S(1)}, f32[24,128]{1,0:T(8,128)S(1)}, u32[]{:S(2)}, u32[]{:S(2)}) collective-permute-start(f32[24,128]{1,0:T(8,128)S(1)} %add.14), channel_id=1, source_target_pairs={{0,32},{1,33},{2,34},{3,35},{4,36},{5,37},{6,38},{7,39},{8,40},{9,... | collective-permute-start | bytes 36872 | tf_op jit(solution)/shard_map/ppermute | solution.py:71
  42.4 2.4 %direct_leaf_far_0.1.refs_0_ = f32[16,16,256]{2,1,0:T(8,128)S(1)} custom-call(f32[17,16,1,256]{3,2,1,0:T(1,128)S(1)} %get-tuple-element.65.mask_ref, bf16[16,32,256]{2,1,0:T(8,128)(2,1)S(1)} %get-tuple-element.57.t_ref, bf16[16,256,32]{2,1,0:T(8,128)(2,1)S(1)} %get-tuple-element.91.s_ref, ...), custom_call_target="tpu_custom_call", output_to_operand_aliasing={{}: (4, {})} | custom-call | flops 12000000000 | bytes 1048576 | tf_op jit(solution)/shard_map/direct_leaf_far_0/pallas_call | solution.py:506
  44.8 2.6 %collective-permute-start.7 = (f32[24,128]{1,0:T(8,128)S(1)}, f32[24,128]{1,0:T(8,128)S(1)}, u32[]{:S(2)}, u32[]{:S(2)}) collective-permute-start(f32[24,128]{1,0:T(8,128)S(1)} %add.15.f_ref), channel_id=1, source_target_pairs={{0,96},{1,97},{2,98},{3,99},{4,100},{5,101},{6,102},{7,103},{8,104... | collective-permute-start | bytes 36872 | tf_op jit(solution)/shard_map/ppermute | solution.py:71
  47.4 2.4 %direct_leaf_far_1.1.acc_ref = f32[16,16,256]{2,1,0:T(8,128)S(1)} custom-call(f32[17,16,1,256]{3,2,1,0:T(1,128)S(1)} %get-tuple-element.65.mask_ref, bf16[16,32,256]{2,1,0:T(8,128)(2,1)S(1)} %get-tuple-element.57.t_ref, bf16[16,256,32]{2,1,0:T(8,128)(2,1)S(1)} %get-tuple-element.91.s_ref, ...), custom_call_target="tpu_custom_call", output_to_operand_aliasing={{}: (4, {})} | custom-call | flops 12000000000 | bytes 1048576 | tf_op jit(solution)/shard_map/direct_leaf_far_1/pallas_call | solution.py:506
  49.7 0.1 collective-permute-done.7.got_ref
  49.8 1.2 %finish.1 = f32[2,4,4,256]{3,2,1,0:T(4,128)} custom-call(f32[3,4,4,256]{3,2,1,0:T(4,128)S(1)} %copy-done.1, f32[16,16,256]{2,1,0:T(8,128)S(1)} %direct_leaf_far_1.1.acc_ref, f32[16,128]{1,0:T(8,128)S(1)} %get-tuple-element.99.near_ref, f32[24,128]{1,0:T(8,128)S(1)} %add.15.f_ref, f32[24,128]{1,0:T(8,128)S(1)} %collective-permute-done.7.got_ref), custom_call_target="tpu_custom_call" | custom-call | flops 4000000 | bytes 1048576 | tf_op jit(solution)/shard_map/finish/pallas_call | solution.py:607
  (13 shorter events, 0.1 us)
Async XLA Ops:
  0.0 0.8 %copy-start = (f32[3,4,4,256]{3,2,1,0:T(4,128)S(1)}, f32[3,4,4,256]{3,2,1,0:T(4,128)}, u32[]{:S(2)}) copy-start(f32[3,4,4,256]{3,2,1,0:T(4,128)} %part_ref.5) | copy-start | bytes 147460
  1.7 0.8 %copy-start.2 = (s32[16,4,4]{0,2,1:T(4,128)S(1)}, s32[16,4,4]{0,2,1:T(4,128)}, u32[]{:S(2)}) copy-start(s32[16,4,4]{0,2,1:T(4,128)} %param.3) | copy-start | bytes 3076
  1.7 8.2 %collective-permute-start = (f32[72,256]{1,0:T(8,128)S(1)}, f32[72,256]{1,0:T(8,128)S(1)}, u32[]{:S(2)}, u32[]{:S(2)}) collective-permute-start(f32[72,256]{1,0:T(8,128)S(1)} %get-tuple-element.53), channel_id=1, source_target_pairs={{0,4},{1,5},{2,6},{3,7},{4,0},{5,1},{6,2},{7,3},{8,12},{9,13},{10,... | collective-permute-start | bytes 221192 | tf_op jit(solution)/shard_map/ppermute | solution.py:71
  1.8 8.1 %collective-permute-start.1 = (f32[72,256]{1,0:T(8,128)S(1)}, f32[72,256]{1,0:T(8,128)S(1)}, u32[]{:S(2)}, u32[]{:S(2)}) collective-permute-start(f32[72,256]{1,0:T(8,128)S(1)} %get-tuple-element.54), channel_id=1, source_target_pairs={{4,8},{5,9},{6,10},{7,11},{8,4},{9,5},{10,6},{11,7},{12,16},{13,17... | collective-permute-start | bytes 221192 | tf_op jit(solution)/shard_map/ppermute | solution.py:71
  2.5 7.4 %copy-start.1 = (f32[3,4,4,256]{3,2,1,0:T(4,128)S(1)}, f32[3,4,4,256]{3,2,1,0:T(4,128)}, u32[]{:S(2)}) copy-start(f32[3,4,4,256]{3,2,1,0:T(4,128)} %part_ref.5) | copy-start | bytes 147460
  10.1 5.7 %collective-permute-start.2 = (f32[96,256]{1,0:T(8,128)S(1)}, f32[96,256]{1,0:T(8,128)S(1)}, u32[]{:S(2)}, u32[]{:S(2)}) collective-permute-start(f32[96,256]{1,0:T(8,128)S(1)} %get-tuple-element.62), channel_id=1, source_target_pairs={{0,1},{1,0},{2,3},{3,2},{4,5},{5,4},{6,7},{7,6},{8,9},{9,8},{10,11... | collective-permute-start | bytes 294920 | tf_op jit(solution)/shard_map/ppermute | solution.py:71
  15.9 6.4 %collective-permute-start.3 = (f32[96,256]{1,0:T(8,128)S(1)}, f32[96,256]{1,0:T(8,128)S(1)}, u32[]{:S(2)}, u32[]{:S(2)}) collective-permute-start(f32[96,256]{1,0:T(8,128)S(1)} %get-tuple-element.70), channel_id=1, source_target_pairs={{0,3},{1,2},{2,1},{3,0},{4,7},{5,6},{6,5},{7,4},{8,11},{9,10},{10,... | collective-permute-start | bytes 294920 | tf_op jit(solution)/shard_map/ppermute | solution.py:71
  22.3 10.4 %collective-permute-start.4 = (f32[24,128]{1,0:T(8,128)S(1)}, f32[24,128]{1,0:T(8,128)S(1)}, u32[]{:S(2)}, u32[]{:S(2)}) collective-permute-start(f32[24,128]{1,0:T(8,128)S(1)} %slice_add_fusion), channel_id=1, source_target_pairs={{0,8},{1,9},{2,10},{3,11},{4,12},{5,13},{6,14},{7,15},{8,0},{9,1},... | collective-permute-start | bytes 36872 | tf_op jit(solution)/shard_map/ppermute | solution.py:71
  32.7 8.1 %collective-permute-start.5 = (f32[24,128]{1,0:T(8,128)S(1)}, f32[24,128]{1,0:T(8,128)S(1)}, u32[]{:S(2)}, u32[]{:S(2)}) collective-permute-start(f32[24,128]{1,0:T(8,128)S(1)} %add.13), channel_id=1, source_target_pairs={{0,24},{1,25},{2,26},{3,27},{4,28},{5,29},{6,30},{7,31},{8,16},{9,... | collective-permute-start | bytes 36872 | tf_op jit(solution)/shard_map/ppermute | solution.py:71
  40.8 4.0 %collective-permute-start.6 = (f32[24,128]{1,0:T(8,128)S(1)}, f32[24,128]{1,0:T(8,128)S(1)}, u32[]{:S(2)}, u32[]{:S(2)}) collective-permute-start(f32[24,128]{1,0:T(8,128)S(1)} %add.14), channel_id=1, source_target_pairs={{0,32},{1,33},{2,34},{3,35},{4,36},{5,37},{6,38},{7,39},{8,40},{9,... | collective-permute-start | bytes 36872 | tf_op jit(solution)/shard_map/ppermute | solution.py:71
  44.8 5.0 %collective-permute-start.7 = (f32[24,128]{1,0:T(8,128)S(1)}, f32[24,128]{1,0:T(8,128)S(1)}, u32[]{:S(2)}, u32[]{:S(2)}) collective-permute-start(f32[24,128]{1,0:T(8,128)S(1)} %add.15.f_ref), channel_id=1, source_target_pairs={{0,96},{1,97},{2,98},{3,99},{4,100},{5,101},{6,102},{7,103},{8,104... | collective-permute-start | bytes 36872 | tf_op jit(solution)/shard_map/ppermute | solution.py:71

commit v4 on v3

--- a/solution.py
+++ b/solution.py
@@ -279,7 +279,24 @@
     return out
 
 
-def direct(tables, by_side, zero, extra, extra_in, mask_ref, t_ref, s_ref, w_ref, *refs):
+HEAD_START = (
+    ((85, 80, 81, 70), (0, -14, -15, -6), (0, -12, -18, -6)),
+    ((86, 58, 39, 47), (0, -13, -20, -11), (0, -14, -26, -11)),
+)
+FLEX_STEPS = (22, 43, 65, 83)
+
+
+def early_bodies():
+    slab, leaf, core, unused, unused = position()
+    ahead = [
+        chosen((slab >> 1) & 3, by_z) + chosen(slab >> 3, by_x) + chosen(leaf, by_y)
+        for by_z, by_x, by_y in HEAD_START
+    ]
+    ahead = jnp.where(core == 0, ahead[0], ahead[1])
+    return sum((ahead >= step).astype(jnp.int32) for step in FLEX_STEPS)
+
+
+def direct(tables, mode, zero, extra, extra_in, mask_ref, t_ref, s_ref, w_ref, *refs):
     if zero:
         acc_ref, rows_ref = refs
         acc_ref[...] = jnp.zeros_like(acc_ref)
@@ -309,12 +326,14 @@
                 acc_ref[t] = acc_ref[t] + mask_ref[o, t] * total
         return 0
 
-    if by_side:
+    if mode == "side":
         step(position()[3], 0)
-    elif tables.shape[0] == 1:
+    elif mode == "early":
+        lax.fori_loop(0, early_bodies(), step, 0)
+    elif mode == "late":
+        lax.fori_loop(early_bodies(), tables.shape[0], step, 0)
+    else:
         step(0, 0)
-    else:
-        lax.fori_loop(0, tables.shape[0], step, 0)
     if extra is not None:
         extra(*others)
 
@@ -500,16 +519,16 @@
 PAIR = 400_000_000
 
 
-def run_direct(name, tables, mask, feats, acc, by_side=False, extra=None, ins=(), outs=(), scratch=()):
+def run_direct(name, tables, mask, feats, acc, mode="", extra=None, ins=(), outs=(), scratch=()):
     zero = acc is None
     args = [mask, *feats] + ([] if zero else [acc]) + list(ins)
     got = call(
-        functools.partial(direct, tables, by_side, zero, extra, len(ins)),
+        functools.partial(direct, tables, mode, zero, extra, len(ins)),
         name,
         [V] * len(args),
         [shaped(LEAVES, 16, SIZE), *outs],
         list(scratch),
-        PAIR * (1 if by_side else tables.shape[0]) * tables.shape[1],
+        PAIR * tables.shape[1],
         {} if zero else {4: 0},
     )(*args)
     return got if outs else got[0]
@@ -530,13 +549,16 @@
         stages(True),
         SMALL,
     )(particles)
+    own = pair_table("own")
+    flex = own[:112].reshape(4, 28, 3)
+    feats = (t0, s0, w0)
+    acc, mask = run_direct(
+        "direct_early", flex, turned, feats, None, "early", outs=[shaped(17, LEAVES, 1, SIZE)]
+    )
+    send_a, send_b, acc = lax.optimization_barrier((send_a, send_b, acc))
     recv_a = swap(send_a, "core")
     recv_b = swap(send_b, "slab")
-    own = pair_table("own")
-    feats = (t0, s0, w0)
-    acc, mask = run_direct(
-        "direct_own_0", own[:98].reshape(2, 49, 3), turned, feats, None, outs=[shaped(17, LEAVES, 1, SIZE)]
-    )
+    acc = run_direct("direct_own_0", own[None, 112:140], mask, feats, acc)
     m1, f1, send_near, send_far = call(
         pack_slab,
         "pack_slab",
@@ -549,7 +571,7 @@
     recv_near = swap(send_near, "leaf_near")
     built = dict(outs=features_out(LEAVES), scratch=stages(False))
     acc, s1, w1 = run_direct(
-        "direct_own_1", own[None, 98:147], mask, feats, acc, extra=slab_halo, ins=(recv_a, recv_b), **built
+        "direct_own_1", own[None, 140:168], mask, feats, acc, extra=slab_halo, ins=(recv_a, recv_b), **built
     )
     f2, send_far = call(
         pack_near, "pack_near", [V, V, V, A], [shaped(24, 128), shaped(LEAF_ROWS, SIZE)], [], SMALL
@@ -557,52 +579,42 @@
     send_far, acc = lax.optimization_barrier((send_far, acc))
     recv_far = swap(send_far, "leaf_far")
     acc, s2, w2 = run_direct(
-        "direct_own_2", own[None, 147:], mask, feats, acc, extra=near_halo, ins=(recv_near,), **built
+        "direct_own_2", own[None, 168:], mask, feats, acc, extra=near_halo, ins=(recv_near,), **built
     )
     recv_far, acc = lax.optimization_barrier((recv_far, acc))
-    f3 = f2 + recv_far[72:96, 0:128]
-    f3, acc = lax.optimization_barrier((f3, acc))
-    got = swap(f3, "z_near")
-    acc, s3, w3 = run_direct(
-        "direct_slab",
-        pair_table("slab").reshape(2, 42, 3),
-        mask,
-        (t0, s1, w1),
-        acc,
-        extra=far_halo,
-        ins=(recv_far,),
-        **built,
-    )
-    got, acc = lax.optimization_barrier((got, acc))
-    f4 = f3 + got
-    f4, acc = lax.optimization_barrier((f4, acc))
-    got = swap(f4, "z_far")
+    blocks = f2 + recv_far[72:96, 0:128]
+    slab_pairs = pair_table("slab").reshape(3, 1, 28, 3)
+    for number, axis in enumerate(("z_near", "z_far", "x_near")):
+        blocks, acc = lax.optimization_barrier((blocks, acc))
+        got = swap(blocks, axis)
+        name = f"direct_slab_{number}"
+        slab_feats = (t0, s1, w1)
+        if number == 0:
+            acc, s3, w3 = run_direct(
+                name, slab_pairs[number], mask, slab_feats, acc, extra=far_halo, ins=(recv_far,), **built
+            )
+        else:
+            acc = run_direct(name, slab_pairs[number], mask, slab_feats, acc)
+        got, acc = lax.optimization_barrier((got, acc))
+        blocks = blocks + got
+    blocks, acc = lax.optimization_barrier((blocks, acc))
+    got = swap(blocks, "x_far")
     right = pair_table("leaf", True)
     left = pair_table("leaf", False)
-    near_pairs = np.stack([right, left])
-    far_pairs = np.stack([left, right])
     acc, local = run_direct(
         "direct_leaf_near",
-        near_pairs,
+        np.stack([right, left]),
         mask,
         (t0, s2, w2),
         acc,
-        True,
+        "side",
         extra=leaf_field,
         ins=(turned, m1, recv_near, recv_far),
         outs=[shaped(LEAVES, 128)],
         scratch=far_scratch(256),
     )
-    got, acc = lax.optimization_barrier((got, acc))
-    f5 = f4 + got
-    f5, acc = lax.optimization_barrier((f5, acc))
-    got = swap(f5, "x_near")
-    acc = run_direct("direct_leaf_far_0", far_pairs[:, :30], mask, (t0, s3, w3), acc, True)
-    got, acc = lax.optimization_barrier((got, acc))
-    f6 = f5 + got
-    f6, acc = lax.optimization_barrier((f6, acc))
-    got = swap(f6, "x_far")
-    acc = run_direct("direct_leaf_far_1", far_pairs[:, 30:], mask, (t0, s3, w3), acc, True)
+    acc = run_direct("direct_leaf_far", np.stack([left, right]), mask, (t0, s3, w3), acc, "side")
+    acc = run_direct("direct_late", flex, mask, feats, acc, "late")
     got, acc = lax.optimization_barrier((got, acc))
     return call(
         finish,
@@ -611,7 +623,7 @@
         shaped(2, SIDE, SIDE, SIZE),
         far_scratch(128) + [pltpu.VMEM((LEAVES, 128), F32)],
         SMALL,
-    )(particles, acc, local, f6, got)
+    )(particles, acc, local, blocks, got)
 
 
 def solution(mesh):

time: 51.2 us -> 55.2 us (1.078)
  the two profiles are of different devices: /device:TPU:0 before, /device:TPU:69 now
where the time goes in v4:
time: 55.2 us; the launch traced here: 55 us
  Pallas kernels  35 us (63%)
  starting transfers between devices  13.7 us (25%)
  waiting for transfers between devices  5.36 us (10%)
  local copies, waits for them, and re-layouts  0.81 us (1%)
    pallas_call x10, Pallas kernels, run_direct(): call(functools.partial(direct, tables, mode, zero, extra, len(ins)), name...  32.7 us
    ppermute x8, starting transfers between devices, swap(): return lax.ppermute(value, ALL, SWAPS[name])  13.7 us
    ppermute x8, waiting for transfers between devices, swap(): return lax.ppermute(value, ALL, SWAPS[name])  5.36 us
    pallas_call x1, Pallas kernels, body(): call(finish, 'finish', [V] * 5, shaped(2, SIDE, SIDE, SIZE), far_scratch(...  1.19 us
  transfers between devices with their start and end apart: 8, of which 5 were waited for; matrix products, arithmetic and copies ran while one was open for 0% of the time, Pallas kernels for 59%

profile of v4, /device:TPU:69, one launch (start us, length us, event | category | flops | bytes accessed | tf_op | source)
XLA Modules:
  0.0 55.0 jit_solution(9315800131719510731)
XLA Ops:
  0.0 0.8 %copy-done = f32[3,4,4,256]{3,2,1,0:T(4,128)S(1)} copy-done((f32[3,4,4,256]{3,2,1,0:T(4,128)S(1)}, f32[3,4,4,256]{3,2,1,0:T(4,128)}, u32[]{:S(2)}) %copy-start) | copy-done | bytes 49176
  0.8 0.9 %prepare_own.1 = (bf16[16,32,256]{2,1,0:T(8,128)(2,1)S(1)}, bf16[16,256,32]{2,1,0:T(8,128)(2,1)S(1)}, bf16[16,16,256]{2,1,0:T(8,128)(2,1)S(1)}, f32[24,128]{1,0:...) custom-call(f32[3,4,4,256]{3,2,1,0:T(4,128)S(1)} %copy-done), custom_call_target="tpu_custom_call" | custom-call | flops 4000000 | bytes 1048576 | tf_op jit(solution)/shard_map/prepare_own/pallas_call | solution.py:543
  1.7 0.2 direct_early.1
  1.9 7.3 %collective-permute-start = (f32[72,256]{1,0:T(8,128)S(1)}, f32[72,256]{1,0:T(8,128)S(1)}, u32[]{:S(2)}, u32[]{:S(2)}) collective-permute-start(f32[72,256]{1,0:T(8,128)S(1)} %get-tuple-element.62), channel_id=1, source_target_pairs={{0,4},{1,5},{2,6},{3,7},{4,0},{5,1},{6,2},{7,3},{8,12},{9,13},{10,... | collective-permute-start | bytes 221192 | tf_op jit(solution)/shard_map/ppermute | solution.py:71
  9.1 1.9 %collective-permute-start.1 = (f32[72,256]{1,0:T(8,128)S(1)}, f32[72,256]{1,0:T(8,128)S(1)}, u32[]{:S(2)}, u32[]{:S(2)}) collective-permute-start(f32[72,256]{1,0:T(8,128)S(1)} %get-tuple-element.63), channel_id=1, source_target_pairs={{4,8},{5,9},{6,10},{7,11},{8,4},{9,5},{10,6},{11,7},{12,16},{13,17... | collective-permute-start | bytes 221192 | tf_op jit(solution)/shard_map/ppermute | solution.py:71
  11.1 2.2 %direct_own_0.1.after_ref.refs_0_ = f32[16,16,256]{2,1,0:T(8,128)S(1)} custom-call(f32[17,16,1,256]{3,2,1,0:T(1,128)S(1)} %get-tuple-element.66.mask_ref, bf16[16,32,256]{2,1,0:T(8,128)(2,1)S(1)} %get-tuple-element.58.t_ref, bf16[16,256,32]{2,1,0:T(8,128)(2,1)S(1)} %get-tuple-element.59.s_ref, ...), custom_call_target="tpu_custom_call", output_to_operand_aliasing={{}: (4, {})} | custom-call | flops 11200000000 | bytes 1048576 | tf_op jit(solution)/shard_map/direct_own_0/pallas_call | solution.py:525
  13.3 1.5 %collective-permute-done.1.rb_ref.refs_2_ = f32[72,256]{1,0:T(8,128)S(1)} collective-permute-done((f32[72,256]{1,0:T(8,128)S(1)}, f32[72,256]{1,0:T(8,128)S(1)}, u32[]{:S(2)}, u32[]{:S(2)}) %collective-permute-start.1) | collective-permute-done | bytes 73760 | tf_op jit(solution)/shard_map/ppermute | solution.py:71
  14.8 0.2 pack_slab.1
  15.0 2.5 %direct_own_1.1 = (f32[16,16,256]{2,1,0:T(8,128)S(1)}, bf16[16,256,32]{2,1,0:T(8,128)(2,1)S(1)}, bf16[16,16,256]{2,1,0:T(8,128)(2,1)S(1)}) custom-call(f32[17,16,1,256]{3,2,1,0:T(1,128)S(1)} %get-tuple-element.66.mask_ref, bf16[16,32,256]{2,1,0:T(8,128)(2,1)S(1)} %get-tuple-element.58.t_ref, ...), custom_call_target="tpu_custom_call", output_to_operand_aliasing={{0}: (4, {})} | custom-call | flops 11200000000 | bytes 1048576 | tf_op jit(solution)/shard_map/direct_own_1/pallas_call | solution.py:525
  17.6 1.8 %collective-permute-done.2.r_ref.refs_1_.refs_3_ = f32[96,256]{1,0:T(8,128)S(1)} collective-permute-done((f32[96,256]{1,0:T(8,128)S(1)}, f32[96,256]{1,0:T(8,128)S(1)}, u32[]{:S(2)}, u32[]{:S(2)}) %collective-permute-start.2) | collective-permute-done | bytes 98336 | tf_op jit(solution)/shard_map/ppermute | solution.py:71
  19.3 0.6 %collective-permute-start.3 = (f32[96,256]{1,0:T(8,128)S(1)}, f32[96,256]{1,0:T(8,128)S(1)}, u32[]{:S(2)}, u32[]{:S(2)}) collective-permute-start(f32[96,256]{1,0:T(8,128)S(1)} %get-tuple-element.76), channel_id=1, source_target_pairs={{0,3},{1,2},{2,1},{3,0},{4,7},{5,6},{6,5},{7,4},{8,11},{9,10},{10,... | collective-permute-start | bytes 294920 | tf_op jit(solution)/shard_map/ppermute | solution.py:71
  20.0 2.5 %direct_own_2.1 = (f32[16,16,256]{2,1,0:T(8,128)S(1)}, bf16[16,256,32]{2,1,0:T(8,128)(2,1)S(1)}, bf16[16,16,256]{2,1,0:T(8,128)(2,1)S(1)}) custom-call(f32[17,16,1,256]{3,2,1,0:T(1,128)S(1)} %get-tuple-element.66.mask_ref, bf16[16,32,256]{2,1,0:T(8,128)(2,1)S(1)} %get-tuple-element.58.t_ref, ...), custom_call_target="tpu_custom_call", output_to_operand_aliasing={{0}: (4, {})} | custom-call | flops 11200000000 | bytes 1048576 | tf_op jit(solution)/shard_map/direct_own_2/pallas_call | solution.py:525
  22.5 1.6 %collective-permute-done.3.refs_1_.refs_4_ = f32[96,256]{1,0:T(8,128)S(1)} collective-permute-done((f32[96,256]{1,0:T(8,128)S(1)}, f32[96,256]{1,0:T(8,128)S(1)}, u32[]{:S(2)}, u32[]{:S(2)}) %collective-permute-start.3) | collective-permute-done | bytes 98336 | tf_op jit(solution)/shard_map/ppermute | solution.py:71
  24.1 1.6 %collective-permute-start.4 = (f32[24,128]{1,0:T(8,128)S(1)}, f32[24,128]{1,0:T(8,128)S(1)}, u32[]{:S(2)}, u32[]{:S(2)}) collective-permute-start(f32[24,128]{1,0:T(8,128)S(1)} %slice_add_fusion), channel_id=1, source_target_pairs={{0,8},{1,9},{2,10},{3,11},{4,12},{5,13},{6,14},{7,15},{8,0},{9,1},... | collective-permute-start | bytes 36872 | tf_op jit(solution)/shard_map/ppermute | solution.py:71
  25.7 2.5 %direct_slab_0.1 = (f32[16,16,256]{2,1,0:T(8,128)S(1)}, bf16[16,256,32]{2,1,0:T(8,128)(2,1)S(1)}, bf16[16,16,256]{2,1,0:T(8,128)(2,1)S(1)}) custom-call(f32[17,16,1,256]{3,2,1,0:T(1,128)S(1)} %get-tuple-element.66.mask_ref, bf16[16,32,256]{2,1,0:T(8,128)(2,1)S(1)} %get-tuple-element.58.t_ref, ...), custom_call_target="tpu_custom_call", output_to_operand_aliasing={{0}: (4, {})} | custom-call | flops 11200000000 | bytes 1048576 | tf_op jit(solution)/shard_map/direct_slab_0/pallas_call | solution.py:525
  28.4 2.2 %direct_slab_1.1.refs_0_ = f32[16,16,256]{2,1,0:T(8,128)S(1)} custom-call(f32[17,16,1,256]{3,2,1,0:T(1,128)S(1)} %get-tuple-element.66.mask_ref, bf16[16,32,256]{2,1,0:T(8,128)(2,1)S(1)} %get-tuple-element.58.t_ref, bf16[16,256,32]{2,1,0:T(8,128)(2,1)S(1)} %get-tuple-element.82.s_ref, ...), custom_call_target="tpu_custom_call", output_to_operand_aliasing={{}: (4, {})} | custom-call | flops 11200000000 | bytes 1048576 | tf_op jit(solution)/shard_map/direct_slab_1/pallas_call | solution.py:525
  30.6 0.3 collective-permute-done.5
  30.9 0.2 collective-permute-start.6
  31.1 2.2 %direct_slab_2.1.refs_0_ = f32[16,16,256]{2,1,0:T(8,128)S(1)} custom-call(f32[17,16,1,256]{3,2,1,0:T(1,128)S(1)} %get-tuple-element.66.mask_ref, bf16[16,32,256]{2,1,0:T(8,128)(2,1)S(1)} %get-tuple-element.58.t_ref, bf16[16,256,32]{2,1,0:T(8,128)(2,1)S(1)} %get-tuple-element.82.s_ref, ...), custom_call_target="tpu_custom_call", output_to_operand_aliasing={{}: (4, {})} | custom-call | flops 11200000000 | bytes 1048576 | tf_op jit(solution)/shard_map/direct_slab_2/pallas_call | solution.py:525
  33.5 2.0 %collective-permute-start.7 = (f32[24,128]{1,0:T(8,128)S(1)}, f32[24,128]{1,0:T(8,128)S(1)}, u32[]{:S(2)}, u32[]{:S(2)}) collective-permute-start(f32[24,128]{1,0:T(8,128)S(1)} %add.15.f_ref), channel_id=1, source_target_pairs={{0,96},{1,97},{2,98},{3,99},{4,100},{5,101},{6,102},{7,103},{8,104... | collective-permute-start | bytes 36872 | tf_op jit(solution)/shard_map/ppermute | solution.py:71
  35.5 5.0 %direct_leaf_near.1 = (f32[16,16,256]{2,1,0:T(8,128)S(1)}, f32[16,128]{1,0:T(8,128)S(1)}) custom-call(f32[17,16,1,256]{3,2,1,0:T(1,128)S(1)} %get-tuple-element.66.mask_ref, bf16[16,32,256]{2,1,0:T(8,128)(2,1)S(1)} %get-tuple-element.58.t_ref, bf16[16,256,32]{2,1,0:T(8,128)(2,1)S(1)} %get-tuple-element.99.s_ref, ...), custom_call_target="tpu_custom_call", output_to_operand_aliasing={{0}: (4, {})} | custom-call | flops 24000000000 | bytes 1048576 | tf_op jit(solution)/shard_map/direct_leaf_near/pallas_call | solution.py:525
  40.5 4.4 %direct_leaf_far.1.refs_0_ = f32[16,16,256]{2,1,0:T(8,128)S(1)} custom-call(f32[17,16,1,256]{3,2,1,0:T(1,128)S(1)} %get-tuple-element.66.mask_ref, bf16[16,32,256]{2,1,0:T(8,128)(2,1)S(1)} %get-tuple-element.58.t_ref, bf16[16,256,32]{2,1,0:T(8,128)(2,1)S(1)} %get-tuple-element.97.s_ref, ...), custom_call_target="tpu_custom_call", output_to_operand_aliasing={{}: (4, {})} | custom-call | flops 24000000000 | bytes 1048576 | tf_op jit(solution)/shard_map/direct_leaf_far/pallas_call | solution.py:525
  44.9 8.8 %direct_late.1.acc_ref = f32[16,16,256]{2,1,0:T(8,128)S(1)} custom-call(f32[17,16,1,256]{3,2,1,0:T(1,128)S(1)} %get-tuple-element.66.mask_ref, bf16[16,32,256]{2,1,0:T(8,128)(2,1)S(1)} %get-tuple-element.58.t_ref, bf16[16,256,32]{2,1,0:T(8,128)(2,1)S(1)} %get-tuple-element.59.s_ref, ...), custom_call_target="tpu_custom_call", output_to_operand_aliasing={{}: (4, {})} | custom-call | flops 11200000000 | bytes 1048576 | tf_op jit(solution)/shard_map/direct_late/pallas_call | solution.py:525
  53.8 1.2 %finish.1 = f32[2,4,4,256]{3,2,1,0:T(4,128)} custom-call(f32[3,4,4,256]{3,2,1,0:T(4,128)S(1)} %copy-done.1, f32[16,16,256]{2,1,0:T(8,128)S(1)} %direct_late.1.acc_ref, f32[16,128]{1,0:T(8,128)S(1)} %get-tuple-element.105.near_ref, f32[24,128]{1,0:T(8,128)S(1)} %add.15.f_ref, f32[24,128]{1,0:T(8,128)S(1)} %collective-permute-done.7.got_ref), custom_call_target="tpu_custom_call" | custom-call | flops 4000000 | bytes 1048576 | tf_op jit(solution)/shard_map/finish/pallas_call | solution.py:619
  (16 shorter events, 0.3 us)
Async XLA Ops:
  0.0 0.8 %copy-start = (f32[3,4,4,256]{3,2,1,0:T(4,128)S(1)}, f32[3,4,4,256]{3,2,1,0:T(4,128)}, u32[]{:S(2)}) copy-start(f32[3,4,4,256]{3,2,1,0:T(4,128)} %part_ref.5) | copy-start | bytes 147460
  0.8 0.9 %copy-start.2 = (s32[16,4,4]{0,2,1:T(4,128)S(1)}, s32[16,4,4]{0,2,1:T(4,128)}, u32[]{:S(2)}) copy-start(s32[16,4,4]{0,2,1:T(4,128)} %param.3) | copy-start | bytes 3076
  1.9 11.4 %collective-permute-start = (f32[72,256]{1,0:T(8,128)S(1)}, f32[72,256]{1,0:T(8,128)S(1)}, u32[]{:S(2)}, u32[]{:S(2)}) collective-permute-start(f32[72,256]{1,0:T(8,128)S(1)} %get-tuple-element.62), channel_id=1, source_target_pairs={{0,4},{1,5},{2,6},{3,7},{4,0},{5,1},{6,2},{7,3},{8,12},{9,13},{10,... | collective-permute-start | bytes 221192 | tf_op jit(solution)/shard_map/ppermute | solution.py:71
  9.1 5.7 %collective-permute-start.1 = (f32[72,256]{1,0:T(8,128)S(1)}, f32[72,256]{1,0:T(8,128)S(1)}, u32[]{:S(2)}, u32[]{:S(2)}) collective-permute-start(f32[72,256]{1,0:T(8,128)S(1)} %get-tuple-element.63), channel_id=1, source_target_pairs={{4,8},{5,9},{6,10},{7,11},{8,4},{9,5},{10,6},{11,7},{12,16},{13,17... | collective-permute-start | bytes 221192 | tf_op jit(solution)/shard_map/ppermute | solution.py:71
  11.1 3.7 %copy-start.1 = (f32[3,4,4,256]{3,2,1,0:T(4,128)S(1)}, f32[3,4,4,256]{3,2,1,0:T(4,128)}, u32[]{:S(2)}) copy-start(f32[3,4,4,256]{3,2,1,0:T(4,128)} %part_ref.5) | copy-start | bytes 147460
  15.0 4.4 %collective-permute-start.2 = (f32[96,256]{1,0:T(8,128)S(1)}, f32[96,256]{1,0:T(8,128)S(1)}, u32[]{:S(2)}, u32[]{:S(2)}) collective-permute-start(f32[96,256]{1,0:T(8,128)S(1)} %get-tuple-element.69), channel_id=1, source_target_pairs={{0,1},{1,0},{2,3},{3,2},{4,5},{5,4},{6,7},{7,6},{8,9},{9,8},{10,11... | collective-permute-start | bytes 294920 | tf_op jit(solution)/shard_map/ppermute | solution.py:71
  19.3 4.8 %collective-permute-start.3 = (f32[96,256]{1,0:T(8,128)S(1)}, f32[96,256]{1,0:T(8,128)S(1)}, u32[]{:S(2)}, u32[]{:S(2)}) collective-permute-start(f32[96,256]{1,0:T(8,128)S(1)} %get-tuple-element.76), channel_id=1, source_target_pairs={{0,3},{1,2},{2,1},{3,0},{4,7},{5,6},{6,5},{7,4},{8,11},{9,10},{10,... | collective-permute-start | bytes 294920 | tf_op jit(solution)/shard_map/ppermute | solution.py:71
  24.1 4.2 %collective-permute-start.4 = (f32[24,128]{1,0:T(8,128)S(1)}, f32[24,128]{1,0:T(8,128)S(1)}, u32[]{:S(2)}, u32[]{:S(2)}) collective-permute-start(f32[24,128]{1,0:T(8,128)S(1)} %slice_add_fusion), channel_id=1, source_target_pairs={{0,8},{1,9},{2,10},{3,11},{4,12},{5,13},{6,14},{7,15},{8,0},{9,1},... | collective-permute-start | bytes 36872 | tf_op jit(solution)/shard_map/ppermute | solution.py:71
  28.3 2.6 %collective-permute-start.5 = (f32[24,128]{1,0:T(8,128)S(1)}, f32[24,128]{1,0:T(8,128)S(1)}, u32[]{:S(2)}, u32[]{:S(2)}) collective-permute-start(f32[24,128]{1,0:T(8,128)S(1)} %add.13), channel_id=1, source_target_pairs={{0,24},{1,25},{2,26},{3,27},{4,28},{5,29},{6,30},{7,31},{8,16},{9,... | collective-permute-start | bytes 36872 | tf_op jit(solution)/shard_map/ppermute | solution.py:71
  30.9 2.5 %collective-permute-start.6 = (f32[24,128]{1,0:T(8,128)S(1)}, f32[24,128]{1,0:T(8,128)S(1)}, u32[]{:S(2)}, u32[]{:S(2)}) collective-permute-start(f32[24,128]{1,0:T(8,128)S(1)} %add.14), channel_id=1, source_target_pairs={{0,32},{1,33},{2,34},{3,35},{4,36},{5,37},{6,38},{7,39},{8,40},{9,... | collective-permute-start | bytes 36872 | tf_op jit(solution)/shard_map/ppermute | solution.py:71
  33.5 20.3 %collective-permute-start.7 = (f32[24,128]{1,0:T(8,128)S(1)}, f32[24,128]{1,0:T(8,128)S(1)}, u32[]{:S(2)}, u32[]{:S(2)}) collective-permute-start(f32[24,128]{1,0:T(8,128)S(1)} %add.15.f_ref), channel_id=1, source_target_pairs={{0,96},{1,97},{2,98},{3,99},{4,100},{5,101},{6,102},{7,103},{8,104... | collective-permute-start | bytes 36872 | tf_op jit(solution)/shard_map/ppermute | solution.py:71

commit v5 on v4

--- a/solution.py
+++ b/solution.py
@@ -15,6 +15,7 @@
 LEAVES = 16
 SIZE = 256
 FEATURES = 32
+FLEX = 3
 DELTA_SQUARED = 0.0025
 TWO_PI = 2.0 * math.pi
 SLAB = ("slab_0", "slab_1", "slab_2")
@@ -279,21 +280,16 @@
     return out
 
 
-HEAD_START = (
-    ((85, 80, 81, 70), (0, -14, -15, -6), (0, -12, -18, -6)),
-    ((86, 58, 39, 47), (0, -13, -20, -11), (0, -14, -26, -11)),
-)
-FLEX_STEPS = (22, 43, 65, 83)
+RELEASE = ((0, 10, 20, 25), (0, 14, 27, 35), (0, 11, 22, 24))
+LAST_RELEASE = 80
+BODY_TIME = 22
 
 
 def early_bodies():
     slab, leaf, core, unused, unused = position()
-    ahead = [
-        chosen((slab >> 1) & 3, by_z) + chosen(slab >> 3, by_x) + chosen(leaf, by_y)
-        for by_z, by_x, by_y in HEAD_START
-    ]
-    ahead = jnp.where(core == 0, ahead[0], ahead[1])
-    return sum((ahead >= step).astype(jnp.int32) for step in FLEX_STEPS)
+    places = (slab >> 3, (slab >> 1) & 3, leaf)
+    ahead = LAST_RELEASE + 6 * core - sum(chosen(place, term) for place, term in zip(places, RELEASE))
+    return sum((ahead >= BODY_TIME * (n + 1)).astype(jnp.int32) for n in range(FLEX))
 
 
 def direct(tables, mode, zero, extra, extra_in, mask_ref, t_ref, s_ref, w_ref, *refs):
@@ -550,7 +546,7 @@
         SMALL,
     )(particles)
     own = pair_table("own")
-    flex = own[:112].reshape(4, 28, 3)
+    flex = own[: 28 * FLEX].reshape(FLEX, 28, 3)
     feats = (t0, s0, w0)
     acc, mask = run_direct(
         "direct_early", flex, turned, feats, None, "early", outs=[shaped(17, LEAVES, 1, SIZE)]
@@ -558,7 +554,7 @@
     send_a, send_b, acc = lax.optimization_barrier((send_a, send_b, acc))
     recv_a = swap(send_a, "core")
     recv_b = swap(send_b, "slab")
-    acc = run_direct("direct_own_0", own[None, 112:140], mask, feats, acc)
+    acc = run_direct("direct_own_0", own[None, 84:112], mask, feats, acc)
     m1, f1, send_near, send_far = call(
         pack_slab,
         "pack_slab",
@@ -571,7 +567,7 @@
     recv_near = swap(send_near, "leaf_near")
     built = dict(outs=features_out(LEAVES), scratch=stages(False))
     acc, s1, w1 = run_direct(
-        "direct_own_1", own[None, 140:168], mask, feats, acc, extra=slab_halo, ins=(recv_a, recv_b), **built
+        "direct_own_1", own[None, 112:154], mask, feats, acc, extra=slab_halo, ins=(recv_a, recv_b), **built
     )
     f2, send_far = call(
         pack_near, "pack_near", [V, V, V, A], [shaped(24, 128), shaped(LEAF_ROWS, SIZE)], [], SMALL
@@ -579,7 +575,7 @@
     send_far, acc = lax.optimization_barrier((send_far, acc))
     recv_far = swap(send_far, "leaf_far")
     acc, s2, w2 = run_direct(
-        "direct_own_2", own[None, 168:], mask, feats, acc, extra=near_halo, ins=(recv_near,), **built
+        "direct_own_2", own[None, 154:], mask, feats, acc, extra=near_halo, ins=(recv_near,), **built
     )
     recv_far, acc = lax.optimization_barrier((recv_far, acc))
     blocks = f2 + recv_far[72:96, 0:128]

time: 55.2 us -> 54.3 us (0.984)
  the two profiles are of different devices: /device:TPU:69 before, /device:TPU:102 now
where the time goes in v5:
time: 54.3 us; the launch traced here: 54.2 us
  Pallas kernels  34.7 us (64%)
  starting transfers between devices  15.5 us (29%)
  waiting for transfers between devices  3.09 us (6%)
  local copies, waits for them, and re-layouts  0.81 us (1%)
    pallas_call x10, Pallas kernels, run_direct(): call(functools.partial(direct, tables, mode, zero, extra, len(ins)), name...  32.4 us
    ppermute x8, starting transfers between devices, swap(): return lax.ppermute(value, ALL, SWAPS[name])  15.5 us
    ppermute x8, waiting for transfers between devices, swap(): return lax.ppermute(value, ALL, SWAPS[name])  3.09 us
    pallas_call x1, Pallas kernels, body(): call(finish, 'finish', [V] * 5, shaped(2, SIDE, SIDE, SIZE), far_scratch(...  1.19 us
  transfers between devices with their start and end apart: 8, of which 3 were waited for; matrix products, arithmetic and copies ran while one was open for 0% of the time, Pallas kernels for 59%

profile of v5, /device:TPU:102, one launch (start us, length us, event | category | flops | bytes accessed | tf_op | source)
XLA Modules:
  0.0 54.2 jit_solution(5216728697525452724)
XLA Ops:
  0.0 0.8 %copy-done = f32[3,4,4,256]{3,2,1,0:T(4,128)S(1)} copy-done((f32[3,4,4,256]{3,2,1,0:T(4,128)S(1)}, f32[3,4,4,256]{3,2,1,0:T(4,128)}, u32[]{:S(2)}) %copy-start) | copy-done | bytes 49176
  0.8 0.9 %prepare_own.1 = (bf16[16,32,256]{2,1,0:T(8,128)(2,1)S(1)}, bf16[16,256,32]{2,1,0:T(8,128)(2,1)S(1)}, bf16[16,16,256]{2,1,0:T(8,128)(2,1)S(1)}, f32[24,128]{1,0:...) custom-call(f32[3,4,4,256]{3,2,1,0:T(4,128)S(1)} %copy-done), custom_call_target="tpu_custom_call" | custom-call | flops 4000000 | bytes 1048576 | tf_op jit(solution)/shard_map/prepare_own/pallas_call | solution.py:539
  1.7 0.2 direct_early.1
  1.9 2.0 %collective-permute-start = (f32[72,256]{1,0:T(8,128)S(1)}, f32[72,256]{1,0:T(8,128)S(1)}, u32[]{:S(2)}, u32[]{:S(2)}) collective-permute-start(f32[72,256]{1,0:T(8,128)S(1)} %get-tuple-element.62), channel_id=1, source_target_pairs={{0,4},{1,5},{2,6},{3,7},{4,0},{5,1},{6,2},{7,3},{8,12},{9,13},{10,... | collective-permute-start | bytes 221192 | tf_op jit(solution)/shard_map/ppermute | solution.py:72
  3.9 2.6 %collective-permute-start.1 = (f32[72,256]{1,0:T(8,128)S(1)}, f32[72,256]{1,0:T(8,128)S(1)}, u32[]{:S(2)}, u32[]{:S(2)}) collective-permute-start(f32[72,256]{1,0:T(8,128)S(1)} %get-tuple-element.63), channel_id=1, source_target_pairs={{4,8},{5,9},{6,10},{7,11},{8,4},{9,5},{10,6},{11,7},{12,16},{13,17... | collective-permute-start | bytes 221192 | tf_op jit(solution)/shard_map/ppermute | solution.py:72
  6.5 2.2 %direct_own_0.1.after_ref.refs_0_ = f32[16,16,256]{2,1,0:T(8,128)S(1)} custom-call(f32[17,16,1,256]{3,2,1,0:T(1,128)S(1)} %get-tuple-element.66.mask_ref, bf16[16,32,256]{2,1,0:T(8,128)(2,1)S(1)} %get-tuple-element.58.t_ref, bf16[16,256,32]{2,1,0:T(8,128)(2,1)S(1)} %get-tuple-element.59.s_ref, ...), custom_call_target="tpu_custom_call", output_to_operand_aliasing={{}: (4, {})} | custom-call | flops 11200000000 | bytes 1048576 | tf_op jit(solution)/shard_map/direct_own_0/pallas_call | solution.py:521
  8.7 0.8 %collective-permute-done.1.rb_ref.refs_2_ = f32[72,256]{1,0:T(8,128)S(1)} collective-permute-done((f32[72,256]{1,0:T(8,128)S(1)}, f32[72,256]{1,0:T(8,128)S(1)}, u32[]{:S(2)}, u32[]{:S(2)}) %collective-permute-start.1) | collective-permute-done | bytes 73760 | tf_op jit(solution)/shard_map/ppermute | solution.py:72
  9.6 0.2 pack_slab.1
  9.9 3.5 %direct_own_1.1 = (f32[16,16,256]{2,1,0:T(8,128)S(1)}, bf16[16,256,32]{2,1,0:T(8,128)(2,1)S(1)}, bf16[16,16,256]{2,1,0:T(8,128)(2,1)S(1)}) custom-call(f32[17,16,1,256]{3,2,1,0:T(1,128)S(1)} %get-tuple-element.66.mask_ref, bf16[16,32,256]{2,1,0:T(8,128)(2,1)S(1)} %get-tuple-element.58.t_ref, ...), custom_call_target="tpu_custom_call", output_to_operand_aliasing={{0}: (4, {})} | custom-call | flops 16800000000 | bytes 1048576 | tf_op jit(solution)/shard_map/direct_own_1/pallas_call | solution.py:521
  13.4 1.0 %collective-permute-done.2.r_ref.refs_1_.refs_3_ = f32[96,256]{1,0:T(8,128)S(1)} collective-permute-done((f32[96,256]{1,0:T(8,128)S(1)}, f32[96,256]{1,0:T(8,128)S(1)}, u32[]{:S(2)}, u32[]{:S(2)}) %collective-permute-start.2) | collective-permute-done | bytes 98336 | tf_op jit(solution)/shard_map/ppermute | solution.py:72
  14.4 1.4 %collective-permute-start.3 = (f32[96,256]{1,0:T(8,128)S(1)}, f32[96,256]{1,0:T(8,128)S(1)}, u32[]{:S(2)}, u32[]{:S(2)}) collective-permute-start(f32[96,256]{1,0:T(8,128)S(1)} %get-tuple-element.76), channel_id=1, source_target_pairs={{0,3},{1,2},{2,1},{3,0},{4,7},{5,6},{6,5},{7,4},{8,11},{9,10},{10,... | collective-permute-start | bytes 294920 | tf_op jit(solution)/shard_map/ppermute | solution.py:72
  15.7 3.5 %direct_own_2.1 = (f32[16,16,256]{2,1,0:T(8,128)S(1)}, bf16[16,256,32]{2,1,0:T(8,128)(2,1)S(1)}, bf16[16,16,256]{2,1,0:T(8,128)(2,1)S(1)}) custom-call(f32[17,16,1,256]{3,2,1,0:T(1,128)S(1)} %get-tuple-element.66.mask_ref, bf16[16,32,256]{2,1,0:T(8,128)(2,1)S(1)} %get-tuple-element.58.t_ref, ...), custom_call_target="tpu_custom_call", output_to_operand_aliasing={{0}: (4, {})} | custom-call | flops 16800000000 | bytes 1048576 | tf_op jit(solution)/shard_map/direct_own_2/pallas_call | solution.py:521
  19.2 1.2 %collective-permute-done.3.refs_1_.refs_4_ = f32[96,256]{1,0:T(8,128)S(1)} collective-permute-done((f32[96,256]{1,0:T(8,128)S(1)}, f32[96,256]{1,0:T(8,128)S(1)}, u32[]{:S(2)}, u32[]{:S(2)}) %collective-permute-start.3) | collective-permute-done | bytes 98336 | tf_op jit(solution)/shard_map/ppermute | solution.py:72
  20.5 1.2 %collective-permute-start.4 = (f32[24,128]{1,0:T(8,128)S(1)}, f32[24,128]{1,0:T(8,128)S(1)}, u32[]{:S(2)}, u32[]{:S(2)}) collective-permute-start(f32[24,128]{1,0:T(8,128)S(1)} %slice_add_fusion), channel_id=1, source_target_pairs={{0,8},{1,9},{2,10},{3,11},{4,12},{5,13},{6,14},{7,15},{8,0},{9,1},... | collective-permute-start | bytes 36872 | tf_op jit(solution)/shard_map/ppermute | solution.py:72
  21.6 2.5 %direct_slab_0.1 = (f32[16,16,256]{2,1,0:T(8,128)S(1)}, bf16[16,256,32]{2,1,0:T(8,128)(2,1)S(1)}, bf16[16,16,256]{2,1,0:T(8,128)(2,1)S(1)}) custom-call(f32[17,16,1,256]{3,2,1,0:T(1,128)S(1)} %get-tuple-element.66.mask_ref, bf16[16,32,256]{2,1,0:T(8,128)(2,1)S(1)} %get-tuple-element.58.t_ref, ...), custom_call_target="tpu_custom_call", output_to_operand_aliasing={{0}: (4, {})} | custom-call | flops 11200000000 | bytes 1048576 | tf_op jit(solution)/shard_map/direct_slab_0/pallas_call | solution.py:521
  24.2 4.1 %collective-permute-start.5 = (f32[24,128]{1,0:T(8,128)S(1)}, f32[24,128]{1,0:T(8,128)S(1)}, u32[]{:S(2)}, u32[]{:S(2)}) collective-permute-start(f32[24,128]{1,0:T(8,128)S(1)} %add.13), channel_id=1, source_target_pairs={{0,24},{1,25},{2,26},{3,27},{4,28},{5,29},{6,30},{7,31},{8,16},{9,... | collective-permute-start | bytes 36872 | tf_op jit(solution)/shard_map/ppermute | solution.py:72
  28.4 2.2 %direct_slab_1.1.refs_0_ = f32[16,16,256]{2,1,0:T(8,128)S(1)} custom-call(f32[17,16,1,256]{3,2,1,0:T(1,128)S(1)} %get-tuple-element.66.mask_ref, bf16[16,32,256]{2,1,0:T(8,128)(2,1)S(1)} %get-tuple-element.58.t_ref, bf16[16,256,32]{2,1,0:T(8,128)(2,1)S(1)} %get-tuple-element.82.s_ref, ...), custom_call_target="tpu_custom_call", output_to_operand_aliasing={{}: (4, {})} | custom-call | flops 11200000000 | bytes 1048576 | tf_op jit(solution)/shard_map/direct_slab_1/pallas_call | solution.py:521
  30.6 2.4 %collective-permute-start.6 = (f32[24,128]{1,0:T(8,128)S(1)}, f32[24,128]{1,0:T(8,128)S(1)}, u32[]{:S(2)}, u32[]{:S(2)}) collective-permute-start(f32[24,128]{1,0:T(8,128)S(1)} %add.14), channel_id=1, source_target_pairs={{0,32},{1,33},{2,34},{3,35},{4,36},{5,37},{6,38},{7,39},{8,40},{9,... | collective-permute-start | bytes 36872 | tf_op jit(solution)/shard_map/ppermute | solution.py:72
  33.0 2.2 %direct_slab_2.1.refs_0_ = f32[16,16,256]{2,1,0:T(8,128)S(1)} custom-call(f32[17,16,1,256]{3,2,1,0:T(1,128)S(1)} %get-tuple-element.66.mask_ref, bf16[16,32,256]{2,1,0:T(8,128)(2,1)S(1)} %get-tuple-element.58.t_ref, bf16[16,256,32]{2,1,0:T(8,128)(2,1)S(1)} %get-tuple-element.82.s_ref, ...), custom_call_target="tpu_custom_call", output_to_operand_aliasing={{}: (4, {})} | custom-call | flops 11200000000 | bytes 1048576 | tf_op jit(solution)/shard_map/direct_slab_2/pallas_call | solution.py:521
  35.3 1.6 %collective-permute-start.7 = (f32[24,128]{1,0:T(8,128)S(1)}, f32[24,128]{1,0:T(8,128)S(1)}, u32[]{:S(2)}, u32[]{:S(2)}) collective-permute-start(f32[24,128]{1,0:T(8,128)S(1)} %add.15.f_ref), channel_id=1, source_target_pairs={{0,96},{1,97},{2,98},{3,99},{4,100},{5,101},{6,102},{7,103},{8,104... | collective-permute-start | bytes 36872 | tf_op jit(solution)/shard_map/ppermute | solution.py:72
  36.9 5.0 %direct_leaf_near.1 = (f32[16,16,256]{2,1,0:T(8,128)S(1)}, f32[16,128]{1,0:T(8,128)S(1)}) custom-call(f32[17,16,1,256]{3,2,1,0:T(1,128)S(1)} %get-tuple-element.66.mask_ref, bf16[16,32,256]{2,1,0:T(8,128)(2,1)S(1)} %get-tuple-element.58.t_ref, bf16[16,256,32]{2,1,0:T(8,128)(2,1)S(1)} %get-tuple-element.99.s_ref, ...), custom_call_target="tpu_custom_call", output_to_operand_aliasing={{0}: (4, {})} | custom-call | flops 24000000000 | bytes 1048576 | tf_op jit(solution)/shard_map/direct_leaf_near/pallas_call | solution.py:521
  41.9 4.4 %direct_leaf_far.1.refs_0_ = f32[16,16,256]{2,1,0:T(8,128)S(1)} custom-call(f32[17,16,1,256]{3,2,1,0:T(1,128)S(1)} %get-tuple-element.66.mask_ref, bf16[16,32,256]{2,1,0:T(8,128)(2,1)S(1)} %get-tuple-element.58.t_ref, bf16[16,256,32]{2,1,0:T(8,128)(2,1)S(1)} %get-tuple-element.97.s_ref, ...), custom_call_target="tpu_custom_call", output_to_operand_aliasing={{}: (4, {})} | custom-call | flops 24000000000 | bytes 1048576 | tf_op jit(solution)/shard_map/direct_leaf_far/pallas_call | solution.py:521
  46.3 6.6 %direct_late.1.acc_ref = f32[16,16,256]{2,1,0:T(8,128)S(1)} custom-call(f32[17,16,1,256]{3,2,1,0:T(1,128)S(1)} %get-tuple-element.66.mask_ref, bf16[16,32,256]{2,1,0:T(8,128)(2,1)S(1)} %get-tuple-element.58.t_ref, bf16[16,256,32]{2,1,0:T(8,128)(2,1)S(1)} %get-tuple-element.59.s_ref, ...), custom_call_target="tpu_custom_call", output_to_operand_aliasing={{}: (4, {})} | custom-call | flops 11200000000 | bytes 1048576 | tf_op jit(solution)/shard_map/direct_late/pallas_call | solution.py:521
  53.0 1.2 %finish.1 = f32[2,4,4,256]{3,2,1,0:T(4,128)} custom-call(f32[3,4,4,256]{3,2,1,0:T(4,128)S(1)} %copy-done.1, f32[16,16,256]{2,1,0:T(8,128)S(1)} %direct_late.1.acc_ref, f32[16,128]{1,0:T(8,128)S(1)} %get-tuple-element.105.near_ref, f32[24,128]{1,0:T(8,128)S(1)} %add.15.f_ref, f32[24,128]{1,0:T(8,128)S(1)} %collective-permute-done.7.got_ref), custom_call_target="tpu_custom_call" | custom-call | flops 4000000 | bytes 1048576 | tf_op jit(solution)/shard_map/finish/pallas_call | solution.py:615
  (16 shorter events, 0.2 us)
Async XLA Ops:
  0.0 0.8 %copy-start = (f32[3,4,4,256]{3,2,1,0:T(4,128)S(1)}, f32[3,4,4,256]{3,2,1,0:T(4,128)}, u32[]{:S(2)}) copy-start(f32[3,4,4,256]{3,2,1,0:T(4,128)} %part_ref.5) | copy-start | bytes 147460
  0.8 0.9 %copy-start.2 = (s32[16,4,4]{0,2,1:T(4,128)S(1)}, s32[16,4,4]{0,2,1:T(4,128)}, u32[]{:S(2)}) copy-start(s32[16,4,4]{0,2,1:T(4,128)} %param.3) | copy-start | bytes 3076
  1.9 6.8 %collective-permute-start = (f32[72,256]{1,0:T(8,128)S(1)}, f32[72,256]{1,0:T(8,128)S(1)}, u32[]{:S(2)}, u32[]{:S(2)}) collective-permute-start(f32[72,256]{1,0:T(8,128)S(1)} %get-tuple-element.62), channel_id=1, source_target_pairs={{0,4},{1,5},{2,6},{3,7},{4,0},{5,1},{6,2},{7,3},{8,12},{9,13},{10,... | collective-permute-start | bytes 221192 | tf_op jit(solution)/shard_map/ppermute | solution.py:72
  3.9 5.7 %collective-permute-start.1 = (f32[72,256]{1,0:T(8,128)S(1)}, f32[72,256]{1,0:T(8,128)S(1)}, u32[]{:S(2)}, u32[]{:S(2)}) collective-permute-start(f32[72,256]{1,0:T(8,128)S(1)} %get-tuple-element.63), channel_id=1, source_target_pairs={{4,8},{5,9},{6,10},{7,11},{8,4},{9,5},{10,6},{11,7},{12,16},{13,17... | collective-permute-start | bytes 221192 | tf_op jit(solution)/shard_map/ppermute | solution.py:72
  6.5 3.1 %copy-start.1 = (f32[3,4,4,256]{3,2,1,0:T(4,128)S(1)}, f32[3,4,4,256]{3,2,1,0:T(4,128)}, u32[]{:S(2)}) copy-start(f32[3,4,4,256]{3,2,1,0:T(4,128)} %part_ref.5) | copy-start | bytes 147460
  9.7 4.6 %collective-permute-start.2 = (f32[96,256]{1,0:T(8,128)S(1)}, f32[96,256]{1,0:T(8,128)S(1)}, u32[]{:S(2)}, u32[]{:S(2)}) collective-permute-start(f32[96,256]{1,0:T(8,128)S(1)} %get-tuple-element.69), channel_id=1, source_target_pairs={{0,1},{1,0},{2,3},{3,2},{4,5},{5,4},{6,7},{7,6},{8,9},{9,8},{10,11... | collective-permute-start | bytes 294920 | tf_op jit(solution)/shard_map/ppermute | solution.py:72
  14.4 6.1 %collective-permute-start.3 = (f32[96,256]{1,0:T(8,128)S(1)}, f32[96,256]{1,0:T(8,128)S(1)}, u32[]{:S(2)}, u32[]{:S(2)}) collective-permute-start(f32[96,256]{1,0:T(8,128)S(1)} %get-tuple-element.76), channel_id=1, source_target_pairs={{0,3},{1,2},{2,1},{3,0},{4,7},{5,6},{6,5},{7,4},{8,11},{9,10},{10,... | collective-permute-start | bytes 294920 | tf_op jit(solution)/shard_map/ppermute | solution.py:72
  20.5 3.7 %collective-permute-start.4 = (f32[24,128]{1,0:T(8,128)S(1)}, f32[24,128]{1,0:T(8,128)S(1)}, u32[]{:S(2)}, u32[]{:S(2)}) collective-permute-start(f32[24,128]{1,0:T(8,128)S(1)} %slice_add_fusion), channel_id=1, source_target_pairs={{0,8},{1,9},{2,10},{3,11},{4,12},{5,13},{6,14},{7,15},{8,0},{9,1},... | collective-permute-start | bytes 36872 | tf_op jit(solution)/shard_map/ppermute | solution.py:72
  24.2 6.3 %collective-permute-start.5 = (f32[24,128]{1,0:T(8,128)S(1)}, f32[24,128]{1,0:T(8,128)S(1)}, u32[]{:S(2)}, u32[]{:S(2)}) collective-permute-start(f32[24,128]{1,0:T(8,128)S(1)} %add.13), channel_id=1, source_target_pairs={{0,24},{1,25},{2,26},{3,27},{4,28},{5,29},{6,30},{7,31},{8,16},{9,... | collective-permute-start | bytes 36872 | tf_op jit(solution)/shard_map/ppermute | solution.py:72
  30.6 4.7 %collective-permute-start.6 = (f32[24,128]{1,0:T(8,128)S(1)}, f32[24,128]{1,0:T(8,128)S(1)}, u32[]{:S(2)}, u32[]{:S(2)}) collective-permute-start(f32[24,128]{1,0:T(8,128)S(1)} %add.14), channel_id=1, source_target_pairs={{0,32},{1,33},{2,34},{3,35},{4,36},{5,37},{6,38},{7,39},{8,40},{9,... | collective-permute-start | bytes 36872 | tf_op jit(solution)/shard_map/ppermute | solution.py:72
  35.3 17.7 %collective-permute-start.7 = (f32[24,128]{1,0:T(8,128)S(1)}, f32[24,128]{1,0:T(8,128)S(1)}, u32[]{:S(2)}, u32[]{:S(2)}) collective-permute-start(f32[24,128]{1,0:T(8,128)S(1)} %add.15.f_ref), channel_id=1, source_target_pairs={{0,96},{1,97},{2,98},{3,99},{4,100},{5,101},{6,102},{7,103},{8,104... | collective-permute-start | bytes 36872 | tf_op jit(solution)/shard_map/ppermute | solution.py:72

commit v6 on v5

--- a/solution.py
+++ b/solution.py
@@ -15,7 +15,7 @@
 LEAVES = 16
 SIZE = 256
 FEATURES = 32
-FLEX = 3
+FLEX = 2
 DELTA_SQUARED = 0.0025
 TWO_PI = 2.0 * math.pi
 SLAB = ("slab_0", "slab_1", "slab_2")
@@ -61,10 +61,10 @@
     "slab": exchange_pairs(slab_between_chips),
     "leaf_near": exchange_pairs(lambda x, z, c, y: (x, z, c, near_side(y))),
     "leaf_far": exchange_pairs(lambda x, z, c, y: (x, z, c, far_side(y))),
-    "z_near": exchange_pairs(lambda x, z, c, y: (x, near_side(z), c, y)),
-    "z_far": exchange_pairs(lambda x, z, c, y: (x, far_side(z), c, y)),
-    "x_near": exchange_pairs(lambda x, z, c, y: (near_side(x), z, c, y)),
-    "x_far": exchange_pairs(lambda x, z, c, y: (far_side(x), z, c, y)),
+    "z_near": exchange_pairs(lambda x, z, c, y: (x, near_side(z), c, y) if c == 1 else None),
+    "z_far": exchange_pairs(lambda x, z, c, y: (x, far_side(z), c, y) if c == 1 else None),
+    "x_near": exchange_pairs(lambda x, z, c, y: (near_side(x), z, c, y) if c == 1 else None),
+    "x_far": exchange_pairs(lambda x, z, c, y: (far_side(x), z, c, y) if c == 1 else None),
 }
 
 
@@ -280,16 +280,16 @@
     return out
 
 
-RELEASE = ((0, 10, 20, 25), (0, 14, 27, 35), (0, 11, 22, 24))
-LAST_RELEASE = 80
-BODY_TIME = 22
+RELEASE = ((0, 8, 15, 12), (0, 18, 30, 30), (0, 8, 15, 12))
+FIRST_STEPS = (18, 40)
+LAST_RELEASE = 60
 
 
 def early_bodies():
-    slab, leaf, core, unused, unused = position()
+    slab, leaf = position()[:2]
     places = (slab >> 3, (slab >> 1) & 3, leaf)
-    ahead = LAST_RELEASE + 6 * core - sum(chosen(place, term) for place, term in zip(places, RELEASE))
-    return sum((ahead >= BODY_TIME * (n + 1)).astype(jnp.int32) for n in range(FLEX))
+    ahead = LAST_RELEASE - sum(chosen(place, term) for place, term in zip(places, RELEASE))
+    return sum((ahead >= step).astype(jnp.int32) for step in FIRST_STEPS)
 
 
 def direct(tables, mode, zero, extra, extra_in, mask_ref, t_ref, s_ref, w_ref, *refs):
@@ -451,7 +451,7 @@
     tx = jnp.where(remote, (bx * SIDE - ti).astype(F32) + 1.5, 1.0)
     ty = jnp.where(remote, (by * SIDE - tj).astype(F32) + 1.5, 1.0)
     weight = jnp.where(remote, 1.0, 0.0).astype(F32)
-    a_ref[...] = (f_ref[...] + got_ref[...]) * source_scale()
+    a_ref[...] = jnp.where(info[2] == 1, f_ref[...], got_ref[...]) * source_scale()
     translate([(tx, ty, weight)], h_ref, a_ref, l_ref)
     local = l_ref[...] + near_ref[...]
     wx = own_rows(part_ref, 0)
@@ -554,7 +554,7 @@
     send_a, send_b, acc = lax.optimization_barrier((send_a, send_b, acc))
     recv_a = swap(send_a, "core")
     recv_b = swap(send_b, "slab")
-    acc = run_direct("direct_own_0", own[None, 84:112], mask, feats, acc)
+    acc = run_direct("direct_own_0", own[None, 56:98], mask, feats, acc)
     m1, f1, send_near, send_far = call(
         pack_slab,
         "pack_slab",
@@ -567,7 +567,7 @@
     recv_near = swap(send_near, "leaf_near")
     built = dict(outs=features_out(LEAVES), scratch=stages(False))
     acc, s1, w1 = run_direct(
-        "direct_own_1", own[None, 112:154], mask, feats, acc, extra=slab_halo, ins=(recv_a, recv_b), **built
+        "direct_own_1", own[None, 98:147], mask, feats, acc, extra=slab_halo, ins=(recv_a, recv_b), **built
     )
     f2, send_far = call(
         pack_near, "pack_near", [V, V, V, A], [shaped(24, 128), shaped(LEAF_ROWS, SIZE)], [], SMALL
@@ -575,28 +575,27 @@
     send_far, acc = lax.optimization_barrier((send_far, acc))
     recv_far = swap(send_far, "leaf_far")
     acc, s2, w2 = run_direct(
-        "direct_own_2", own[None, 154:], mask, feats, acc, extra=near_halo, ins=(recv_near,), **built
+        "direct_own_2", own[None, 147:], mask, feats, acc, extra=near_halo, ins=(recv_near,), **built
     )
     recv_far, acc = lax.optimization_barrier((recv_far, acc))
     blocks = f2 + recv_far[72:96, 0:128]
-    slab_pairs = pair_table("slab").reshape(3, 1, 28, 3)
-    for number, axis in enumerate(("z_near", "z_far", "x_near")):
-        blocks, acc = lax.optimization_barrier((blocks, acc))
-        got = swap(blocks, axis)
-        name = f"direct_slab_{number}"
-        slab_feats = (t0, s1, w1)
-        if number == 0:
-            acc, s3, w3 = run_direct(
-                name, slab_pairs[number], mask, slab_feats, acc, extra=far_halo, ins=(recv_far,), **built
-            )
-        else:
-            acc = run_direct(name, slab_pairs[number], mask, slab_feats, acc)
-        got, acc = lax.optimization_barrier((got, acc))
-        blocks = blocks + got
-    blocks, acc = lax.optimization_barrier((blocks, acc))
-    got = swap(blocks, "x_far")
+    slab_pairs = pair_table("slab").reshape(2, 1, 42, 3)
     right = pair_table("leaf", True)
     left = pair_table("leaf", False)
+    far_pairs = np.stack([left, right])
+    slab_feats = (t0, s1, w1)
+    blocks, acc = lax.optimization_barrier((blocks, acc))
+    got = swap(blocks, "z_near")
+    acc, s3, w3 = run_direct(
+        "direct_slab_0", slab_pairs[0], mask, slab_feats, acc, extra=far_halo, ins=(recv_far,), **built
+    )
+    got, acc = lax.optimization_barrier((got, acc))
+    blocks, acc = lax.optimization_barrier((blocks + got, acc))
+    got = swap(blocks, "z_far")
+    acc = run_direct("direct_slab_1", slab_pairs[1], mask, slab_feats, acc)
+    got, acc = lax.optimization_barrier((got, acc))
+    blocks, acc = lax.optimization_barrier((blocks + got, acc))
+    got = swap(blocks, "x_near")
     acc, local = run_direct(
         "direct_leaf_near",
         np.stack([right, left]),
@@ -609,7 +608,14 @@
         outs=[shaped(LEAVES, 128)],
         scratch=far_scratch(256),
     )
-    acc = run_direct("direct_leaf_far", np.stack([left, right]), mask, (t0, s3, w3), acc, "side")
+    got, acc = lax.optimization_barrier((got, acc))
+    blocks, acc = lax.optimization_barrier((blocks + got, acc))
+    got = swap(blocks, "x_far")
+    acc = run_direct("direct_leaf_far_0", far_pairs[:, :30], mask, (t0, s3, w3), acc, "side")
+    got, acc = lax.optimization_barrier((got, acc))
+    blocks, acc = lax.optimization_barrier((blocks + got, acc))
+    got = swap(blocks, "core")
+    acc = run_direct("direct_leaf_far_1", far_pairs[:, 30:], mask, (t0, s3, w3), acc, "side")
     acc = run_direct("direct_late", flex, mask, feats, acc, "late")
     got, acc = lax.optimization_barrier((got, acc))
     return call(

time: 54.3 us -> 56.7 us (1.044)
  the two profiles are of different devices: /device:TPU:102 before, /device:TPU:1 now
where the time goes in v6:
time: 56.7 us; the launch traced here: 56.5 us
  Pallas kernels  34.7 us (61%)
  starting transfers between devices  19.9 us (35%)
  waiting for transfers between devices  0.88 us (2%)
  local copies, waits for them, and re-layouts  0.81 us (1%)
    pallas_call x10, Pallas kernels, run_direct(): call(functools.partial(direct, tables, mode, zero, extra, len(ins)), name...  32.4 us
    ppermute x9, starting transfers between devices, swap(): return lax.ppermute(value, ALL, SWAPS[name])  19.9 us
    pallas_call x1, Pallas kernels, body(): call(finish, 'finish', [V] * 5, shaped(2, SIDE, SIDE, SIZE), far_scratch(...  1.18 us
  transfers between devices with their start and end apart: 9, of which 1 were waited for; matrix products, arithmetic and copies ran while one was open for 0% of the time, Pallas kernels for 45%

profile of v6, /device:TPU:1, one launch (start us, length us, event | category | flops | bytes accessed | tf_op | source)
XLA Modules:
  0.0 56.5 jit_solution(3733368107861134636)
XLA Ops:
  0.0 0.8 %copy-done = f32[3,4,4,256]{3,2,1,0:T(4,128)S(1)} copy-done((f32[3,4,4,256]{3,2,1,0:T(4,128)S(1)}, f32[3,4,4,256]{3,2,1,0:T(4,128)}, u32[]{:S(2)}) %copy-start) | copy-done | bytes 49176
  0.8 0.9 %prepare_own.1 = (bf16[16,32,256]{2,1,0:T(8,128)(2,1)S(1)}, bf16[16,256,32]{2,1,0:T(8,128)(2,1)S(1)}, bf16[16,16,256]{2,1,0:T(8,128)(2,1)S(1)}, f32[24,128]{1,0:...) custom-call(f32[3,4,4,256]{3,2,1,0:T(4,128)S(1)} %copy-done), custom_call_target="tpu_custom_call" | custom-call | flops 4000000 | bytes 1048576 | tf_op jit(solution)/shard_map/prepare_own/pallas_call | solution.py:539
  1.7 4.5 %direct_early.1 = (f32[16,16,256]{2,1,0:T(8,128)S(1)}, f32[17,16,1,256]{3,2,1,0:T(1,128)S(1)}) custom-call(s32[4,4,16]{2,1,0:T(4,128)S(1)} %bitcast.1, bf16[16,32,256]{2,1,0:T(8,128)(2,1)S(1)} %get-tuple-element.62.t_ref, bf16[16,256,32]{2,1,0:T(8,128)(2,1)S(1)} %get-tuple-element.63.s_ref, bf16[16,16,256]{2,1,0:T(8,128)(2,1)S(1)} %get-tuple-element.64.w_ref), custom_call_target="tpu_custom_call" | custom-call | flops 11200000000 | bytes 1048576 | tf_op jit(solution)/shard_map/direct_early/pallas_call | solution.py:521
  6.2 1.4 %collective-permute-start = (f32[72,256]{1,0:T(8,128)S(1)}, f32[72,256]{1,0:T(8,128)S(1)}, u32[]{:S(2)}, u32[]{:S(2)}) collective-permute-start(f32[72,256]{1,0:T(8,128)S(1)} %get-tuple-element.66), channel_id=1, source_target_pairs={{0,4},{1,5},{2,6},{3,7},{4,0},{5,1},{6,2},{7,3},{8,12},{9,13},{10,... | collective-permute-start | bytes 221192 | tf_op jit(solution)/shard_map/ppermute | solution.py:72
  7.6 3.5 %collective-permute-start.1 = (f32[72,256]{1,0:T(8,128)S(1)}, f32[72,256]{1,0:T(8,128)S(1)}, u32[]{:S(2)}, u32[]{:S(2)}) collective-permute-start(f32[72,256]{1,0:T(8,128)S(1)} %get-tuple-element.67), channel_id=1, source_target_pairs={{4,8},{5,9},{6,10},{7,11},{8,4},{9,5},{10,6},{11,7},{12,16},{13,17... | collective-permute-start | bytes 221192 | tf_op jit(solution)/shard_map/ppermute | solution.py:72
  11.2 3.2 %direct_own_0.1.after_ref.refs_0_ = f32[16,16,256]{2,1,0:T(8,128)S(1)} custom-call(f32[17,16,1,256]{3,2,1,0:T(1,128)S(1)} %get-tuple-element.70.mask_ref, bf16[16,32,256]{2,1,0:T(8,128)(2,1)S(1)} %get-tuple-element.62.t_ref, bf16[16,256,32]{2,1,0:T(8,128)(2,1)S(1)} %get-tuple-element.63.s_ref, ...), custom_call_target="tpu_custom_call", output_to_operand_aliasing={{}: (4, {})} | custom-call | flops 16800000000 | bytes 1048576 | tf_op jit(solution)/shard_map/direct_own_0/pallas_call | solution.py:521
  14.4 0.0 collective-permute-done.1.rb_ref.refs_2_
  14.4 0.2 pack_slab.1
  14.6 0.3 collective-permute-start.2
  14.9 4.0 %direct_own_1.1 = (f32[16,16,256]{2,1,0:T(8,128)S(1)}, bf16[16,256,32]{2,1,0:T(8,128)(2,1)S(1)}, bf16[16,16,256]{2,1,0:T(8,128)(2,1)S(1)}) custom-call(f32[17,16,1,256]{3,2,1,0:T(1,128)S(1)} %get-tuple-element.70.mask_ref, bf16[16,32,256]{2,1,0:T(8,128)(2,1)S(1)} %get-tuple-element.62.t_ref, ...), custom_call_target="tpu_custom_call", output_to_operand_aliasing={{0}: (4, {})} | custom-call | flops 19599998976 | bytes 1048576 | tf_op jit(solution)/shard_map/direct_own_1/pallas_call | solution.py:521
  18.9 2.2 %collective-permute-start.3 = (f32[96,256]{1,0:T(8,128)S(1)}, f32[96,256]{1,0:T(8,128)S(1)}, u32[]{:S(2)}, u32[]{:S(2)}) collective-permute-start(f32[96,256]{1,0:T(8,128)S(1)} %get-tuple-element.80), channel_id=1, source_target_pairs={{0,3},{1,2},{2,1},{3,0},{4,7},{5,6},{6,5},{7,4},{8,11},{9,10},{10,... | collective-permute-start | bytes 294920 | tf_op jit(solution)/shard_map/ppermute | solution.py:72
  21.1 4.0 %direct_own_2.1 = (f32[16,16,256]{2,1,0:T(8,128)S(1)}, bf16[16,256,32]{2,1,0:T(8,128)(2,1)S(1)}, bf16[16,16,256]{2,1,0:T(8,128)(2,1)S(1)}) custom-call(f32[17,16,1,256]{3,2,1,0:T(1,128)S(1)} %get-tuple-element.70.mask_ref, bf16[16,32,256]{2,1,0:T(8,128)(2,1)S(1)} %get-tuple-element.62.t_ref, ...), custom_call_target="tpu_custom_call", output_to_operand_aliasing={{0}: (4, {})} | custom-call | flops 19599998976 | bytes 1048576 | tf_op jit(solution)/shard_map/direct_own_2/pallas_call | solution.py:521
  25.1 1.9 %collective-permute-start.4 = (f32[24,128]{1,0:T(8,128)S(1)}, f32[24,128]{1,0:T(8,128)S(1)}, u32[]{:S(2)}, u32[]{:S(2)}) collective-permute-start(f32[24,128]{1,0:T(8,128)S(1)} %slice_add_fusion), channel_id=1, source_target_pairs={{4,12},{5,13},{6,14},{7,15},{12,4},{13,5},{14,6},{15,7},{20,28},{2... | collective-permute-start | bytes 36872 | tf_op jit(solution)/shard_map/ppermute | solution.py:72
  27.0 3.5 %direct_slab_0.1 = (f32[16,16,256]{2,1,0:T(8,128)S(1)}, bf16[16,256,32]{2,1,0:T(8,128)(2,1)S(1)}, bf16[16,16,256]{2,1,0:T(8,128)(2,1)S(1)}) custom-call(f32[17,16,1,256]{3,2,1,0:T(1,128)S(1)} %get-tuple-element.70.mask_ref, bf16[16,32,256]{2,1,0:T(8,128)(2,1)S(1)} %get-tuple-element.62.t_ref, ...), custom_call_target="tpu_custom_call", output_to_operand_aliasing={{0}: (4, {})} | custom-call | flops 16800000000 | bytes 1048576 | tf_op jit(solution)/shard_map/direct_slab_0/pallas_call | solution.py:521
  30.5 5.1 %collective-permute-start.5 = (f32[24,128]{1,0:T(8,128)S(1)}, f32[24,128]{1,0:T(8,128)S(1)}, u32[]{:S(2)}, u32[]{:S(2)}) collective-permute-start(f32[24,128]{1,0:T(8,128)S(1)} %add.16), channel_id=1, source_target_pairs={{4,28},{5,29},{6,30},{7,31},{12,20},{13,21},{14,22},{15,23},{20,12... | collective-permute-start | bytes 36872 | tf_op jit(solution)/shard_map/ppermute | solution.py:72
  35.7 3.2 %direct_slab_1.1.refs_0_ = f32[16,16,256]{2,1,0:T(8,128)S(1)} custom-call(f32[17,16,1,256]{3,2,1,0:T(1,128)S(1)} %get-tuple-element.70.mask_ref, bf16[16,32,256]{2,1,0:T(8,128)(2,1)S(1)} %get-tuple-element.62.t_ref, bf16[16,256,32]{2,1,0:T(8,128)(2,1)S(1)} %get-tuple-element.86.s_ref, ...), custom_call_target="tpu_custom_call", output_to_operand_aliasing={{}: (4, {})} | custom-call | flops 16800000000 | bytes 1048576 | tf_op jit(solution)/shard_map/direct_slab_1/pallas_call | solution.py:521
  38.9 2.1 %collective-permute-start.6 = (f32[24,128]{1,0:T(8,128)S(1)}, f32[24,128]{1,0:T(8,128)S(1)}, u32[]{:S(2)}, u32[]{:S(2)}) collective-permute-start(f32[24,128]{1,0:T(8,128)S(1)} %add.17), channel_id=1, source_target_pairs={{4,36},{5,37},{6,38},{7,39},{12,44},{13,45},{14,46},{15,47},{20,52... | collective-permute-start | bytes 36872 | tf_op jit(solution)/shard_map/ppermute | solution.py:72
  41.0 5.0 %direct_leaf_near.1 = (f32[16,16,256]{2,1,0:T(8,128)S(1)}, f32[16,128]{1,0:T(8,128)S(1)}) custom-call(f32[17,16,1,256]{3,2,1,0:T(1,128)S(1)} %get-tuple-element.70.mask_ref, bf16[16,32,256]{2,1,0:T(8,128)(2,1)S(1)} %get-tuple-element.62.t_ref, bf16[16,256,32]{2,1,0:T(8,128)(2,1)S(1)} %get-tuple-element.97.s_ref, ...), custom_call_target="tpu_custom_call", output_to_operand_aliasing={{0}: (4, {})} | custom-call | flops 24000000000 | bytes 1048576 | tf_op jit(solution)/shard_map/direct_leaf_near/pallas_call | solution.py:521
  46.1 3.3 %collective-permute-start.7 = (f32[24,128]{1,0:T(8,128)S(1)}, f32[24,128]{1,0:T(8,128)S(1)}, u32[]{:S(2)}, u32[]{:S(2)}) collective-permute-start(f32[24,128]{1,0:T(8,128)S(1)} %add.18), channel_id=1, source_target_pairs={{4,100},{5,101},{6,102},{7,103},{12,108},{13,109},{14,110},{15,111... | collective-permute-start | bytes 36872 | tf_op jit(solution)/shard_map/ppermute | solution.py:72
  49.3 2.4 %direct_leaf_far_0.1.refs_0_ = f32[16,16,256]{2,1,0:T(8,128)S(1)} custom-call(f32[17,16,1,256]{3,2,1,0:T(1,128)S(1)} %get-tuple-element.70.mask_ref, bf16[16,32,256]{2,1,0:T(8,128)(2,1)S(1)} %get-tuple-element.62.t_ref, bf16[16,256,32]{2,1,0:T(8,128)(2,1)S(1)} %get-tuple-element.105.s_ref, ...), custom_call_target="tpu_custom_call", output_to_operand_aliasing={{}: (4, {})} | custom-call | flops 12000000000 | bytes 1048576 | tf_op jit(solution)/shard_map/direct_leaf_far_0/pallas_call | solution.py:521
  51.7 2.4 %direct_leaf_far_1.1.refs_0_ = f32[16,16,256]{2,1,0:T(8,128)S(1)} custom-call(f32[17,16,1,256]{3,2,1,0:T(1,128)S(1)} %get-tuple-element.70.mask_ref, bf16[16,32,256]{2,1,0:T(8,128)(2,1)S(1)} %get-tuple-element.62.t_ref, bf16[16,256,32]{2,1,0:T(8,128)(2,1)S(1)} %get-tuple-element.105.s_ref, ...), custom_call_target="tpu_custom_call", output_to_operand_aliasing={{}: (4, {})} | custom-call | flops 12000000000 | bytes 1048576 | tf_op jit(solution)/shard_map/direct_leaf_far_1/pallas_call | solution.py:521
  54.1 0.3 direct_late.1.acc_ref
  54.4 0.8 %collective-permute-done.8.got_ref = f32[24,128]{1,0:T(8,128)S(1)} collective-permute-done((f32[24,128]{1,0:T(8,128)S(1)}, f32[24,128]{1,0:T(8,128)S(1)}, u32[]{:S(2)}, u32[]{:S(2)}) %collective-permute-start.8) | collective-permute-done | bytes 12320 | tf_op jit(solution)/shard_map/ppermute | solution.py:72
  55.3 1.2 %finish.1 = f32[2,4,4,256]{3,2,1,0:T(4,128)} custom-call(f32[3,4,4,256]{3,2,1,0:T(4,128)S(1)} %copy-done.1, f32[16,16,256]{2,1,0:T(8,128)S(1)} %direct_late.1.acc_ref, f32[16,128]{1,0:T(8,128)S(1)} %get-tuple-element.113.near_ref, f32[24,128]{1,0:T(8,128)S(1)} %add.19.f_ref, f32[24,128]{1,0:T(8,128)S(1)} %collective-permute-done.8.got_ref), custom_call_target="tpu_custom_call" | custom-call | flops 4000000 | bytes 1048576 | tf_op jit(solution)/shard_map/finish/pallas_call | solution.py:621
  (19 shorter events, 0.1 us)
Async XLA Ops:
  0.0 0.8 %copy-start = (f32[3,4,4,256]{3,2,1,0:T(4,128)S(1)}, f32[3,4,4,256]{3,2,1,0:T(4,128)}, u32[]{:S(2)}) copy-start(f32[3,4,4,256]{3,2,1,0:T(4,128)} %part_ref.5) | copy-start | bytes 147460
  0.8 0.9 %copy-start.2 = (s32[16,4,4]{0,2,1:T(4,128)S(1)}, s32[16,4,4]{0,2,1:T(4,128)}, u32[]{:S(2)}) copy-start(s32[16,4,4]{0,2,1:T(4,128)} %param.3) | copy-start | bytes 3076
  6.2 8.1 %collective-permute-start = (f32[72,256]{1,0:T(8,128)S(1)}, f32[72,256]{1,0:T(8,128)S(1)}, u32[]{:S(2)}, u32[]{:S(2)}) collective-permute-start(f32[72,256]{1,0:T(8,128)S(1)} %get-tuple-element.66), channel_id=1, source_target_pairs={{0,4},{1,5},{2,6},{3,7},{4,0},{5,1},{6,2},{7,3},{8,12},{9,13},{10,... | collective-permute-start | bytes 221192 | tf_op jit(solution)/shard_map/ppermute | solution.py:72
  7.6 6.7 %collective-permute-start.1 = (f32[72,256]{1,0:T(8,128)S(1)}, f32[72,256]{1,0:T(8,128)S(1)}, u32[]{:S(2)}, u32[]{:S(2)}) collective-permute-start(f32[72,256]{1,0:T(8,128)S(1)} %get-tuple-element.67), channel_id=1, source_target_pairs={{4,8},{5,9},{6,10},{7,11},{8,4},{9,5},{10,6},{11,7},{12,16},{13,17... | collective-permute-start | bytes 221192 | tf_op jit(solution)/shard_map/ppermute | solution.py:72
  11.2 3.2 %copy-start.1 = (f32[3,4,4,256]{3,2,1,0:T(4,128)S(1)}, f32[3,4,4,256]{3,2,1,0:T(4,128)}, u32[]{:S(2)}) copy-start(f32[3,4,4,256]{3,2,1,0:T(4,128)} %part_ref.5) | copy-start | bytes 147460
  14.6 4.3 %collective-permute-start.2 = (f32[96,256]{1,0:T(8,128)S(1)}, f32[96,256]{1,0:T(8,128)S(1)}, u32[]{:S(2)}, u32[]{:S(2)}) collective-permute-start(f32[96,256]{1,0:T(8,128)S(1)} %get-tuple-element.73), channel_id=1, source_target_pairs={{0,1},{1,0},{2,3},{3,2},{4,5},{5,4},{6,7},{7,6},{8,9},{9,8},{10,11... | collective-permute-start | bytes 294920 | tf_op jit(solution)/shard_map/ppermute | solution.py:72
  18.9 6.1 %collective-permute-start.3 = (f32[96,256]{1,0:T(8,128)S(1)}, f32[96,256]{1,0:T(8,128)S(1)}, u32[]{:S(2)}, u32[]{:S(2)}) collective-permute-start(f32[96,256]{1,0:T(8,128)S(1)} %get-tuple-element.80), channel_id=1, source_target_pairs={{0,3},{1,2},{2,1},{3,0},{4,7},{5,6},{6,5},{7,4},{8,11},{9,10},{10,... | collective-permute-start | bytes 294920 | tf_op jit(solution)/shard_map/ppermute | solution.py:72
  25.1 5.4 %collective-permute-start.4 = (f32[24,128]{1,0:T(8,128)S(1)}, f32[24,128]{1,0:T(8,128)S(1)}, u32[]{:S(2)}, u32[]{:S(2)}) collective-permute-start(f32[24,128]{1,0:T(8,128)S(1)} %slice_add_fusion), channel_id=1, source_target_pairs={{4,12},{5,13},{6,14},{7,15},{12,4},{13,5},{14,6},{15,7},{20,28},{2... | collective-permute-start | bytes 36872 | tf_op jit(solution)/shard_map/ppermute | solution.py:72
  30.5 8.3 %collective-permute-start.5 = (f32[24,128]{1,0:T(8,128)S(1)}, f32[24,128]{1,0:T(8,128)S(1)}, u32[]{:S(2)}, u32[]{:S(2)}) collective-permute-start(f32[24,128]{1,0:T(8,128)S(1)} %add.16), channel_id=1, source_target_pairs={{4,28},{5,29},{6,30},{7,31},{12,20},{13,21},{14,22},{15,23},{20,12... | collective-permute-start | bytes 36872 | tf_op jit(solution)/shard_map/ppermute | solution.py:72
  38.9 7.2 %collective-permute-start.6 = (f32[24,128]{1,0:T(8,128)S(1)}, f32[24,128]{1,0:T(8,128)S(1)}, u32[]{:S(2)}, u32[]{:S(2)}) collective-permute-start(f32[24,128]{1,0:T(8,128)S(1)} %add.17), channel_id=1, source_target_pairs={{4,36},{5,37},{6,38},{7,39},{12,44},{13,45},{14,46},{15,47},{20,52... | collective-permute-start | bytes 36872 | tf_op jit(solution)/shard_map/ppermute | solution.py:72
  46.1 5.6 %collective-permute-start.7 = (f32[24,128]{1,0:T(8,128)S(1)}, f32[24,128]{1,0:T(8,128)S(1)}, u32[]{:S(2)}, u32[]{:S(2)}) collective-permute-start(f32[24,128]{1,0:T(8,128)S(1)} %add.18), channel_id=1, source_target_pairs={{4,100},{5,101},{6,102},{7,103},{12,108},{13,109},{14,110},{15,111... | collective-permute-start | bytes 36872 | tf_op jit(solution)/shard_map/ppermute | solution.py:72
  54.1 1.2 %collective-permute-start.8 = (f32[24,128]{1,0:T(8,128)S(1)}, f32[24,128]{1,0:T(8,128)S(1)}, u32[]{:S(2)}, u32[]{:S(2)}) collective-permute-start(f32[24,128]{1,0:T(8,128)S(1)} %add.19.f_ref), channel_id=1, source_target_pairs={{0,4},{1,5},{2,6},{3,7},{4,0},{5,1},{6,2},{7,3},{8,12},{9,13},{10,... | collective-permute-start | bytes 36872 | tf_op jit(solution)/shard_map/ppermute | solution.py:72

commit v7 on v3

--- a/solution.py
+++ b/solution.py
@@ -39,11 +39,13 @@
     return pairs
 
 
+def inner_slab(slab):
+    return jnp.logical_and(slab > 0, slab < 31).astype(F32)
+
+
 def slab_between_chips(x, z, c, y):
     slab = (x * 4 + z) * 2 + c
-    other = slab + 1 if c == 1 else slab - 1
-    if not 0 <= other < 32:
-        return None
+    other = (slab + 1 if c == 1 else slab - 1) % 32
     return (other // 8, (other // 2) % 4, other % 2, y)
 
 
@@ -199,9 +201,12 @@
     info = position()
     even = info[2] == 0
     leaf_even = info[3] == 0
+    inner = inner_slab(info[0])
     for c in range(3):
         ra = ra_ref[8 * c : 8 * c + 8]
         rb = rb_ref[8 * c : 8 * c + 8]
+        if c == 2:
+            rb = rb * inner
         before = jnp.where(even, rb, ra)
         after = jnp.where(even, ra, rb)
         rows = [before[0:4], before[4:8]] + [part_ref[c, i] for i in range(SIDE)] + [after[0:4], after[4:8]]
@@ -210,7 +215,7 @@
         near_ref[16 * c : 16 * c + 16] = jnp.where(leaf_even, right, left)
         far_ref[16 * c : 16 * c + 16] = jnp.where(leaf_even, left, right)
     ma = ra_ref[24:48, 0:16]
-    mb = rb_ref[24:48, 0:16]
+    mb = rb_ref[24:48, 0:16] * inner
     window = jnp.concatenate(
         [m_ref[:, 0:16], jnp.where(even, mb, ma), jnp.where(even, ma, mb), jnp.zeros((24, 80), F32)], axis=1
     )
@@ -228,10 +233,13 @@
 
 def slab_halo(ra_ref, rb_ref, s_ref, w_ref, stage_s, stage_w):
     even = position()[2] == 0
+    inner = inner_slab(position()[0])
     halo = []
     for c in range(3):
         ra = ra_ref[8 * c : 8 * c + 8]
         rb = rb_ref[8 * c : 8 * c + 8]
+        if c == 2:
+            rb = rb * inner
         halo.append(jnp.concatenate([jnp.where(even, rb, ra), jnp.where(even, ra, rb)], axis=0))
     n = row_of(LEAVES)
     i = (n >> 2) - 2

time: 51.2 us -> 50.4 us (0.984)
  starting transfers between devices: 15.6 us -> 13.9 us
  waiting for transfers between devices: 0.09 us -> 0.99 us
    ppermute x8, starting transfers between devices: 15.6 us -> 13.9 us  [swap(): return lax.ppermute(value, ALL, SWAPS[name])]
    ppermute x8, waiting for transfers between devices: 0.09 us -> 0.99 us  [swap(): return lax.ppermute(value, ALL, SWAPS[name])]
  transfers between devices with their start and end apart: 8 -> 8, of which waited for: 1 -> 2; matrix products, arithmetic and copies ran while one was open for 0% -> 0% of each run, Pallas kernels for 63% -> 64%
where the time goes in v7:
time: 50.4 us; the launch traced here: 50.2 us
  Pallas kernels  34.3 us (68%)
  starting transfers between devices  13.9 us (28%)
  waiting for transfers between devices  0.99 us (2%)
  local copies, waits for them, and re-layouts  0.81 us (2%)
    pallas_call x7, Pallas kernels, run_direct(): call(functools.partial(direct, tables, by_side, zero, extra, len(ins)), n...  32 us
    ppermute x8, starting transfers between devices, swap(): return lax.ppermute(value, ALL, SWAPS[name])  13.9 us
    pallas_call x1, Pallas kernels, body(): call(finish, 'finish', [V] * 5, shaped(2, SIDE, SIDE, SIZE), far_scratch(...  1.18 us
  transfers between devices with their start and end apart: 8, of which 2 were waited for; matrix products, arithmetic and copies ran while one was open for 0% of the time, Pallas kernels for 64%

profile of v7, /device:TPU:0, one launch (start us, length us, event | category | flops | bytes accessed | tf_op | source)
XLA Modules:
  0.0 50.2 jit_solution(11477073135549210042)
XLA Ops:
  0.0 0.8 %copy-done = f32[3,4,4,256]{3,2,1,0:T(4,128)S(1)} copy-done((f32[3,4,4,256]{3,2,1,0:T(4,128)S(1)}, f32[3,4,4,256]{3,2,1,0:T(4,128)}, u32[]{:S(2)}) %copy-start) | copy-done | bytes 49176
  0.8 0.9 %prepare_own.1 = (bf16[16,32,256]{2,1,0:T(8,128)(2,1)S(1)}, bf16[16,256,32]{2,1,0:T(8,128)(2,1)S(1)}, bf16[16,16,256]{2,1,0:T(8,128)(2,1)S(1)}, f32[24,128]{1,0:...) custom-call(f32[3,4,4,256]{3,2,1,0:T(4,128)S(1)} %copy-done), custom_call_target="tpu_custom_call" | custom-call | flops 4000000 | bytes 1048576 | tf_op jit(solution)/shard_map/prepare_own/pallas_call | solution.py:532
  1.7 0.0 copy-start.2
  1.7 0.1 collective-permute-start
  1.8 6.4 %collective-permute-start.1 = (f32[72,256]{1,0:T(8,128)S(1)}, f32[72,256]{1,0:T(8,128)S(1)}, u32[]{:S(2)}, u32[]{:S(2)}) collective-permute-start(f32[72,256]{1,0:T(8,128)S(1)} %get-tuple-element.54), channel_id=1, source_target_pairs={{0,124},{1,125},{2,126},{3,127},{4,8},{5,9},{6,10},{7,11},{8,4},{9... | collective-permute-start | bytes 221192 | tf_op jit(solution)/shard_map/ppermute | solution.py:73
  8.2 7.4 %direct_own_0.1 = (f32[16,16,256]{2,1,0:T(8,128)S(1)}, f32[17,16,1,256]{3,2,1,0:T(1,128)S(1)}) custom-call(s32[4,4,16]{2,1,0:T(4,128)S(1)} %bitcast.1, bf16[16,32,256]{2,1,0:T(8,128)(2,1)S(1)} %get-tuple-element.57.t_ref, bf16[16,256,32]{2,1,0:T(8,128)(2,1)S(1)} %get-tuple-element.58.s_ref, bf16[16,16,256]{2,1,0:T(8,128)(2,1)S(1)} %get-tuple-element.59.w_ref), custom_call_target="tpu_custom_call" | custom-call | flops 39199997952 | bytes 1048576 | tf_op jit(solution)/shard_map/direct_own_0/pallas_call | solution.py:514
  15.7 0.0 collective-permute-done.ra_ref.refs_1_
  15.7 0.0 collective-permute-done.1.rb_ref.refs_2_
  15.7 0.2 pack_slab.1
  15.9 1.6 %collective-permute-start.2 = (f32[96,256]{1,0:T(8,128)S(1)}, f32[96,256]{1,0:T(8,128)S(1)}, u32[]{:S(2)}, u32[]{:S(2)}) collective-permute-start(f32[96,256]{1,0:T(8,128)S(1)} %get-tuple-element.62), channel_id=1, source_target_pairs={{0,1},{1,0},{2,3},{3,2},{4,5},{5,4},{6,7},{7,6},{8,9},{9,8},{10,11... | collective-permute-start | bytes 294920 | tf_op jit(solution)/shard_map/ppermute | solution.py:73
  17.5 4.0 %direct_own_1.1 = (f32[16,16,256]{2,1,0:T(8,128)S(1)}, bf16[16,256,32]{2,1,0:T(8,128)(2,1)S(1)}, bf16[16,16,256]{2,1,0:T(8,128)(2,1)S(1)}) custom-call(f32[17,16,1,256]{3,2,1,0:T(1,128)S(1)} %get-tuple-element.65.mask_ref, bf16[16,32,256]{2,1,0:T(8,128)(2,1)S(1)} %get-tuple-element.57.t_ref, ...), custom_call_target="tpu_custom_call", output_to_operand_aliasing={{0}: (4, {})} | custom-call | flops 19599998976 | bytes 1048576 | tf_op jit(solution)/shard_map/direct_own_1/pallas_call | solution.py:514
  21.5 2.4 %collective-permute-start.3 = (f32[96,256]{1,0:T(8,128)S(1)}, f32[96,256]{1,0:T(8,128)S(1)}, u32[]{:S(2)}, u32[]{:S(2)}) collective-permute-start(f32[96,256]{1,0:T(8,128)S(1)} %get-tuple-element.70), channel_id=1, source_target_pairs={{0,3},{1,2},{2,1},{3,0},{4,7},{5,6},{6,5},{7,4},{8,11},{9,10},{10,... | collective-permute-start | bytes 294920 | tf_op jit(solution)/shard_map/ppermute | solution.py:73
  23.9 4.0 %direct_own_2.1 = (f32[16,16,256]{2,1,0:T(8,128)S(1)}, bf16[16,256,32]{2,1,0:T(8,128)(2,1)S(1)}, bf16[16,16,256]{2,1,0:T(8,128)(2,1)S(1)}) custom-call(f32[17,16,1,256]{3,2,1,0:T(1,128)S(1)} %get-tuple-element.65.mask_ref, bf16[16,32,256]{2,1,0:T(8,128)(2,1)S(1)} %get-tuple-element.57.t_ref, ...), custom_call_target="tpu_custom_call", output_to_operand_aliasing={{0}: (4, {})} | custom-call | flops 19599998976 | bytes 1048576 | tf_op jit(solution)/shard_map/direct_own_2/pallas_call | solution.py:514
  27.9 0.1 collective-permute-start.4
  28.0 6.9 %direct_slab.1 = (f32[16,16,256]{2,1,0:T(8,128)S(1)}, bf16[16,256,32]{2,1,0:T(8,128)(2,1)S(1)}, bf16[16,16,256]{2,1,0:T(8,128)(2,1)S(1)}) custom-call(f32[17,16,1,256]{3,2,1,0:T(1,128)S(1)} %get-tuple-element.65.mask_ref, bf16[16,32,256]{2,1,0:T(8,128)(2,1)S(1)} %get-tuple-element.57.t_ref, ...), custom_call_target="tpu_custom_call", output_to_operand_aliasing={{0}: (4, {})} | custom-call | flops 33600000000 | bytes 1048576 | tf_op jit(solution)/shard_map/direct_slab/pallas_call | solution.py:514
  35.0 0.3 collective-permute-start.5
  35.3 5.0 %direct_leaf_near.1 = (f32[16,16,256]{2,1,0:T(8,128)S(1)}, f32[16,128]{1,0:T(8,128)S(1)}) custom-call(f32[17,16,1,256]{3,2,1,0:T(1,128)S(1)} %get-tuple-element.65.mask_ref, bf16[16,32,256]{2,1,0:T(8,128)(2,1)S(1)} %get-tuple-element.57.t_ref, bf16[16,256,32]{2,1,0:T(8,128)(2,1)S(1)} %get-tuple-element.83.s_ref, ...), custom_call_target="tpu_custom_call", output_to_operand_aliasing={{0}: (4, {})} | custom-call | flops 24000000000 | bytes 1048576 | tf_op jit(solution)/shard_map/direct_leaf_near/pallas_call | solution.py:514
  40.3 0.9 %collective-permute-start.6 = (f32[24,128]{1,0:T(8,128)S(1)}, f32[24,128]{1,0:T(8,128)S(1)}, u32[]{:S(2)}, u32[]{:S(2)}) collective-permute-start(f32[24,128]{1,0:T(8,128)S(1)} %add.14), channel_id=1, source_target_pairs={{0,32},{1,33},{2,34},{3,35},{4,36},{5,37},{6,38},{7,39},{8,40},{9,... | collective-permute-start | bytes 36872 | tf_op jit(solution)/shard_map/ppermute | solution.py:73
  41.2 2.4 %direct_leaf_far_0.1.refs_0_ = f32[16,16,256]{2,1,0:T(8,128)S(1)} custom-call(f32[17,16,1,256]{3,2,1,0:T(1,128)S(1)} %get-tuple-element.65.mask_ref, bf16[16,32,256]{2,1,0:T(8,128)(2,1)S(1)} %get-tuple-element.57.t_ref, bf16[16,256,32]{2,1,0:T(8,128)(2,1)S(1)} %get-tuple-element.91.s_ref, ...), custom_call_target="tpu_custom_call", output_to_operand_aliasing={{}: (4, {})} | custom-call | flops 12000000000 | bytes 1048576 | tf_op jit(solution)/shard_map/direct_leaf_far_0/pallas_call | solution.py:514
  43.6 0.5 %collective-permute-done.6 = f32[24,128]{1,0:T(8,128)S(1)} collective-permute-done((f32[24,128]{1,0:T(8,128)S(1)}, f32[24,128]{1,0:T(8,128)S(1)}, u32[]{:S(2)}, u32[]{:S(2)}) %collective-permute-start.6) | collective-permute-done | bytes 12320 | tf_op jit(solution)/shard_map/ppermute | solution.py:73
  44.1 2.1 %collective-permute-start.7 = (f32[24,128]{1,0:T(8,128)S(1)}, f32[24,128]{1,0:T(8,128)S(1)}, u32[]{:S(2)}, u32[]{:S(2)}) collective-permute-start(f32[24,128]{1,0:T(8,128)S(1)} %add.15.f_ref), channel_id=1, source_target_pairs={{0,96},{1,97},{2,98},{3,99},{4,100},{5,101},{6,102},{7,103},{8,104... | collective-permute-start | bytes 36872 | tf_op jit(solution)/shard_map/ppermute | solution.py:73
  46.2 2.4 %direct_leaf_far_1.1.acc_ref = f32[16,16,256]{2,1,0:T(8,128)S(1)} custom-call(f32[17,16,1,256]{3,2,1,0:T(1,128)S(1)} %get-tuple-element.65.mask_ref, bf16[16,32,256]{2,1,0:T(8,128)(2,1)S(1)} %get-tuple-element.57.t_ref, bf16[16,256,32]{2,1,0:T(8,128)(2,1)S(1)} %get-tuple-element.91.s_ref, ...), custom_call_target="tpu_custom_call", output_to_operand_aliasing={{}: (4, {})} | custom-call | flops 12000000000 | bytes 1048576 | tf_op jit(solution)/shard_map/direct_leaf_far_1/pallas_call | solution.py:514
  48.5 0.5 collective-permute-done.7.got_ref
  49.0 1.2 %finish.1 = f32[2,4,4,256]{3,2,1,0:T(4,128)} custom-call(f32[3,4,4,256]{3,2,1,0:T(4,128)S(1)} %copy-done.1, f32[16,16,256]{2,1,0:T(8,128)S(1)} %direct_leaf_far_1.1.acc_ref, f32[16,128]{1,0:T(8,128)S(1)} %get-tuple-element.99.near_ref, f32[24,128]{1,0:T(8,128)S(1)} %add.15.f_ref, f32[24,128]{1,0:T(8,128)S(1)} %collective-permute-done.7.got_ref), custom_call_target="tpu_custom_call" | custom-call | flops 4000000 | bytes 1048576 | tf_op jit(solution)/shard_map/finish/pallas_call | solution.py:615
  (13 shorter events, 0.0 us)
Async XLA Ops:
  0.0 0.8 %copy-start = (f32[3,4,4,256]{3,2,1,0:T(4,128)S(1)}, f32[3,4,4,256]{3,2,1,0:T(4,128)}, u32[]{:S(2)}) copy-start(f32[3,4,4,256]{3,2,1,0:T(4,128)} %part_ref.5) | copy-start | bytes 147460
  1.7 6.6 %copy-start.2 = (s32[16,4,4]{0,2,1:T(4,128)S(1)}, s32[16,4,4]{0,2,1:T(4,128)}, u32[]{:S(2)}) copy-start(s32[16,4,4]{0,2,1:T(4,128)} %param.3) | copy-start | bytes 3076
  1.7 14.0 %collective-permute-start = (f32[72,256]{1,0:T(8,128)S(1)}, f32[72,256]{1,0:T(8,128)S(1)}, u32[]{:S(2)}, u32[]{:S(2)}) collective-permute-start(f32[72,256]{1,0:T(8,128)S(1)} %get-tuple-element.53), channel_id=1, source_target_pairs={{0,4},{1,5},{2,6},{3,7},{4,0},{5,1},{6,2},{7,3},{8,12},{9,13},{10,... | collective-permute-start | bytes 221192 | tf_op jit(solution)/shard_map/ppermute | solution.py:73
  1.8 13.9 %collective-permute-start.1 = (f32[72,256]{1,0:T(8,128)S(1)}, f32[72,256]{1,0:T(8,128)S(1)}, u32[]{:S(2)}, u32[]{:S(2)}) collective-permute-start(f32[72,256]{1,0:T(8,128)S(1)} %get-tuple-element.54), channel_id=1, source_target_pairs={{0,124},{1,125},{2,126},{3,127},{4,8},{5,9},{6,10},{7,11},{8,4},{9... | collective-permute-start | bytes 221192 | tf_op jit(solution)/shard_map/ppermute | solution.py:73
  8.2 7.4 %copy-start.1 = (f32[3,4,4,256]{3,2,1,0:T(4,128)S(1)}, f32[3,4,4,256]{3,2,1,0:T(4,128)}, u32[]{:S(2)}) copy-start(f32[3,4,4,256]{3,2,1,0:T(4,128)} %part_ref.5) | copy-start | bytes 147460
  15.9 5.6 %collective-permute-start.2 = (f32[96,256]{1,0:T(8,128)S(1)}, f32[96,256]{1,0:T(8,128)S(1)}, u32[]{:S(2)}, u32[]{:S(2)}) collective-permute-start(f32[96,256]{1,0:T(8,128)S(1)} %get-tuple-element.62), channel_id=1, source_target_pairs={{0,1},{1,0},{2,3},{3,2},{4,5},{5,4},{6,7},{7,6},{8,9},{9,8},{10,11... | collective-permute-start | bytes 294920 | tf_op jit(solution)/shard_map/ppermute | solution.py:73
  21.5 6.4 %collective-permute-start.3 = (f32[96,256]{1,0:T(8,128)S(1)}, f32[96,256]{1,0:T(8,128)S(1)}, u32[]{:S(2)}, u32[]{:S(2)}) collective-permute-start(f32[96,256]{1,0:T(8,128)S(1)} %get-tuple-element.70), channel_id=1, source_target_pairs={{0,3},{1,2},{2,1},{3,0},{4,7},{5,6},{6,5},{7,4},{8,11},{9,10},{10,... | collective-permute-start | bytes 294920 | tf_op jit(solution)/shard_map/ppermute | solution.py:73
  27.9 7.0 %collective-permute-start.4 = (f32[24,128]{1,0:T(8,128)S(1)}, f32[24,128]{1,0:T(8,128)S(1)}, u32[]{:S(2)}, u32[]{:S(2)}) collective-permute-start(f32[24,128]{1,0:T(8,128)S(1)} %slice_add_fusion), channel_id=1, source_target_pairs={{0,8},{1,9},{2,10},{3,11},{4,12},{5,13},{6,14},{7,15},{8,0},{9,1},... | collective-permute-start | bytes 36872 | tf_op jit(solution)/shard_map/ppermute | solution.py:73
  35.0 5.3 %collective-permute-start.5 = (f32[24,128]{1,0:T(8,128)S(1)}, f32[24,128]{1,0:T(8,128)S(1)}, u32[]{:S(2)}, u32[]{:S(2)}) collective-permute-start(f32[24,128]{1,0:T(8,128)S(1)} %add.13), channel_id=1, source_target_pairs={{0,24},{1,25},{2,26},{3,27},{4,28},{5,29},{6,30},{7,31},{8,16},{9,... | collective-permute-start | bytes 36872 | tf_op jit(solution)/shard_map/ppermute | solution.py:73
  40.3 3.8 %collective-permute-start.6 = (f32[24,128]{1,0:T(8,128)S(1)}, f32[24,128]{1,0:T(8,128)S(1)}, u32[]{:S(2)}, u32[]{:S(2)}) collective-permute-start(f32[24,128]{1,0:T(8,128)S(1)} %add.14), channel_id=1, source_target_pairs={{0,32},{1,33},{2,34},{3,35},{4,36},{5,37},{6,38},{7,39},{8,40},{9,... | collective-permute-start | bytes 36872 | tf_op jit(solution)/shard_map/ppermute | solution.py:73
  44.1 4.9 %collective-permute-start.7 = (f32[24,128]{1,0:T(8,128)S(1)}, f32[24,128]{1,0:T(8,128)S(1)}, u32[]{:S(2)}, u32[]{:S(2)}) collective-permute-start(f32[24,128]{1,0:T(8,128)S(1)} %add.15.f_ref), channel_id=1, source_target_pairs={{0,96},{1,97},{2,98},{3,99},{4,100},{5,101},{6,102},{7,103},{8,104... | collective-permute-start | bytes 36872 | tf_op jit(solution)/shard_map/ppermute | solution.py:73

commit v8 on v7

--- a/solution.py
+++ b/solution.py
@@ -317,7 +317,12 @@
                 acc_ref[t] = acc_ref[t] + mask_ref[o, t] * total
         return 0
 
-    if by_side:
+    if by_side == "far":
+        @pl.when(position()[4] == 1)
+        def _():
+            step(position()[3], 0)
+
+    elif by_side:
         step(position()[3], 0)
     elif tables.shape[0] == 1:
         step(0, 0)
@@ -543,7 +548,7 @@
     own = pair_table("own")
     feats = (t0, s0, w0)
     acc, mask = run_direct(
-        "direct_own_0", own[:98].reshape(2, 49, 3), turned, feats, None, outs=[shaped(17, LEAVES, 1, SIZE)]
+        "direct_own_0", own[None, :98], turned, feats, None, outs=[shaped(17, LEAVES, 1, SIZE)]
     )
     m1, f1, send_near, send_far = call(
         pack_slab,
@@ -605,12 +610,12 @@
     f5 = f4 + got
     f5, acc = lax.optimization_barrier((f5, acc))
     got = swap(f5, "x_near")
-    acc = run_direct("direct_leaf_far_0", far_pairs[:, :30], mask, (t0, s3, w3), acc, True)
+    acc = run_direct("direct_leaf_far_0", far_pairs[:, :30], mask, (t0, s3, w3), acc, "far")
     got, acc = lax.optimization_barrier((got, acc))
     f6 = f5 + got
     f6, acc = lax.optimization_barrier((f6, acc))
     got = swap(f6, "x_far")
-    acc = run_direct("direct_leaf_far_1", far_pairs[:, 30:], mask, (t0, s3, w3), acc, True)
+    acc = run_direct("direct_leaf_far_1", far_pairs[:, 30:], mask, (t0, s3, w3), acc, "far")
     got, acc = lax.optimization_barrier((got, acc))
     return call(
         finish,

time: 50.4 us -> 50 us (level)
  Pallas kernels: 34.3 us -> 29.4 us
  waiting for transfers between devices: 0.99 us -> 5.4 us
    pallas_call x7, Pallas kernels: 32 us -> 27.2 us  [run_direct(): call(functools.partial(direct, tables, by_side, zero, extra, len(ins)), n...]
    ppermute x8, waiting for transfers between devices: 0.99 us -> 5.4 us  [swap(): return lax.ppermute(value, ALL, SWAPS[name])]
  transfers between devices with their start and end apart: 8 -> 8, of which waited for: 2 -> 2; matrix products, arithmetic and copies ran while one was open for 0% -> 0% of each run, Pallas kernels for 64% -> 55%
where the time goes in v8:
time: 50 us; the launch traced here: 49.7 us
  Pallas kernels  29.4 us (59%)
  starting transfers between devices  13.9 us (28%)
  waiting for transfers between devices  5.4 us (11%)
  local copies, waits for them, and re-layouts  0.81 us (2%)
    pallas_call x7, Pallas kernels, run_direct(): call(functools.partial(direct, tables, by_side, zero, extra, len(ins)), n...  27.2 us
    ppermute x8, starting transfers between devices, swap(): return lax.ppermute(value, ALL, SWAPS[name])  13.9 us
    ppermute x8, waiting for transfers between devices, swap(): return lax.ppermute(value, ALL, SWAPS[name])  5.4 us
    pallas_call x1, Pallas kernels, body(): call(finish, 'finish', [V] * 5, shaped(2, SIDE, SIDE, SIZE), far_scratch(...  1.18 us
  transfers between devices with their start and end apart: 8, of which 2 were waited for; matrix products, arithmetic and copies ran while one was open for 0% of the time, Pallas kernels for 55%

profile of v8, /device:TPU:0, one launch (start us, length us, event | category | flops | bytes accessed | tf_op | source)
XLA Modules:
  0.0 49.7 jit_solution(16136930938840247230)
XLA Ops:
  0.0 0.8 %copy-done = f32[3,4,4,256]{3,2,1,0:T(4,128)S(1)} copy-done((f32[3,4,4,256]{3,2,1,0:T(4,128)S(1)}, f32[3,4,4,256]{3,2,1,0:T(4,128)}, u32[]{:S(2)}) %copy-start) | copy-done | bytes 49176
  0.8 0.9 %prepare_own.1 = (bf16[16,32,256]{2,1,0:T(8,128)(2,1)S(1)}, bf16[16,256,32]{2,1,0:T(8,128)(2,1)S(1)}, bf16[16,16,256]{2,1,0:T(8,128)(2,1)S(1)}, f32[24,128]{1,0:...) custom-call(f32[3,4,4,256]{3,2,1,0:T(4,128)S(1)} %copy-done), custom_call_target="tpu_custom_call" | custom-call | flops 4000000 | bytes 1048576 | tf_op jit(solution)/shard_map/prepare_own/pallas_call | solution.py:537
  1.7 0.0 copy-start.2
  1.7 0.1 collective-permute-start
  1.8 6.4 %collective-permute-start.1 = (f32[72,256]{1,0:T(8,128)S(1)}, f32[72,256]{1,0:T(8,128)S(1)}, u32[]{:S(2)}, u32[]{:S(2)}) collective-permute-start(f32[72,256]{1,0:T(8,128)S(1)} %get-tuple-element.54), channel_id=1, source_target_pairs={{0,124},{1,125},{2,126},{3,127},{4,8},{5,9},{6,10},{7,11},{8,4},{9... | collective-permute-start | bytes 221192 | tf_op jit(solution)/shard_map/ppermute | solution.py:73
  8.2 7.0 %direct_own_0.1 = (f32[16,16,256]{2,1,0:T(8,128)S(1)}, f32[17,16,1,256]{3,2,1,0:T(1,128)S(1)}) custom-call(s32[4,4,16]{2,1,0:T(4,128)S(1)} %bitcast.1, bf16[16,32,256]{2,1,0:T(8,128)(2,1)S(1)} %get-tuple-element.57.t_ref, bf16[16,256,32]{2,1,0:T(8,128)(2,1)S(1)} %get-tuple-element.58.s_ref, bf16[16,16,256]{2,1,0:T(8,128)(2,1)S(1)} %get-tuple-element.59.w_ref), custom_call_target="tpu_custom_call" | custom-call | flops 39199997952 | bytes 1048576 | tf_op jit(solution)/shard_map/direct_own_0/pallas_call | solution.py:519
  15.2 0.2 pack_slab.1
  15.4 1.8 %collective-permute-start.2 = (f32[96,256]{1,0:T(8,128)S(1)}, f32[96,256]{1,0:T(8,128)S(1)}, u32[]{:S(2)}, u32[]{:S(2)}) collective-permute-start(f32[96,256]{1,0:T(8,128)S(1)} %get-tuple-element.62), channel_id=1, source_target_pairs={{0,1},{1,0},{2,3},{3,2},{4,5},{5,4},{6,7},{7,6},{8,9},{9,8},{10,11... | collective-permute-start | bytes 294920 | tf_op jit(solution)/shard_map/ppermute | solution.py:73
  17.2 4.0 %direct_own_1.1 = (f32[16,16,256]{2,1,0:T(8,128)S(1)}, bf16[16,256,32]{2,1,0:T(8,128)(2,1)S(1)}, bf16[16,16,256]{2,1,0:T(8,128)(2,1)S(1)}) custom-call(f32[17,16,1,256]{3,2,1,0:T(1,128)S(1)} %get-tuple-element.65.mask_ref, bf16[16,32,256]{2,1,0:T(8,128)(2,1)S(1)} %get-tuple-element.57.t_ref, ...), custom_call_target="tpu_custom_call", output_to_operand_aliasing={{0}: (4, {})} | custom-call | flops 19599998976 | bytes 1048576 | tf_op jit(solution)/shard_map/direct_own_1/pallas_call | solution.py:519
  21.2 0.0 collective-permute-done.2.r_ref.refs_1_.refs_3_
  21.2 2.3 %collective-permute-start.3 = (f32[96,256]{1,0:T(8,128)S(1)}, f32[96,256]{1,0:T(8,128)S(1)}, u32[]{:S(2)}, u32[]{:S(2)}) collective-permute-start(f32[96,256]{1,0:T(8,128)S(1)} %get-tuple-element.70), channel_id=1, source_target_pairs={{0,3},{1,2},{2,1},{3,0},{4,7},{5,6},{6,5},{7,4},{8,11},{9,10},{10,... | collective-permute-start | bytes 294920 | tf_op jit(solution)/shard_map/ppermute | solution.py:73
  23.5 4.0 %direct_own_2.1 = (f32[16,16,256]{2,1,0:T(8,128)S(1)}, bf16[16,256,32]{2,1,0:T(8,128)(2,1)S(1)}, bf16[16,16,256]{2,1,0:T(8,128)(2,1)S(1)}) custom-call(f32[17,16,1,256]{3,2,1,0:T(1,128)S(1)} %get-tuple-element.65.mask_ref, bf16[16,32,256]{2,1,0:T(8,128)(2,1)S(1)} %get-tuple-element.57.t_ref, ...), custom_call_target="tpu_custom_call", output_to_operand_aliasing={{0}: (4, {})} | custom-call | flops 19599998976 | bytes 1048576 | tf_op jit(solution)/shard_map/direct_own_2/pallas_call | solution.py:519
  27.5 0.0 collective-permute-done.3.refs_1_.refs_4_
  27.5 0.3 collective-permute-start.4
  27.8 6.9 %direct_slab.1 = (f32[16,16,256]{2,1,0:T(8,128)S(1)}, bf16[16,256,32]{2,1,0:T(8,128)(2,1)S(1)}, bf16[16,16,256]{2,1,0:T(8,128)(2,1)S(1)}) custom-call(f32[17,16,1,256]{3,2,1,0:T(1,128)S(1)} %get-tuple-element.65.mask_ref, bf16[16,32,256]{2,1,0:T(8,128)(2,1)S(1)} %get-tuple-element.57.t_ref, ...), custom_call_target="tpu_custom_call", output_to_operand_aliasing={{0}: (4, {})} | custom-call | flops 33600000000 | bytes 1048576 | tf_op jit(solution)/shard_map/direct_slab/pallas_call | solution.py:519
  34.7 0.1 collective-permute-start.5
  34.8 5.0 %direct_leaf_near.1 = (f32[16,16,256]{2,1,0:T(8,128)S(1)}, f32[16,128]{1,0:T(8,128)S(1)}) custom-call(f32[17,16,1,256]{3,2,1,0:T(1,128)S(1)} %get-tuple-element.65.mask_ref, bf16[16,32,256]{2,1,0:T(8,128)(2,1)S(1)} %get-tuple-element.57.t_ref, bf16[16,256,32]{2,1,0:T(8,128)(2,1)S(1)} %get-tuple-element.83.s_ref, ...), custom_call_target="tpu_custom_call", output_to_operand_aliasing={{0}: (4, {})} | custom-call | flops 24000000000 | bytes 1048576 | tf_op jit(solution)/shard_map/direct_leaf_near/pallas_call | solution.py:519
  39.9 0.0 collective-permute-done.5
  39.9 0.9 %collective-permute-start.6 = (f32[24,128]{1,0:T(8,128)S(1)}, f32[24,128]{1,0:T(8,128)S(1)}, u32[]{:S(2)}, u32[]{:S(2)}) collective-permute-start(f32[24,128]{1,0:T(8,128)S(1)} %add.14), channel_id=1, source_target_pairs={{0,32},{1,33},{2,34},{3,35},{4,36},{5,37},{6,38},{7,39},{8,40},{9,... | collective-permute-start | bytes 36872 | tf_op jit(solution)/shard_map/ppermute | solution.py:73
  40.8 2.9 %collective-permute-done.6 = f32[24,128]{1,0:T(8,128)S(1)} collective-permute-done((f32[24,128]{1,0:T(8,128)S(1)}, f32[24,128]{1,0:T(8,128)S(1)}, u32[]{:S(2)}, u32[]{:S(2)}) %collective-permute-start.6) | collective-permute-done | bytes 12320 | tf_op jit(solution)/shard_map/ppermute | solution.py:73
  43.6 2.1 %collective-permute-start.7 = (f32[24,128]{1,0:T(8,128)S(1)}, f32[24,128]{1,0:T(8,128)S(1)}, u32[]{:S(2)}, u32[]{:S(2)}) collective-permute-start(f32[24,128]{1,0:T(8,128)S(1)} %add.15.f_ref), channel_id=1, source_target_pairs={{0,96},{1,97},{2,98},{3,99},{4,100},{5,101},{6,102},{7,103},{8,104... | collective-permute-start | bytes 36872 | tf_op jit(solution)/shard_map/ppermute | solution.py:73
  45.7 0.3 direct_leaf_far_1.1.acc_ref
  46.0 2.5 %collective-permute-done.7.got_ref = f32[24,128]{1,0:T(8,128)S(1)} collective-permute-done((f32[24,128]{1,0:T(8,128)S(1)}, f32[24,128]{1,0:T(8,128)S(1)}, u32[]{:S(2)}, u32[]{:S(2)}) %collective-permute-start.7) | collective-permute-done | bytes 12320 | tf_op jit(solution)/shard_map/ppermute | solution.py:73
  48.6 1.2 %finish.1 = f32[2,4,4,256]{3,2,1,0:T(4,128)} custom-call(f32[3,4,4,256]{3,2,1,0:T(4,128)S(1)} %copy-done.1, f32[16,16,256]{2,1,0:T(8,128)S(1)} %direct_leaf_far_1.1.acc_ref, f32[16,128]{1,0:T(8,128)S(1)} %get-tuple-element.99.near_ref, f32[24,128]{1,0:T(8,128)S(1)} %add.15.f_ref, f32[24,128]{1,0:T(8,128)S(1)} %collective-permute-done.7.got_ref), custom_call_target="tpu_custom_call" | custom-call | flops 4000000 | bytes 1048576 | tf_op jit(solution)/shard_map/finish/pallas_call | solution.py:620
  (13 shorter events, 0.1 us)
Async XLA Ops:
  0.0 0.8 %copy-start = (f32[3,4,4,256]{3,2,1,0:T(4,128)S(1)}, f32[3,4,4,256]{3,2,1,0:T(4,128)}, u32[]{:S(2)}) copy-start(f32[3,4,4,256]{3,2,1,0:T(4,128)} %part_ref.5) | copy-start | bytes 147460
  1.7 6.6 %copy-start.2 = (s32[16,4,4]{0,2,1:T(4,128)S(1)}, s32[16,4,4]{0,2,1:T(4,128)}, u32[]{:S(2)}) copy-start(s32[16,4,4]{0,2,1:T(4,128)} %param.3) | copy-start | bytes 3076
  1.7 13.5 %collective-permute-start = (f32[72,256]{1,0:T(8,128)S(1)}, f32[72,256]{1,0:T(8,128)S(1)}, u32[]{:S(2)}, u32[]{:S(2)}) collective-permute-start(f32[72,256]{1,0:T(8,128)S(1)} %get-tuple-element.53), channel_id=1, source_target_pairs={{0,4},{1,5},{2,6},{3,7},{4,0},{5,1},{6,2},{7,3},{8,12},{9,13},{10,... | collective-permute-start | bytes 221192 | tf_op jit(solution)/shard_map/ppermute | solution.py:73
  1.8 13.4 %collective-permute-start.1 = (f32[72,256]{1,0:T(8,128)S(1)}, f32[72,256]{1,0:T(8,128)S(1)}, u32[]{:S(2)}, u32[]{:S(2)}) collective-permute-start(f32[72,256]{1,0:T(8,128)S(1)} %get-tuple-element.54), channel_id=1, source_target_pairs={{0,124},{1,125},{2,126},{3,127},{4,8},{5,9},{6,10},{7,11},{8,4},{9... | collective-permute-start | bytes 221192 | tf_op jit(solution)/shard_map/ppermute | solution.py:73
  8.2 7.0 %copy-start.1 = (f32[3,4,4,256]{3,2,1,0:T(4,128)S(1)}, f32[3,4,4,256]{3,2,1,0:T(4,128)}, u32[]{:S(2)}) copy-start(f32[3,4,4,256]{3,2,1,0:T(4,128)} %part_ref.5) | copy-start | bytes 147460
  15.4 5.8 %collective-permute-start.2 = (f32[96,256]{1,0:T(8,128)S(1)}, f32[96,256]{1,0:T(8,128)S(1)}, u32[]{:S(2)}, u32[]{:S(2)}) collective-permute-start(f32[96,256]{1,0:T(8,128)S(1)} %get-tuple-element.62), channel_id=1, source_target_pairs={{0,1},{1,0},{2,3},{3,2},{4,5},{5,4},{6,7},{7,6},{8,9},{9,8},{10,11... | collective-permute-start | bytes 294920 | tf_op jit(solution)/shard_map/ppermute | solution.py:73
  21.2 6.2 %collective-permute-start.3 = (f32[96,256]{1,0:T(8,128)S(1)}, f32[96,256]{1,0:T(8,128)S(1)}, u32[]{:S(2)}, u32[]{:S(2)}) collective-permute-start(f32[96,256]{1,0:T(8,128)S(1)} %get-tuple-element.70), channel_id=1, source_target_pairs={{0,3},{1,2},{2,1},{3,0},{4,7},{5,6},{6,5},{7,4},{8,11},{9,10},{10,... | collective-permute-start | bytes 294920 | tf_op jit(solution)/shard_map/ppermute | solution.py:73
  27.5 7.2 %collective-permute-start.4 = (f32[24,128]{1,0:T(8,128)S(1)}, f32[24,128]{1,0:T(8,128)S(1)}, u32[]{:S(2)}, u32[]{:S(2)}) collective-permute-start(f32[24,128]{1,0:T(8,128)S(1)} %slice_add_fusion), channel_id=1, source_target_pairs={{0,8},{1,9},{2,10},{3,11},{4,12},{5,13},{6,14},{7,15},{8,0},{9,1},... | collective-permute-start | bytes 36872 | tf_op jit(solution)/shard_map/ppermute | solution.py:73
  34.7 5.1 %collective-permute-start.5 = (f32[24,128]{1,0:T(8,128)S(1)}, f32[24,128]{1,0:T(8,128)S(1)}, u32[]{:S(2)}, u32[]{:S(2)}) collective-permute-start(f32[24,128]{1,0:T(8,128)S(1)} %add.13), channel_id=1, source_target_pairs={{0,24},{1,25},{2,26},{3,27},{4,28},{5,29},{6,30},{7,31},{8,16},{9,... | collective-permute-start | bytes 36872 | tf_op jit(solution)/shard_map/ppermute | solution.py:73
  39.9 3.8 %collective-permute-start.6 = (f32[24,128]{1,0:T(8,128)S(1)}, f32[24,128]{1,0:T(8,128)S(1)}, u32[]{:S(2)}, u32[]{:S(2)}) collective-permute-start(f32[24,128]{1,0:T(8,128)S(1)} %add.14), channel_id=1, source_target_pairs={{0,32},{1,33},{2,34},{3,35},{4,36},{5,37},{6,38},{7,39},{8,40},{9,... | collective-permute-start | bytes 36872 | tf_op jit(solution)/shard_map/ppermute | solution.py:73
  43.6 4.9 %collective-permute-start.7 = (f32[24,128]{1,0:T(8,128)S(1)}, f32[24,128]{1,0:T(8,128)S(1)}, u32[]{:S(2)}, u32[]{:S(2)}) collective-permute-start(f32[24,128]{1,0:T(8,128)S(1)} %add.15.f_ref), channel_id=1, source_target_pairs={{0,96},{1,97},{2,98},{3,99},{4,100},{5,101},{6,102},{7,103},{8,104... | collective-permute-start | bytes 36872 | tf_op jit(solution)/shard_map/ppermute | solution.py:73

commit v9 on v7

--- a/solution.py
+++ b/solution.py
@@ -287,7 +287,36 @@
     return out
 
 
-def direct(tables, by_side, zero, extra, extra_in, mask_ref, t_ref, s_ref, w_ref, *refs):
+def pairs(tables, mask_ref, t_ref, s_ref, w_ref, acc_ref, index, unused):
+    for n in range(tables.shape[1]):
+        t, s, o = (chosen(index, [int(v) for v in tables[:, n, c]]) for c in range(3))
+        distance = jnp.dot(s_ref[s], t_ref[t], preferred_element_type=F32)
+        kernel = 1.0 / distance
+        high = kernel.astype(BF16)
+        low = (kernel - high.astype(F32)).astype(BF16)
+        w = w_ref[s]
+        total = jnp.dot(w, high, preferred_element_type=F32) + jnp.dot(w, low, preferred_element_type=F32)
+        if isinstance(o, int) and o == 16:
+            acc_ref[t] = acc_ref[t] + total
+        else:
+            acc_ref[t] = acc_ref[t] + mask_ref[o, t] * total
+    return 0
+
+
+def direct_sides(near, far, extra, extra_in, mask_ref, t_ref, s2_ref, w2_ref, s3_ref, w3_ref, acc_in, *refs):
+    acc_ref = refs[extra_in]
+    acc_ref[...] = acc_in[...]
+    parity = position()[3]
+    pairs(near, mask_ref, t_ref, s2_ref, w2_ref, acc_ref, parity, 0)
+    if extra is not None:
+        extra(*refs[:extra_in], *refs[extra_in + 1 :])
+
+    @pl.when(position()[4] == 1)
+    def _():
+        pairs(far, mask_ref, t_ref, s3_ref, w3_ref, acc_ref, parity, 0)
+
+
+def direct(tables, zero, extra, extra_in, mask_ref, t_ref, s_ref, w_ref, *refs):
     if zero:
         acc_ref, rows_ref = refs
         acc_ref[...] = jnp.zeros_like(acc_ref)
@@ -300,26 +329,8 @@
         acc_ref = refs[extra_in + 1]
         acc_ref[...] = refs[0][...]
         others = refs[1 : extra_in + 1] + refs[extra_in + 2 :]
-    count = tables.shape[1]
-
-    def step(index, unused):
-        for n in range(count):
-            t, s, o = (chosen(index, [int(v) for v in tables[:, n, c]]) for c in range(3))
-            distance = jnp.dot(s_ref[s], t_ref[t], preferred_element_type=F32)
-            kernel = 1.0 / distance
-            high = kernel.astype(BF16)
-            low = (kernel - high.astype(F32)).astype(BF16)
-            w = w_ref[s]
-            total = jnp.dot(w, high, preferred_element_type=F32) + jnp.dot(w, low, preferred_element_type=F32)
-            if isinstance(o, int) and o == 16:
-                acc_ref[t] = acc_ref[t] + total
-            else:
-                acc_ref[t] = acc_ref[t] + mask_ref[o, t] * total
-        return 0
-
-    if by_side:
-        step(position()[3], 0)
-    elif tables.shape[0] == 1:
+    step = functools.partial(pairs, tables, mask_ref, t_ref, s_ref, w_ref, acc_ref)
+    if tables.shape[0] == 1:
         step(0, 0)
     else:
         lax.fori_loop(0, tables.shape[0], step, 0)
@@ -508,17 +519,31 @@
 PAIR = 400_000_000
 
 
-def run_direct(name, tables, mask, feats, acc, by_side=False, extra=None, ins=(), outs=(), scratch=()):
+def run_direct(name, tables, mask, feats, acc, extra=None, ins=(), outs=(), scratch=()):
     zero = acc is None
     args = [mask, *feats] + ([] if zero else [acc]) + list(ins)
     got = call(
-        functools.partial(direct, tables, by_side, zero, extra, len(ins)),
+        functools.partial(direct, tables, zero, extra, len(ins)),
         name,
         [V] * len(args),
         [shaped(LEAVES, 16, SIZE), *outs],
         list(scratch),
-        PAIR * (1 if by_side else tables.shape[0]) * tables.shape[1],
+        PAIR * tables.shape[0] * tables.shape[1],
         {} if zero else {4: 0},
+    )(*args)
+    return got if outs else got[0]
+
+
+def run_sides(name, near, far, args, extra=None, ins=(), outs=(), scratch=()):
+    args = [*args, *ins]
+    got = call(
+        functools.partial(direct_sides, near, far, extra, len(ins)),
+        name,
+        [V] * len(args),
+        [shaped(LEAVES, 16, SIZE), *outs],
+        list(scratch),
+        PAIR * 60,
+        {6: 0},
     )(*args)
     return got if outs else got[0]
 
@@ -571,46 +596,39 @@
     f3 = f2 + recv_far[72:96, 0:128]
     f3, acc = lax.optimization_barrier((f3, acc))
     got = swap(f3, "z_near")
+    slab_pairs = pair_table("slab").reshape(2, 1, 42, 3)
     acc, s3, w3 = run_direct(
-        "direct_slab",
-        pair_table("slab").reshape(2, 42, 3),
-        mask,
-        (t0, s1, w1),
-        acc,
-        extra=far_halo,
-        ins=(recv_far,),
-        **built,
+        "direct_slab_0", slab_pairs[0], mask, (t0, s1, w1), acc, extra=far_halo, ins=(recv_far,), **built
     )
     got, acc = lax.optimization_barrier((got, acc))
     f4 = f3 + got
     f4, acc = lax.optimization_barrier((f4, acc))
     got = swap(f4, "z_far")
+    acc = run_direct("direct_slab_1", slab_pairs[1], mask, (t0, s1, w1), acc)
+    got, acc = lax.optimization_barrier((got, acc))
+    f5 = f4 + got
+    f5, acc = lax.optimization_barrier((f5, acc))
+    got = swap(f5, "x_near")
     right = pair_table("leaf", True)
     left = pair_table("leaf", False)
     near_pairs = np.stack([right, left])
     far_pairs = np.stack([left, right])
-    acc, local = run_direct(
-        "direct_leaf_near",
-        near_pairs,
-        mask,
-        (t0, s2, w2),
-        acc,
-        True,
+    shared = (mask, t0, s2, w2, s3, w3)
+    acc, local = run_sides(
+        "direct_sides_0",
+        near_pairs[:, :30],
+        far_pairs[:, :30],
+        (*shared, acc),
         extra=leaf_field,
         ins=(turned, m1, recv_near, recv_far),
         outs=[shaped(LEAVES, 128)],
         scratch=far_scratch(256),
     )
     got, acc = lax.optimization_barrier((got, acc))
-    f5 = f4 + got
-    f5, acc = lax.optimization_barrier((f5, acc))
-    got = swap(f5, "x_near")
-    acc = run_direct("direct_leaf_far_0", far_pairs[:, :30], mask, (t0, s3, w3), acc, True)
-    got, acc = lax.optimization_barrier((got, acc))
     f6 = f5 + got
     f6, acc = lax.optimization_barrier((f6, acc))
     got = swap(f6, "x_far")
-    acc = run_direct("direct_leaf_far_1", far_pairs[:, 30:], mask, (t0, s3, w3), acc, True)
+    acc = run_sides("direct_sides_1", near_pairs[:, 30:], far_pairs[:, 30:], (*shared, acc))
     got, acc = lax.optimization_barrier((got, acc))
     return call(
         finish,

time: 50.4 us -> 48.4 us (0.960)
  the two profiles are of different devices: /device:TPU:0 before, /device:TPU:8 now
where the time goes in v9:
time: 48.4 us; the launch traced here: 48.3 us
  Pallas kernels  34.3 us (71%)
  starting transfers between devices  10.9 us (23%)
  waiting for transfers between devices  2.12 us (4%)
  local copies, waits for them, and re-layouts  0.81 us (2%)
    pallas_call x5, Pallas kernels, run_direct(): call(functools.partial(direct, tables, zero, extra, len(ins)), name, [V]...  22 us
    ppermute x8, starting transfers between devices, swap(): return lax.ppermute(value, ALL, SWAPS[name])  10.9 us
    pallas_call x2, Pallas kernels, run_sides(): call(functools.partial(direct_sides, near, far, extra, len(ins)), name, [...  9.99 us
    ppermute x8, waiting for transfers between devices, swap(): return lax.ppermute(value, ALL, SWAPS[name])  2.12 us
    pallas_call x1, Pallas kernels, body(): call(finish, 'finish', [V] * 5, shaped(2, SIDE, SIDE, SIZE), far_scratch(...  1.2 us
  transfers between devices with their start and end apart: 8, of which 3 were waited for; matrix products, arithmetic and copies ran while one was open for 0% of the time, Pallas kernels for 66%

profile of v9, /device:TPU:8, one launch (start us, length us, event | category | flops | bytes accessed | tf_op | source)
XLA Modules:
  0.0 48.3 jit_solution(4321813591236001212)
XLA Ops:
  0.0 0.8 %copy-done = f32[3,4,4,256]{3,2,1,0:T(4,128)S(1)} copy-done((f32[3,4,4,256]{3,2,1,0:T(4,128)S(1)}, f32[3,4,4,256]{3,2,1,0:T(4,128)}, u32[]{:S(2)}) %copy-start) | copy-done | bytes 49176
  0.8 0.9 %prepare_own.1 = (bf16[16,32,256]{2,1,0:T(8,128)(2,1)S(1)}, bf16[16,256,32]{2,1,0:T(8,128)(2,1)S(1)}, bf16[16,16,256]{2,1,0:T(8,128)(2,1)S(1)}, f32[24,128]{1,0:...) custom-call(f32[3,4,4,256]{3,2,1,0:T(4,128)S(1)} %copy-done), custom_call_target="tpu_custom_call" | custom-call | flops 4000000 | bytes 1048576 | tf_op jit(solution)/shard_map/prepare_own/pallas_call | solution.py:557
  1.7 0.0 copy-start.2
  1.7 0.1 collective-permute-start
  1.8 6.3 %collective-permute-start.1 = (f32[72,256]{1,0:T(8,128)S(1)}, f32[72,256]{1,0:T(8,128)S(1)}, u32[]{:S(2)}, u32[]{:S(2)}) collective-permute-start(f32[72,256]{1,0:T(8,128)S(1)} %get-tuple-element.54), channel_id=1, source_target_pairs={{0,124},{1,125},{2,126},{3,127},{4,8},{5,9},{6,10},{7,11},{8,4},{9... | collective-permute-start | bytes 221192 | tf_op jit(solution)/shard_map/ppermute | solution.py:73
  8.1 7.4 %direct_own_0.1 = (f32[16,16,256]{2,1,0:T(8,128)S(1)}, f32[17,16,1,256]{3,2,1,0:T(1,128)S(1)}) custom-call(s32[4,4,16]{2,1,0:T(4,128)S(1)} %bitcast.1, bf16[16,32,256]{2,1,0:T(8,128)(2,1)S(1)} %get-tuple-element.57.t_ref, bf16[16,256,32]{2,1,0:T(8,128)(2,1)S(1)} %get-tuple-element.58.s_ref, bf16[16,16,256]{2,1,0:T(8,128)(2,1)S(1)} %get-tuple-element.59.w_ref), custom_call_target="tpu_custom_call" | custom-call | flops 39199997952 | bytes 1048576 | tf_op jit(solution)/shard_map/direct_own_0/pallas_call | solution.py:525
  15.5 0.0 collective-permute-done.ra_ref.refs_1_
  15.6 0.0 collective-permute-done.1.rb_ref.refs_2_
  15.6 0.2 pack_slab.1
  15.8 0.5 collective-permute-start.2
  16.2 4.0 %direct_own_1.1 = (f32[16,16,256]{2,1,0:T(8,128)S(1)}, bf16[16,256,32]{2,1,0:T(8,128)(2,1)S(1)}, bf16[16,16,256]{2,1,0:T(8,128)(2,1)S(1)}) custom-call(f32[17,16,1,256]{3,2,1,0:T(1,128)S(1)} %get-tuple-element.65.mask_ref, bf16[16,32,256]{2,1,0:T(8,128)(2,1)S(1)} %get-tuple-element.57.t_ref, ...), custom_call_target="tpu_custom_call", output_to_operand_aliasing={{0}: (4, {})} | custom-call | flops 19599998976 | bytes 1048576 | tf_op jit(solution)/shard_map/direct_own_1/pallas_call | solution.py:525
  20.2 0.2 collective-permute-done.2.r_ref.refs_1_.refs_2_
  20.4 2.5 %collective-permute-start.3 = (f32[96,256]{1,0:T(8,128)S(1)}, f32[96,256]{1,0:T(8,128)S(1)}, u32[]{:S(2)}, u32[]{:S(2)}) collective-permute-start(f32[96,256]{1,0:T(8,128)S(1)} %get-tuple-element.70), channel_id=1, source_target_pairs={{0,3},{1,2},{2,1},{3,0},{4,7},{5,6},{6,5},{7,4},{8,11},{9,10},{10,... | collective-permute-start | bytes 294920 | tf_op jit(solution)/shard_map/ppermute | solution.py:73
  22.9 4.0 %direct_own_2.1 = (f32[16,16,256]{2,1,0:T(8,128)S(1)}, bf16[16,256,32]{2,1,0:T(8,128)(2,1)S(1)}, bf16[16,16,256]{2,1,0:T(8,128)(2,1)S(1)}) custom-call(f32[17,16,1,256]{3,2,1,0:T(1,128)S(1)} %get-tuple-element.65.mask_ref, bf16[16,32,256]{2,1,0:T(8,128)(2,1)S(1)} %get-tuple-element.57.t_ref, ...), custom_call_target="tpu_custom_call", output_to_operand_aliasing={{0}: (4, {})} | custom-call | flops 19599998976 | bytes 1048576 | tf_op jit(solution)/shard_map/direct_own_2/pallas_call | solution.py:525
  26.9 0.1 collective-permute-start.4
  27.0 3.5 %direct_slab_0.1 = (f32[16,16,256]{2,1,0:T(8,128)S(1)}, bf16[16,256,32]{2,1,0:T(8,128)(2,1)S(1)}, bf16[16,16,256]{2,1,0:T(8,128)(2,1)S(1)}) custom-call(f32[17,16,1,256]{3,2,1,0:T(1,128)S(1)} %get-tuple-element.65.mask_ref, bf16[16,32,256]{2,1,0:T(8,128)(2,1)S(1)} %get-tuple-element.57.t_ref, ...), custom_call_target="tpu_custom_call", output_to_operand_aliasing={{0}: (4, {})} | custom-call | flops 16800000000 | bytes 1048576 | tf_op jit(solution)/shard_map/direct_slab_0/pallas_call | solution.py:525
  30.5 0.2 collective-permute-done.4
  30.7 3.2 %direct_slab_1.1.acc_in = f32[16,16,256]{2,1,0:T(8,128)S(1)} custom-call(f32[17,16,1,256]{3,2,1,0:T(1,128)S(1)} %get-tuple-element.65.mask_ref, bf16[16,32,256]{2,1,0:T(8,128)(2,1)S(1)} %get-tuple-element.57.t_ref, bf16[16,256,32]{2,1,0:T(8,128)(2,1)S(1)} %get-tuple-element.76.s_ref, ...), custom_call_target="tpu_custom_call", output_to_operand_aliasing={{}: (4, {})} | custom-call | flops 16800000000 | bytes 1048576 | tf_op jit(solution)/shard_map/direct_slab_1/pallas_call | solution.py:525
  33.9 1.7 %collective-permute-done.5 = f32[24,128]{1,0:T(8,128)S(1)} collective-permute-done((f32[24,128]{1,0:T(8,128)S(1)}, f32[24,128]{1,0:T(8,128)S(1)}, u32[]{:S(2)}, u32[]{:S(2)}) %collective-permute-start.5) | collective-permute-done | bytes 12320 | tf_op jit(solution)/shard_map/ppermute | solution.py:73
  35.6 0.0 collective-permute-start.6
  35.6 5.3 %direct_sides_0.1 = (f32[16,16,256]{2,1,0:T(8,128)S(1)}, f32[16,128]{1,0:T(8,128)S(1)}) custom-call(f32[17,16,1,256]{3,2,1,0:T(1,128)S(1)} %get-tuple-element.65.mask_ref, bf16[16,32,256]{2,1,0:T(8,128)(2,1)S(1)} %get-tuple-element.57.t_ref, bf16[16,256,32]{2,1,0:T(8,128)(2,1)S(1)} %get-tuple-element.87.s2_ref, ...), custom_call_target="tpu_custom_call", output_to_operand_aliasing={{0}: (6, {})} | custom-call | flops 24000000000 | bytes 1048576 | tf_op jit(solution)/shard_map/direct_sides_0/pallas_call | solution.py:539
  40.9 1.4 %collective-permute-start.7 = (f32[24,128]{1,0:T(8,128)S(1)}, f32[24,128]{1,0:T(8,128)S(1)}, u32[]{:S(2)}, u32[]{:S(2)}) collective-permute-start(f32[24,128]{1,0:T(8,128)S(1)} %add.15.f_ref), channel_id=1, source_target_pairs={{0,96},{1,97},{2,98},{3,99},{4,100},{5,101},{6,102},{7,103},{8,104... | collective-permute-start | bytes 36872 | tf_op jit(solution)/shard_map/ppermute | solution.py:73
  42.4 4.7 %direct_sides_1.1.acc_ref = f32[16,16,256]{2,1,0:T(8,128)S(1)} custom-call(f32[17,16,1,256]{3,2,1,0:T(1,128)S(1)} %get-tuple-element.65.mask_ref, bf16[16,32,256]{2,1,0:T(8,128)(2,1)S(1)} %get-tuple-element.57.t_ref, bf16[16,256,32]{2,1,0:T(8,128)(2,1)S(1)} %get-tuple-element.87.s2_ref, ...), custom_call_target="tpu_custom_call", output_to_operand_aliasing={{}: (6, {})} | custom-call | flops 24000000000 | bytes 1048576 | tf_op jit(solution)/shard_map/direct_sides_1/pallas_call | solution.py:539
  47.1 1.2 %finish.1 = f32[2,4,4,256]{3,2,1,0:T(4,128)} custom-call(f32[3,4,4,256]{3,2,1,0:T(4,128)S(1)} %copy-done.1, f32[16,16,256]{2,1,0:T(8,128)S(1)} %direct_sides_1.1.acc_ref, f32[16,128]{1,0:T(8,128)S(1)} %get-tuple-element.99.near_ref, f32[24,128]{1,0:T(8,128)S(1)} %add.15.f_ref, f32[24,128]{1,0:T(8,128)S(1)} %collective-permute-done.7.got_ref), custom_call_target="tpu_custom_call" | custom-call | flops 4000000 | bytes 1048576 | tf_op jit(solution)/shard_map/finish/pallas_call | solution.py:633
  (13 shorter events, 0.1 us)
Async XLA Ops:
  0.0 0.8 %copy-start = (f32[3,4,4,256]{3,2,1,0:T(4,128)S(1)}, f32[3,4,4,256]{3,2,1,0:T(4,128)}, u32[]{:S(2)}) copy-start(f32[3,4,4,256]{3,2,1,0:T(4,128)} %part_ref.5) | copy-start | bytes 147460
  1.7 6.4 %copy-start.2 = (s32[16,4,4]{0,2,1:T(4,128)S(1)}, s32[16,4,4]{0,2,1:T(4,128)}, u32[]{:S(2)}) copy-start(s32[16,4,4]{0,2,1:T(4,128)} %param.3) | copy-start | bytes 3076
  1.7 13.8 %collective-permute-start = (f32[72,256]{1,0:T(8,128)S(1)}, f32[72,256]{1,0:T(8,128)S(1)}, u32[]{:S(2)}, u32[]{:S(2)}) collective-permute-start(f32[72,256]{1,0:T(8,128)S(1)} %get-tuple-element.53), channel_id=1, source_target_pairs={{0,4},{1,5},{2,6},{3,7},{4,0},{5,1},{6,2},{7,3},{8,12},{9,13},{10,... | collective-permute-start | bytes 221192 | tf_op jit(solution)/shard_map/ppermute | solution.py:73
  1.8 13.8 %collective-permute-start.1 = (f32[72,256]{1,0:T(8,128)S(1)}, f32[72,256]{1,0:T(8,128)S(1)}, u32[]{:S(2)}, u32[]{:S(2)}) collective-permute-start(f32[72,256]{1,0:T(8,128)S(1)} %get-tuple-element.54), channel_id=1, source_target_pairs={{0,124},{1,125},{2,126},{3,127},{4,8},{5,9},{6,10},{7,11},{8,4},{9... | collective-permute-start | bytes 221192 | tf_op jit(solution)/shard_map/ppermute | solution.py:73
  8.1 7.4 %copy-start.1 = (f32[3,4,4,256]{3,2,1,0:T(4,128)S(1)}, f32[3,4,4,256]{3,2,1,0:T(4,128)}, u32[]{:S(2)}) copy-start(f32[3,4,4,256]{3,2,1,0:T(4,128)} %part_ref.5) | copy-start | bytes 147460
  15.8 4.6 %collective-permute-start.2 = (f32[96,256]{1,0:T(8,128)S(1)}, f32[96,256]{1,0:T(8,128)S(1)}, u32[]{:S(2)}, u32[]{:S(2)}) collective-permute-start(f32[96,256]{1,0:T(8,128)S(1)} %get-tuple-element.62), channel_id=1, source_target_pairs={{0,1},{1,0},{2,3},{3,2},{4,5},{5,4},{6,7},{7,6},{8,9},{9,8},{10,11... | collective-permute-start | bytes 294920 | tf_op jit(solution)/shard_map/ppermute | solution.py:73
  20.4 6.5 %collective-permute-start.3 = (f32[96,256]{1,0:T(8,128)S(1)}, f32[96,256]{1,0:T(8,128)S(1)}, u32[]{:S(2)}, u32[]{:S(2)}) collective-permute-start(f32[96,256]{1,0:T(8,128)S(1)} %get-tuple-element.70), channel_id=1, source_target_pairs={{0,3},{1,2},{2,1},{3,0},{4,7},{5,6},{6,5},{7,4},{8,11},{9,10},{10,... | collective-permute-start | bytes 294920 | tf_op jit(solution)/shard_map/ppermute | solution.py:73
  26.9 3.8 %collective-permute-start.4 = (f32[24,128]{1,0:T(8,128)S(1)}, f32[24,128]{1,0:T(8,128)S(1)}, u32[]{:S(2)}, u32[]{:S(2)}) collective-permute-start(f32[24,128]{1,0:T(8,128)S(1)} %slice_add_fusion), channel_id=1, source_target_pairs={{0,8},{1,9},{2,10},{3,11},{4,12},{5,13},{6,14},{7,15},{8,0},{9,1},... | collective-permute-start | bytes 36872 | tf_op jit(solution)/shard_map/ppermute | solution.py:73
  30.7 4.9 %collective-permute-start.5 = (f32[24,128]{1,0:T(8,128)S(1)}, f32[24,128]{1,0:T(8,128)S(1)}, u32[]{:S(2)}, u32[]{:S(2)}) collective-permute-start(f32[24,128]{1,0:T(8,128)S(1)} %add.13), channel_id=1, source_target_pairs={{0,24},{1,25},{2,26},{3,27},{4,28},{5,29},{6,30},{7,31},{8,16},{9,... | collective-permute-start | bytes 36872 | tf_op jit(solution)/shard_map/ppermute | solution.py:73
  35.6 5.3 %collective-permute-start.6 = (f32[24,128]{1,0:T(8,128)S(1)}, f32[24,128]{1,0:T(8,128)S(1)}, u32[]{:S(2)}, u32[]{:S(2)}) collective-permute-start(f32[24,128]{1,0:T(8,128)S(1)} %add.14), channel_id=1, source_target_pairs={{0,32},{1,33},{2,34},{3,35},{4,36},{5,37},{6,38},{7,39},{8,40},{9,... | collective-permute-start | bytes 36872 | tf_op jit(solution)/shard_map/ppermute | solution.py:73
  40.9 6.1 %collective-permute-start.7 = (f32[24,128]{1,0:T(8,128)S(1)}, f32[24,128]{1,0:T(8,128)S(1)}, u32[]{:S(2)}, u32[]{:S(2)}) collective-permute-start(f32[24,128]{1,0:T(8,128)S(1)} %add.15.f_ref), channel_id=1, source_target_pairs={{0,96},{1,97},{2,98},{3,99},{4,100},{5,101},{6,102},{7,103},{8,104... | collective-permute-start | bytes 36872 | tf_op jit(solution)/shard_map/ppermute | solution.py:73

commit v10 on v9

--- a/solution.py
+++ b/solution.py
@@ -316,6 +316,17 @@
         pairs(far, mask_ref, t_ref, s3_ref, w3_ref, acc_ref, parity, 0)
 
 
+RELEASE = ((0, 8, 15, 12), (0, 18, 30, 30), (0, 8, 15, 12))
+LATE_STEPS = (20, 42)
+
+
+def late_bodies():
+    slab, leaf = position()[:2]
+    places = (slab >> 3, (slab >> 1) & 3, leaf)
+    late = sum(chosen(place, term) for place, term in zip(places, RELEASE))
+    return sum((late >= step).astype(jnp.int32) for step in LATE_STEPS)
+
+
 def direct(tables, zero, extra, extra_in, mask_ref, t_ref, s_ref, w_ref, *refs):
     if zero:
         acc_ref, rows_ref = refs
@@ -330,10 +341,13 @@
         acc_ref[...] = refs[0][...]
         others = refs[1 : extra_in + 1] + refs[extra_in + 2 :]
     step = functools.partial(pairs, tables, mask_ref, t_ref, s_ref, w_ref, acc_ref)
+    split = tables.shape[0] - late_bodies()
     if tables.shape[0] == 1:
         step(0, 0)
+    elif zero:
+        lax.fori_loop(0, split, step, 0)
     else:
-        lax.fori_loop(0, tables.shape[0], step, 0)
+        lax.fori_loop(split, tables.shape[0], step, 0)
     if extra is not None:
         extra(*others)
 
@@ -566,9 +580,10 @@
     recv_a = swap(send_a, "core")
     recv_b = swap(send_b, "slab")
     own = pair_table("own")
+    split_pairs = own[:84].reshape(3, 28, 3)
     feats = (t0, s0, w0)
     acc, mask = run_direct(
-        "direct_own_0", own[:98].reshape(2, 49, 3), turned, feats, None, outs=[shaped(17, LEAVES, 1, SIZE)]
+        "direct_own_0", split_pairs, turned, feats, None, outs=[shaped(17, LEAVES, 1, SIZE)]
     )
     m1, f1, send_near, send_far = call(
         pack_slab,
@@ -582,7 +597,7 @@
     recv_near = swap(send_near, "leaf_near")
     built = dict(outs=features_out(LEAVES), scratch=stages(False))
     acc, s1, w1 = run_direct(
-        "direct_own_1", own[None, 98:147], mask, feats, acc, extra=slab_halo, ins=(recv_a, recv_b), **built
+        "direct_own_1", own[None, 84:140], mask, feats, acc, extra=slab_halo, ins=(recv_a, recv_b), **built
     )
     f2, send_far = call(
         pack_near, "pack_near", [V, V, V, A], [shaped(24, 128), shaped(LEAF_ROWS, SIZE)], [], SMALL
@@ -590,7 +605,7 @@
     send_far, acc = lax.optimization_barrier((send_far, acc))
     recv_far = swap(send_far, "leaf_far")
     acc, s2, w2 = run_direct(
-        "direct_own_2", own[None, 147:], mask, feats, acc, extra=near_halo, ins=(recv_near,), **built
+        "direct_own_2", own[None, 140:], mask, feats, acc, extra=near_halo, ins=(recv_near,), **built
     )
     recv_far, acc = lax.optimization_barrier((recv_far, acc))
     f3 = f2 + recv_far[72:96, 0:128]
@@ -629,6 +644,7 @@
     f6, acc = lax.optimization_barrier((f6, acc))
     got = swap(f6, "x_far")
     acc = run_sides("direct_sides_1", near_pairs[:, 30:], far_pairs[:, 30:], (*shared, acc))
+    acc = run_direct("direct_late", split_pairs, mask, feats, acc)
     got, acc = lax.optimization_barrier((got, acc))
     return call(
         finish,

time: 48.4 us -> 52.2 us (1.079)
  waiting for transfers between devices: 2.12 us -> 6.77 us
  starting transfers between devices: 10.9 us -> 9.69 us
    ppermute x8, waiting for transfers between devices: 2.12 us -> 6.77 us  [swap(): return lax.ppermute(value, ALL, SWAPS[name])]
    ppermute x8, starting transfers between devices: 10.9 us -> 9.69 us  [swap(): return lax.ppermute(value, ALL, SWAPS[name])]
    pallas_call x5 -> x6, Pallas kernels: 22 us -> 22.3 us  [run_direct(): call(functools.partial(direct, tables, zero, extra, len(ins)), name, [V]...]
  transfers between devices with their start and end apart: 8 -> 8, of which waited for: 3 -> 3; matrix products, arithmetic and copies ran while one was open for 0% -> 0% of each run, Pallas kernels for 66% -> 53%
where the time goes in v10:
time: 52.2 us; the launch traced here: 52 us
  Pallas kernels  34.6 us (66%)
  starting transfers between devices  9.69 us (19%)
  waiting for transfers between devices  6.77 us (13%)
  local copies, waits for them, and re-layouts  0.81 us (2%)
    pallas_call x6, Pallas kernels, run_direct(): call(functools.partial(direct, tables, zero, extra, len(ins)), name, [V]...  22.3 us
    pallas_call x2, Pallas kernels, run_sides(): call(functools.partial(direct_sides, near, far, extra, len(ins)), name, [...  10 us
    ppermute x8, starting transfers between devices, swap(): return lax.ppermute(value, ALL, SWAPS[name])  9.69 us
    ppermute x8, waiting for transfers between devices, swap(): return lax.ppermute(value, ALL, SWAPS[name])  6.77 us
    pallas_call x1, Pallas kernels, body(): call(finish, 'finish', [V] * 5, shaped(2, SIDE, SIDE, SIZE), far_scratch(...  1.18 us
  transfers between devices with their start and end apart: 8, of which 3 were waited for; matrix products, arithmetic and copies ran while one was open for 0% of the time, Pallas kernels for 53%

profile of v10, /device:TPU:8, one launch (start us, length us, event | category | flops | bytes accessed | tf_op | source)
XLA Modules:
  0.0 52.0 jit_solution(3108504764929409127)
XLA Ops:
  0.0 0.8 %copy-done = f32[3,4,4,256]{3,2,1,0:T(4,128)S(1)} copy-done((f32[3,4,4,256]{3,2,1,0:T(4,128)S(1)}, f32[3,4,4,256]{3,2,1,0:T(4,128)}, u32[]{:S(2)}) %copy-start) | copy-done | bytes 49176
  0.8 0.9 %prepare_own.1 = (bf16[16,32,256]{2,1,0:T(8,128)(2,1)S(1)}, bf16[16,256,32]{2,1,0:T(8,128)(2,1)S(1)}, bf16[16,16,256]{2,1,0:T(8,128)(2,1)S(1)}, f32[24,128]{1,0:...) custom-call(f32[3,4,4,256]{3,2,1,0:T(4,128)S(1)} %copy-done), custom_call_target="tpu_custom_call" | custom-call | flops 4000000 | bytes 1048576 | tf_op jit(solution)/shard_map/prepare_own/pallas_call | solution.py:571
  1.7 0.0 copy-start.3
  1.7 0.1 collective-permute-start
  1.8 6.3 %collective-permute-start.1 = (f32[72,256]{1,0:T(8,128)S(1)}, f32[72,256]{1,0:T(8,128)S(1)}, u32[]{:S(2)}, u32[]{:S(2)}) collective-permute-start(f32[72,256]{1,0:T(8,128)S(1)} %get-tuple-element.54), channel_id=1, source_target_pairs={{0,124},{1,125},{2,126},{3,127},{4,8},{5,9},{6,10},{7,11},{8,4},{9... | collective-permute-start | bytes 221192 | tf_op jit(solution)/shard_map/ppermute | solution.py:73
  8.1 6.7 %direct_own_0.1 = (f32[16,16,256]{2,1,0:T(8,128)S(1)}, f32[17,16,1,256]{3,2,1,0:T(1,128)S(1)}) custom-call(s32[4,4,16]{2,1,0:T(4,128)S(1)} %bitcast.1, bf16[16,32,256]{2,1,0:T(8,128)(2,1)S(1)} %get-tuple-element.57.t_ref, bf16[16,256,32]{2,1,0:T(8,128)(2,1)S(1)} %get-tuple-element.58.s_ref, bf16[16,16,256]{2,1,0:T(8,128)(2,1)S(1)} %get-tuple-element.59.w_ref), custom_call_target="tpu_custom_call" | custom-call | flops 33600000000 | bytes 1048576 | tf_op jit(solution)/shard_map/direct_own_0/pallas_call | solution.py:539
  14.9 0.0 collective-permute-done.1.rb_ref.refs_2_
  14.9 0.2 pack_slab.1
  15.1 0.5 collective-permute-start.2
  15.6 4.4 %direct_own_1.1 = (f32[16,16,256]{2,1,0:T(8,128)S(1)}, bf16[16,256,32]{2,1,0:T(8,128)(2,1)S(1)}, bf16[16,16,256]{2,1,0:T(8,128)(2,1)S(1)}) custom-call(f32[17,16,1,256]{3,2,1,0:T(1,128)S(1)} %get-tuple-element.65.mask_ref, bf16[16,32,256]{2,1,0:T(8,128)(2,1)S(1)} %get-tuple-element.57.t_ref, ...), custom_call_target="tpu_custom_call", output_to_operand_aliasing={{0}: (4, {})} | custom-call | flops 22400000000 | bytes 1048576 | tf_op jit(solution)/shard_map/direct_own_1/pallas_call | solution.py:539
  20.1 2.7 %collective-permute-start.3 = (f32[96,256]{1,0:T(8,128)S(1)}, f32[96,256]{1,0:T(8,128)S(1)}, u32[]{:S(2)}, u32[]{:S(2)}) collective-permute-start(f32[96,256]{1,0:T(8,128)S(1)} %get-tuple-element.70), channel_id=1, source_target_pairs={{0,3},{1,2},{2,1},{3,0},{4,7},{5,6},{6,5},{7,4},{8,11},{9,10},{10,... | collective-permute-start | bytes 294920 | tf_op jit(solution)/shard_map/ppermute | solution.py:73
  22.7 4.4 %direct_own_2.1 = (f32[16,16,256]{2,1,0:T(8,128)S(1)}, bf16[16,256,32]{2,1,0:T(8,128)(2,1)S(1)}, bf16[16,16,256]{2,1,0:T(8,128)(2,1)S(1)}) custom-call(f32[17,16,1,256]{3,2,1,0:T(1,128)S(1)} %get-tuple-element.65.mask_ref, bf16[16,32,256]{2,1,0:T(8,128)(2,1)S(1)} %get-tuple-element.57.t_ref, ...), custom_call_target="tpu_custom_call", output_to_operand_aliasing={{0}: (4, {})} | custom-call | flops 22400000000 | bytes 1048576 | tf_op jit(solution)/shard_map/direct_own_2/pallas_call | solution.py:539
  27.2 0.1 collective-permute-start.4
  27.3 3.5 %direct_slab_0.1 = (f32[16,16,256]{2,1,0:T(8,128)S(1)}, bf16[16,256,32]{2,1,0:T(8,128)(2,1)S(1)}, bf16[16,16,256]{2,1,0:T(8,128)(2,1)S(1)}) custom-call(f32[17,16,1,256]{3,2,1,0:T(1,128)S(1)} %get-tuple-element.65.mask_ref, bf16[16,32,256]{2,1,0:T(8,128)(2,1)S(1)} %get-tuple-element.57.t_ref, ...), custom_call_target="tpu_custom_call", output_to_operand_aliasing={{0}: (4, {})} | custom-call | flops 16800000000 | bytes 1048576 | tf_op jit(solution)/shard_map/direct_slab_0/pallas_call | solution.py:539
  30.8 0.2 collective-permute-done.4
  31.0 3.2 %direct_slab_1.1.acc_in = f32[16,16,256]{2,1,0:T(8,128)S(1)} custom-call(f32[17,16,1,256]{3,2,1,0:T(1,128)S(1)} %get-tuple-element.65.mask_ref, bf16[16,32,256]{2,1,0:T(8,128)(2,1)S(1)} %get-tuple-element.57.t_ref, bf16[16,256,32]{2,1,0:T(8,128)(2,1)S(1)} %get-tuple-element.76.s_ref, ...), custom_call_target="tpu_custom_call", output_to_operand_aliasing={{}: (4, {})} | custom-call | flops 16800000000 | bytes 1048576 | tf_op jit(solution)/shard_map/direct_slab_1/pallas_call | solution.py:539
  34.1 1.7 %collective-permute-done.5 = f32[24,128]{1,0:T(8,128)S(1)} collective-permute-done((f32[24,128]{1,0:T(8,128)S(1)}, f32[24,128]{1,0:T(8,128)S(1)}, u32[]{:S(2)}, u32[]{:S(2)}) %collective-permute-start.5) | collective-permute-done | bytes 12320 | tf_op jit(solution)/shard_map/ppermute | solution.py:73
  35.9 0.0 collective-permute-start.6
  35.9 5.3 %direct_sides_0.1 = (f32[16,16,256]{2,1,0:T(8,128)S(1)}, f32[16,128]{1,0:T(8,128)S(1)}) custom-call(f32[17,16,1,256]{3,2,1,0:T(1,128)S(1)} %get-tuple-element.65.mask_ref, bf16[16,32,256]{2,1,0:T(8,128)(2,1)S(1)} %get-tuple-element.57.t_ref, bf16[16,256,32]{2,1,0:T(8,128)(2,1)S(1)} %get-tuple-element.87.s2_ref, ...), custom_call_target="tpu_custom_call", output_to_operand_aliasing={{0}: (6, {})} | custom-call | flops 24000000000 | bytes 1048576 | tf_op jit(solution)/shard_map/direct_sides_0/pallas_call | solution.py:553
  41.2 4.7 %direct_sides_1.1.refs_0_ = f32[16,16,256]{2,1,0:T(8,128)S(1)} custom-call(f32[17,16,1,256]{3,2,1,0:T(1,128)S(1)} %get-tuple-element.65.mask_ref, bf16[16,32,256]{2,1,0:T(8,128)(2,1)S(1)} %get-tuple-element.57.t_ref, bf16[16,256,32]{2,1,0:T(8,128)(2,1)S(1)} %get-tuple-element.87.s2_ref, ...), custom_call_target="tpu_custom_call", output_to_operand_aliasing={{}: (6, {})} | custom-call | flops 24000000000 | bytes 1048576 | tf_op jit(solution)/shard_map/direct_sides_1/pallas_call | solution.py:553
  45.9 0.0 collective-permute-start.7
  46.0 0.1 direct_late.1.acc_ref
  46.0 4.8 %collective-permute-done.7.got_ref = f32[24,128]{1,0:T(8,128)S(1)} collective-permute-done((f32[24,128]{1,0:T(8,128)S(1)}, f32[24,128]{1,0:T(8,128)S(1)}, u32[]{:S(2)}, u32[]{:S(2)}) %collective-permute-start.7) | collective-permute-done | bytes 12320 | tf_op jit(solution)/shard_map/ppermute | solution.py:73
  50.9 1.2 %finish.1 = f32[2,4,4,256]{3,2,1,0:T(4,128)} custom-call(f32[3,4,4,256]{3,2,1,0:T(4,128)S(1)} %copy-done.2, f32[16,16,256]{2,1,0:T(8,128)S(1)} %direct_late.1.acc_ref, f32[16,128]{1,0:T(8,128)S(1)} %get-tuple-element.99.near_ref, f32[24,128]{1,0:T(8,128)S(1)} %add.15.f_ref, f32[24,128]{1,0:T(8,128)S(1)} %collective-permute-done.7.got_ref), custom_call_target="tpu_custom_call" | custom-call | flops 4000000 | bytes 1048576 | tf_op jit(solution)/shard_map/finish/pallas_call | solution.py:649
  (16 shorter events, 0.1 us)
Async XLA Ops:
  0.0 0.8 %copy-start = (f32[3,4,4,256]{3,2,1,0:T(4,128)S(1)}, f32[3,4,4,256]{3,2,1,0:T(4,128)}, u32[]{:S(2)}) copy-start(f32[3,4,4,256]{3,2,1,0:T(4,128)} %part_ref.5) | copy-start | bytes 147460
  1.7 6.4 %copy-start.3 = (s32[16,4,4]{0,2,1:T(4,128)S(1)}, s32[16,4,4]{0,2,1:T(4,128)}, u32[]{:S(2)}) copy-start(s32[16,4,4]{0,2,1:T(4,128)} %param.3) | copy-start | bytes 3076
  1.7 13.2 %collective-permute-start = (f32[72,256]{1,0:T(8,128)S(1)}, f32[72,256]{1,0:T(8,128)S(1)}, u32[]{:S(2)}, u32[]{:S(2)}) collective-permute-start(f32[72,256]{1,0:T(8,128)S(1)} %get-tuple-element.53), channel_id=1, source_target_pairs={{0,4},{1,5},{2,6},{3,7},{4,0},{5,1},{6,2},{7,3},{8,12},{9,13},{10,... | collective-permute-start | bytes 221192 | tf_op jit(solution)/shard_map/ppermute | solution.py:73
  1.8 13.1 %collective-permute-start.1 = (f32[72,256]{1,0:T(8,128)S(1)}, f32[72,256]{1,0:T(8,128)S(1)}, u32[]{:S(2)}, u32[]{:S(2)}) collective-permute-start(f32[72,256]{1,0:T(8,128)S(1)} %get-tuple-element.54), channel_id=1, source_target_pairs={{0,124},{1,125},{2,126},{3,127},{4,8},{5,9},{6,10},{7,11},{8,4},{9... | collective-permute-start | bytes 221192 | tf_op jit(solution)/shard_map/ppermute | solution.py:73
  8.1 6.8 %copy-start.1 = (f32[3,4,4,256]{3,2,1,0:T(4,128)S(1)}, f32[3,4,4,256]{3,2,1,0:T(4,128)}, u32[]{:S(2)}) copy-start(f32[3,4,4,256]{3,2,1,0:T(4,128)} %part_ref.5) | copy-start | bytes 147460
  15.1 4.9 %collective-permute-start.2 = (f32[96,256]{1,0:T(8,128)S(1)}, f32[96,256]{1,0:T(8,128)S(1)}, u32[]{:S(2)}, u32[]{:S(2)}) collective-permute-start(f32[96,256]{1,0:T(8,128)S(1)} %get-tuple-element.62), channel_id=1, source_target_pairs={{0,1},{1,0},{2,3},{3,2},{4,5},{5,4},{6,7},{7,6},{8,9},{9,8},{10,11... | collective-permute-start | bytes 294920 | tf_op jit(solution)/shard_map/ppermute | solution.py:73
  20.1 7.1 %collective-permute-start.3 = (f32[96,256]{1,0:T(8,128)S(1)}, f32[96,256]{1,0:T(8,128)S(1)}, u32[]{:S(2)}, u32[]{:S(2)}) collective-permute-start(f32[96,256]{1,0:T(8,128)S(1)} %get-tuple-element.70), channel_id=1, source_target_pairs={{0,3},{1,2},{2,1},{3,0},{4,7},{5,6},{6,5},{7,4},{8,11},{9,10},{10,... | collective-permute-start | bytes 294920 | tf_op jit(solution)/shard_map/ppermute | solution.py:73
  27.2 3.8 %collective-permute-start.4 = (f32[24,128]{1,0:T(8,128)S(1)}, f32[24,128]{1,0:T(8,128)S(1)}, u32[]{:S(2)}, u32[]{:S(2)}) collective-permute-start(f32[24,128]{1,0:T(8,128)S(1)} %slice_add_fusion), channel_id=1, source_target_pairs={{0,8},{1,9},{2,10},{3,11},{4,12},{5,13},{6,14},{7,15},{8,0},{9,1},... | collective-permute-start | bytes 36872 | tf_op jit(solution)/shard_map/ppermute | solution.py:73
  31.0 4.9 %collective-permute-start.5 = (f32[24,128]{1,0:T(8,128)S(1)}, f32[24,128]{1,0:T(8,128)S(1)}, u32[]{:S(2)}, u32[]{:S(2)}) collective-permute-start(f32[24,128]{1,0:T(8,128)S(1)} %add.13), channel_id=1, source_target_pairs={{0,24},{1,25},{2,26},{3,27},{4,28},{5,29},{6,30},{7,31},{8,16},{9,... | collective-permute-start | bytes 36872 | tf_op jit(solution)/shard_map/ppermute | solution.py:73
  35.9 5.3 %collective-permute-start.6 = (f32[24,128]{1,0:T(8,128)S(1)}, f32[24,128]{1,0:T(8,128)S(1)}, u32[]{:S(2)}, u32[]{:S(2)}) collective-permute-start(f32[24,128]{1,0:T(8,128)S(1)} %add.14), channel_id=1, source_target_pairs={{0,32},{1,33},{2,34},{3,35},{4,36},{5,37},{6,38},{7,39},{8,40},{9,... | collective-permute-start | bytes 36872 | tf_op jit(solution)/shard_map/ppermute | solution.py:73
  45.9 4.9 %copy-start.2 = (f32[3,4,4,256]{3,2,1,0:T(4,128)S(1)}, f32[3,4,4,256]{3,2,1,0:T(4,128)}, u32[]{:S(2)}) copy-start(f32[3,4,4,256]{3,2,1,0:T(4,128)} %part_ref.5) | copy-start | bytes 147460
  45.9 4.9 %collective-permute-start.7 = (f32[24,128]{1,0:T(8,128)S(1)}, f32[24,128]{1,0:T(8,128)S(1)}, u32[]{:S(2)}, u32[]{:S(2)}) collective-permute-start(f32[24,128]{1,0:T(8,128)S(1)} %add.15.f_ref), channel_id=1, source_target_pairs={{0,96},{1,97},{2,98},{3,99},{4,100},{5,101},{6,102},{7,103},{8,104... | collective-permute-start | bytes 36872 | tf_op jit(solution)/shard_map/ppermute | solution.py:73

commit v11 on v10

--- a/solution.py
+++ b/solution.py
@@ -303,7 +303,7 @@
     return 0
 
 
-def direct_sides(near, far, extra, extra_in, mask_ref, t_ref, s2_ref, w2_ref, s3_ref, w3_ref, acc_in, *refs):
+def direct_sides(near, far, late, extra, extra_in, mask_ref, t_ref, s2_ref, w2_ref, s3_ref, w3_ref, acc_in, *refs):
     acc_ref = refs[extra_in]
     acc_ref[...] = acc_in[...]
     parity = position()[3]
@@ -314,6 +314,10 @@
     @pl.when(position()[4] == 1)
     def _():
         pairs(far, mask_ref, t_ref, s3_ref, w3_ref, acc_ref, parity, 0)
+
+    if late is not None:
+        step = functools.partial(pairs, late, mask_ref, t_ref, refs[0], refs[1], acc_ref)
+        lax.fori_loop(late.shape[0] - late_bodies(), late.shape[0], step, 0)
 
 
 RELEASE = ((0, 8, 15, 12), (0, 18, 30, 30), (0, 8, 15, 12))
@@ -344,10 +348,8 @@
     split = tables.shape[0] - late_bodies()
     if tables.shape[0] == 1:
         step(0, 0)
-    elif zero:
+    else:
         lax.fori_loop(0, split, step, 0)
-    else:
-        lax.fori_loop(split, tables.shape[0], step, 0)
     if extra is not None:
         extra(*others)
 
@@ -548,10 +550,10 @@
     return got if outs else got[0]
 
 
-def run_sides(name, near, far, args, extra=None, ins=(), outs=(), scratch=()):
+def run_sides(name, near, far, args, late=None, extra=None, ins=(), outs=(), scratch=()):
     args = [*args, *ins]
     got = call(
-        functools.partial(direct_sides, near, far, extra, len(ins)),
+        functools.partial(direct_sides, near, far, late, extra, len(ins)),
         name,
         [V] * len(args),
         [shaped(LEAVES, 16, SIZE), *outs],
@@ -643,8 +645,9 @@
     f6 = f5 + got
     f6, acc = lax.optimization_barrier((f6, acc))
     got = swap(f6, "x_far")
-    acc = run_sides("direct_sides_1", near_pairs[:, 30:], far_pairs[:, 30:], (*shared, acc))
-    acc = run_direct("direct_late", split_pairs, mask, feats, acc)
+    acc = run_sides(
+        "direct_sides_1", near_pairs[:, 30:], far_pairs[:, 30:], (*shared, acc), split_pairs, ins=(s0, w0)
+    )
     got, acc = lax.optimization_barrier((got, acc))
     return call(
         finish,

time: 52.2 us -> 51.5 us (0.987)
  the two profiles are of different devices: /device:TPU:8 before, /device:TPU:76 now
where the time goes in v11:
time: 51.5 us; the launch traced here: 51.3 us
  Pallas kernels  34.5 us (67%)
  starting transfers between devices  14.3 us (28%)
  local copies, waits for them, and re-layouts  1.19 us (2%)
  waiting for transfers between devices  1.14 us (2%)
    pallas_call x5, Pallas kernels, run_direct(): call(functools.partial(direct, tables, zero, extra, len(ins)), name, [V]...  17.9 us
    pallas_call x2, Pallas kernels, run_sides(): call(functools.partial(direct_sides, near, far, late, extra, len(ins)), n...  14.4 us
    ppermute x8, starting transfers between devices, swap(): return lax.ppermute(value, ALL, SWAPS[name])  14.3 us
    pallas_call x1, Pallas kernels, body(): call(finish, 'finish', [V] * 5, shaped(2, SIDE, SIDE, SIZE), far_scratch(...  1.19 us
    unnamed x6, local copies, waits for them, and re-layouts  1.19 us
    ppermute x8, waiting for transfers between devices, swap(): return lax.ppermute(value, ALL, SWAPS[name])  1.14 us
  transfers between devices with their start and end apart: 8, of which 2 were waited for; matrix products, arithmetic and copies ran while one was open for 0% of the time, Pallas kernels for 63%

profile of v11, /device:TPU:76, one launch (start us, length us, event | category | flops | bytes accessed | tf_op | source)
XLA Modules:
  0.0 51.3 jit_solution(7101052507395846240)
XLA Ops:
  0.0 0.8 %copy-done = f32[3,4,4,256]{3,2,1,0:T(4,128)S(1)} copy-done((f32[3,4,4,256]{3,2,1,0:T(4,128)S(1)}, f32[3,4,4,256]{3,2,1,0:T(4,128)}, u32[]{:S(2)}) %copy-start) | copy-done | bytes 49176
  0.8 0.9 %prepare_own.1 = (bf16[16,32,256]{2,1,0:T(8,128)(2,1)S(1)}, bf16[16,256,32]{2,1,0:T(8,128)(2,1)S(1)}, bf16[16,16,256]{2,1,0:T(8,128)(2,1)S(1)}, f32[24,128]{1,0:...) custom-call(f32[3,4,4,256]{3,2,1,0:T(4,128)S(1)} %copy-done), custom_call_target="tpu_custom_call" | custom-call | flops 4000000 | bytes 1048576 | tf_op jit(solution)/shard_map/prepare_own/pallas_call | solution.py:573
  1.7 0.0 copy-start.2
  1.7 0.1 collective-permute-start
  1.8 0.2 collective-permute-start.1
  2.0 0.4 copy-done.2
  2.4 2.3 %direct_own_0.1 = (f32[16,16,256]{2,1,0:T(8,128)S(1)}, f32[17,16,1,256]{3,2,1,0:T(1,128)S(1)}) custom-call(s32[4,4,16]{2,1,0:T(4,128)S(1)} %bitcast.1, bf16[16,32,256]{2,1,0:T(8,128)(2,1)S(1)} %get-tuple-element.57.t_ref, bf16[16,256,32]{2,1,0:T(8,128)(2,1)S(1)} %get-tuple-element.58.s_ref.refs_0_, bf16[16,16,256]{2,1,0:T(8,128)(2,1)S(1)} %get-tuple-element.59.w_ref.refs_1_), custom_call_target="tpu_custom_call" | custom-call | flops 33600000000 | bytes 1048576 | tf_op jit(solution)/shard_map/direct_own_0/pallas_call | solution.py:541
  4.7 0.9 %collective-permute-done.1.rb_ref.refs_2_ = f32[72,256]{1,0:T(8,128)S(1)} collective-permute-done((f32[72,256]{1,0:T(8,128)S(1)}, f32[72,256]{1,0:T(8,128)S(1)}, u32[]{:S(2)}, u32[]{:S(2)}) %collective-permute-start.1) | collective-permute-done | bytes 73760 | tf_op jit(solution)/shard_map/ppermute | solution.py:73
  5.7 0.2 pack_slab.1
  5.8 0.5 collective-permute-start.2
  6.3 4.4 %direct_own_1.1 = (f32[16,16,256]{2,1,0:T(8,128)S(1)}, bf16[16,256,32]{2,1,0:T(8,128)(2,1)S(1)}, bf16[16,16,256]{2,1,0:T(8,128)(2,1)S(1)}) custom-call(f32[17,16,1,256]{3,2,1,0:T(1,128)S(1)} %get-tuple-element.65.mask_ref, bf16[16,32,256]{2,1,0:T(8,128)(2,1)S(1)} %get-tuple-element.57.t_ref, ...), custom_call_target="tpu_custom_call", output_to_operand_aliasing={{0}: (4, {})} | custom-call | flops 22400000000 | bytes 1048576 | tf_op jit(solution)/shard_map/direct_own_1/pallas_call | solution.py:541
  10.8 0.2 collective-permute-done.2.r_ref.refs_1_.refs_2_
  11.0 2.5 %collective-permute-start.3 = (f32[96,256]{1,0:T(8,128)S(1)}, f32[96,256]{1,0:T(8,128)S(1)}, u32[]{:S(2)}, u32[]{:S(2)}) collective-permute-start(f32[96,256]{1,0:T(8,128)S(1)} %get-tuple-element.70), channel_id=1, source_target_pairs={{0,3},{1,2},{2,1},{3,0},{4,7},{5,6},{6,5},{7,4},{8,11},{9,10},{10,... | collective-permute-start | bytes 294920 | tf_op jit(solution)/shard_map/ppermute | solution.py:73
  13.5 4.4 %direct_own_2.1 = (f32[16,16,256]{2,1,0:T(8,128)S(1)}, bf16[16,256,32]{2,1,0:T(8,128)(2,1)S(1)}, bf16[16,16,256]{2,1,0:T(8,128)(2,1)S(1)}) custom-call(f32[17,16,1,256]{3,2,1,0:T(1,128)S(1)} %get-tuple-element.65.mask_ref, bf16[16,32,256]{2,1,0:T(8,128)(2,1)S(1)} %get-tuple-element.57.t_ref, ...), custom_call_target="tpu_custom_call", output_to_operand_aliasing={{0}: (4, {})} | custom-call | flops 22400000000 | bytes 1048576 | tf_op jit(solution)/shard_map/direct_own_2/pallas_call | solution.py:541
  17.9 0.0 collective-permute-done.3.refs_1_.refs_3_
  17.9 1.7 %collective-permute-start.4 = (f32[24,128]{1,0:T(8,128)S(1)}, f32[24,128]{1,0:T(8,128)S(1)}, u32[]{:S(2)}, u32[]{:S(2)}) collective-permute-start(f32[24,128]{1,0:T(8,128)S(1)} %slice_add_fusion), channel_id=1, source_target_pairs={{0,8},{1,9},{2,10},{3,11},{4,12},{5,13},{6,14},{7,15},{8,0},{9,1},... | collective-permute-start | bytes 36872 | tf_op jit(solution)/shard_map/ppermute | solution.py:73
  19.6 3.5 %direct_slab_0.1 = (f32[16,16,256]{2,1,0:T(8,128)S(1)}, bf16[16,256,32]{2,1,0:T(8,128)(2,1)S(1)}, bf16[16,16,256]{2,1,0:T(8,128)(2,1)S(1)}) custom-call(f32[17,16,1,256]{3,2,1,0:T(1,128)S(1)} %get-tuple-element.65.mask_ref, bf16[16,32,256]{2,1,0:T(8,128)(2,1)S(1)} %get-tuple-element.57.t_ref, ...), custom_call_target="tpu_custom_call", output_to_operand_aliasing={{0}: (4, {})} | custom-call | flops 16800000000 | bytes 1048576 | tf_op jit(solution)/shard_map/direct_slab_0/pallas_call | solution.py:541
  23.2 3.5 %collective-permute-start.5 = (f32[24,128]{1,0:T(8,128)S(1)}, f32[24,128]{1,0:T(8,128)S(1)}, u32[]{:S(2)}, u32[]{:S(2)}) collective-permute-start(f32[24,128]{1,0:T(8,128)S(1)} %add.13), channel_id=1, source_target_pairs={{0,24},{1,25},{2,26},{3,27},{4,28},{5,29},{6,30},{7,31},{8,16},{9,... | collective-permute-start | bytes 36872 | tf_op jit(solution)/shard_map/ppermute | solution.py:73
  26.7 3.2 %direct_slab_1.1.acc_in = f32[16,16,256]{2,1,0:T(8,128)S(1)} custom-call(f32[17,16,1,256]{3,2,1,0:T(1,128)S(1)} %get-tuple-element.65.mask_ref, bf16[16,32,256]{2,1,0:T(8,128)(2,1)S(1)} %get-tuple-element.57.t_ref, bf16[16,256,32]{2,1,0:T(8,128)(2,1)S(1)} %get-tuple-element.76.s_ref, ...), custom_call_target="tpu_custom_call", output_to_operand_aliasing={{}: (4, {})} | custom-call | flops 16800000000 | bytes 1048576 | tf_op jit(solution)/shard_map/direct_slab_1/pallas_call | solution.py:541
  29.9 1.8 %collective-permute-start.6 = (f32[24,128]{1,0:T(8,128)S(1)}, f32[24,128]{1,0:T(8,128)S(1)}, u32[]{:S(2)}, u32[]{:S(2)}) collective-permute-start(f32[24,128]{1,0:T(8,128)S(1)} %add.14), channel_id=1, source_target_pairs={{0,32},{1,33},{2,34},{3,35},{4,36},{5,37},{6,38},{7,39},{8,40},{9,... | collective-permute-start | bytes 36872 | tf_op jit(solution)/shard_map/ppermute | solution.py:73
  31.7 5.3 %direct_sides_0.1 = (f32[16,16,256]{2,1,0:T(8,128)S(1)}, f32[16,128]{1,0:T(8,128)S(1)}) custom-call(f32[17,16,1,256]{3,2,1,0:T(1,128)S(1)} %get-tuple-element.65.mask_ref, bf16[16,32,256]{2,1,0:T(8,128)(2,1)S(1)} %get-tuple-element.57.t_ref, bf16[16,256,32]{2,1,0:T(8,128)(2,1)S(1)} %get-tuple-element.87.s2_ref, ...), custom_call_target="tpu_custom_call", output_to_operand_aliasing={{0}: (6, {})} | custom-call | flops 24000000000 | bytes 1048576 | tf_op jit(solution)/shard_map/direct_sides_0/pallas_call | solution.py:555
  37.0 4.1 %collective-permute-start.7 = (f32[24,128]{1,0:T(8,128)S(1)}, f32[24,128]{1,0:T(8,128)S(1)}, u32[]{:S(2)}, u32[]{:S(2)}) collective-permute-start(f32[24,128]{1,0:T(8,128)S(1)} %add.15.f_ref), channel_id=1, source_target_pairs={{0,96},{1,97},{2,98},{3,99},{4,100},{5,101},{6,102},{7,103},{8,104... | collective-permute-start | bytes 36872 | tf_op jit(solution)/shard_map/ppermute | solution.py:73
  41.0 9.1 %direct_sides_1.1.acc_ref = f32[16,16,256]{2,1,0:T(8,128)S(1)} custom-call(f32[17,16,1,256]{3,2,1,0:T(1,128)S(1)} %get-tuple-element.65.mask_ref, bf16[16,32,256]{2,1,0:T(8,128)(2,1)S(1)} %get-tuple-element.57.t_ref, bf16[16,256,32]{2,1,0:T(8,128)(2,1)S(1)} %get-tuple-element.87.s2_ref, ...), custom_call_target="tpu_custom_call", output_to_operand_aliasing={{}: (6, {})} | custom-call | flops 24000000000 | bytes 1048576 | tf_op jit(solution)/shard_map/direct_sides_1/pallas_call | solution.py:555
  50.1 1.2 %finish.1 = f32[2,4,4,256]{3,2,1,0:T(4,128)} custom-call(f32[3,4,4,256]{3,2,1,0:T(4,128)S(1)} %copy-done.1, f32[16,16,256]{2,1,0:T(8,128)S(1)} %direct_sides_1.1.acc_ref, f32[16,128]{1,0:T(8,128)S(1)} %get-tuple-element.99.near_ref, f32[24,128]{1,0:T(8,128)S(1)} %add.15.f_ref, f32[24,128]{1,0:T(8,128)S(1)} %collective-permute-done.7.got_ref), custom_call_target="tpu_custom_call" | custom-call | flops 4000000 | bytes 1048576 | tf_op jit(solution)/shard_map/finish/pallas_call | solution.py:652
  (13 shorter events, 0.1 us)
Async XLA Ops:
  0.0 0.8 %copy-start = (f32[3,4,4,256]{3,2,1,0:T(4,128)S(1)}, f32[3,4,4,256]{3,2,1,0:T(4,128)}, u32[]{:S(2)}) copy-start(f32[3,4,4,256]{3,2,1,0:T(4,128)} %part_ref.5) | copy-start | bytes 147460
  1.7 0.7 %copy-start.2 = (s32[16,4,4]{0,2,1:T(4,128)S(1)}, s32[16,4,4]{0,2,1:T(4,128)}, u32[]{:S(2)}) copy-start(s32[16,4,4]{0,2,1:T(4,128)} %param.3) | copy-start | bytes 3076
  1.7 3.0 %collective-permute-start = (f32[72,256]{1,0:T(8,128)S(1)}, f32[72,256]{1,0:T(8,128)S(1)}, u32[]{:S(2)}, u32[]{:S(2)}) collective-permute-start(f32[72,256]{1,0:T(8,128)S(1)} %get-tuple-element.53), channel_id=1, source_target_pairs={{0,4},{1,5},{2,6},{3,7},{4,0},{5,1},{6,2},{7,3},{8,12},{9,13},{10,... | collective-permute-start | bytes 221192 | tf_op jit(solution)/shard_map/ppermute | solution.py:73
  1.8 3.9 %collective-permute-start.1 = (f32[72,256]{1,0:T(8,128)S(1)}, f32[72,256]{1,0:T(8,128)S(1)}, u32[]{:S(2)}, u32[]{:S(2)}) collective-permute-start(f32[72,256]{1,0:T(8,128)S(1)} %get-tuple-element.54), channel_id=1, source_target_pairs={{0,124},{1,125},{2,126},{3,127},{4,8},{5,9},{6,10},{7,11},{8,4},{9... | collective-permute-start | bytes 221192 | tf_op jit(solution)/shard_map/ppermute | solution.py:73
  2.4 3.3 %copy-start.1 = (f32[3,4,4,256]{3,2,1,0:T(4,128)S(1)}, f32[3,4,4,256]{3,2,1,0:T(4,128)}, u32[]{:S(2)}) copy-start(f32[3,4,4,256]{3,2,1,0:T(4,128)} %part_ref.5) | copy-start | bytes 147460
  5.8 5.1 %collective-permute-start.2 = (f32[96,256]{1,0:T(8,128)S(1)}, f32[96,256]{1,0:T(8,128)S(1)}, u32[]{:S(2)}, u32[]{:S(2)}) collective-permute-start(f32[96,256]{1,0:T(8,128)S(1)} %get-tuple-element.62), channel_id=1, source_target_pairs={{0,1},{1,0},{2,3},{3,2},{4,5},{5,4},{6,7},{7,6},{8,9},{9,8},{10,11... | collective-permute-start | bytes 294920 | tf_op jit(solution)/shard_map/ppermute | solution.py:73
  11.0 6.9 %collective-permute-start.3 = (f32[96,256]{1,0:T(8,128)S(1)}, f32[96,256]{1,0:T(8,128)S(1)}, u32[]{:S(2)}, u32[]{:S(2)}) collective-permute-start(f32[96,256]{1,0:T(8,128)S(1)} %get-tuple-element.70), channel_id=1, source_target_pairs={{0,3},{1,2},{2,1},{3,0},{4,7},{5,6},{6,5},{7,4},{8,11},{9,10},{10,... | collective-permute-start | bytes 294920 | tf_op jit(solution)/shard_map/ppermute | solution.py:73
  17.9 5.2 %collective-permute-start.4 = (f32[24,128]{1,0:T(8,128)S(1)}, f32[24,128]{1,0:T(8,128)S(1)}, u32[]{:S(2)}, u32[]{:S(2)}) collective-permute-start(f32[24,128]{1,0:T(8,128)S(1)} %slice_add_fusion), channel_id=1, source_target_pairs={{0,8},{1,9},{2,10},{3,11},{4,12},{5,13},{6,14},{7,15},{8,0},{9,1},... | collective-permute-start | bytes 36872 | tf_op jit(solution)/shard_map/ppermute | solution.py:73
  23.2 6.7 %collective-permute-start.5 = (f32[24,128]{1,0:T(8,128)S(1)}, f32[24,128]{1,0:T(8,128)S(1)}, u32[]{:S(2)}, u32[]{:S(2)}) collective-permute-start(f32[24,128]{1,0:T(8,128)S(1)} %add.13), channel_id=1, source_target_pairs={{0,24},{1,25},{2,26},{3,27},{4,28},{5,29},{6,30},{7,31},{8,16},{9,... | collective-permute-start | bytes 36872 | tf_op jit(solution)/shard_map/ppermute | solution.py:73
  29.9 7.1 %collective-permute-start.6 = (f32[24,128]{1,0:T(8,128)S(1)}, f32[24,128]{1,0:T(8,128)S(1)}, u32[]{:S(2)}, u32[]{:S(2)}) collective-permute-start(f32[24,128]{1,0:T(8,128)S(1)} %add.14), channel_id=1, source_target_pairs={{0,32},{1,33},{2,34},{3,35},{4,36},{5,37},{6,38},{7,39},{8,40},{9,... | collective-permute-start | bytes 36872 | tf_op jit(solution)/shard_map/ppermute | solution.py:73
  37.0 13.2 %collective-permute-start.7 = (f32[24,128]{1,0:T(8,128)S(1)}, f32[24,128]{1,0:T(8,128)S(1)}, u32[]{:S(2)}, u32[]{:S(2)}) collective-permute-start(f32[24,128]{1,0:T(8,128)S(1)} %add.15.f_ref), channel_id=1, source_target_pairs={{0,96},{1,97},{2,98},{3,99},{4,100},{5,101},{6,102},{7,103},{8,104... | collective-permute-start | bytes 36872 | tf_op jit(solution)/shard_map/ppermute | solution.py:73
